TPU v7x, 32 devices: a whole 2x2x4 slice. The times are simulated.
32 devices in a mesh: box: 8 (over z, y), col: 4 (over x, core).
Axes of the slice: x: 2, y: 2, z: 4, core: 2. Of those that a mesh axis runs over, the one named last changes fastest.
Arguments:
- box_points: float32 [16, 3, 512], P('box'), may hold values from 0 to 1
- proxy_directions: float32 [3, 1024], P(None, 'col'), may hold values from -1 to 1, as said below
- point_order: int32 [16, 512], P('box'), may hold values from 0 to 511, each once within a row
- neighbour_boxes: int32 [16, 8], P('box'), may hold values from 0 to 15, as said below
- neighbour_places: int32 [16, 8], P('box'), may hold values from 0 to 25
- pivot_inverse: float32 [16, 2, 256], P('box', None, 'col'), may hold values from -6 to 6
Outputs:
- interpolation: float32 [16, 2, 256, 256], P('box', None, None, 'col')
- skeleton_update: float32 [16, 2, 256, 256], P('box', None, 'col')
Inputs may be any that keep to these rules, and one draw needn't show every extreme that they name: `neighbour_boxes`: box g is held by index g // 2 of the box axis. Every entry names a box of the same index or of the index just before or just after it, cyclically. Of the 16 entries of one index's boxes exactly half name boxes of that same index, never the listing box itself; a box may be listed twice in one row. `proxy_directions`: unit vectors.
All inputs are finite; a program needn't handle non-finite values.
Results may differ from a plain program's by a relative error of at most 0.0038.
Values sent between devices are 32-bit elements; how exact they have to be, the bound alone decides.
A program may use at most 64 MiB of HBM per device.

v0:
```python
import functools
import math

import jax
import jax.numpy as jnp
from jax import lax
from jax.experimental import pallas as pl
from jax.experimental.pallas import tpu as pltpu
from jax.sharding import PartitionSpec as P

S = 256

softening = 0.05
proxy_radius = 1.5
ridge_share = 0.05
highest = lax.Precision.HIGHEST
NBLK = 32
ROWS = 16

COS = (1.4142135381698608, -6.978850841522217, 5.739460468292236, -1.883557915687561, 0.3106880187988281)
SIN = (4.442883014678955, -7.308245658874512, 3.606354236602783, -0.8461116552352905, 0.1098245158791542)

VMEM = pl.BlockSpec(memory_space=pltpu.VMEM)
SMEM = pl.BlockSpec(memory_space=pltpu.SMEM)


def params(**more):
    return pltpu.CompilerParams(vmem_limit_bytes=24 * 1024 * 1024, **more)


def horner(coefficients, z):
    total = jnp.full_like(z, coefficients[-1])
    for one in coefficients[-2::-1]:
        total = total * z + one
    return total


def kernel_values(tx, ty, tz, sx, sy, sz):
    dx = tx - sx
    dy = ty - sy
    dz = tz - sz
    square = (dx * dx + dy * dy) + (dz * dz + 4.0 * softening * softening)
    inverse = lax.rsqrt(square)
    turns = square * inverse
    part = turns - jnp.floor(turns + 0.5)
    z = part * part
    amplitude = inverse * (1.0 / (2.0 * math.pi))
    sine = part * horner(SIN, z)
    scaled = amplitude * sine
    return amplitude - scaled * sine, scaled * horner(COS, z)


def slot_of(nb_ref, where_ref, row, entry, box_count, box_total):
    owner_box = nb_ref[row, entry]
    step = owner_box // box_count - where_ref[0] + 1
    step = jnp.where(step < 0, step + box_total, step)
    step = jnp.where(step >= box_total, step - box_total, step)
    return step * box_count + owner_box % box_count


def dot_tn(a, b):
    return lax.dot_general(a, b, (((0,), (0,)), ((), ())), preferred_element_type=jnp.float32)


def tile_kernel(box_count, box_total, entries, where_ref, nb_ref, place_ref, points_ref, order_ref,
                proxy_ref, cross_ref, kern_ref, tcol, srow, raw, tiles, total):
    count = points_ref.shape[3]
    share = proxy_ref.shape[2]
    proxies = box_count * share
    raw[...] = jnp.zeros_like(raw)
    box = where_ref[1]
    first = where_ref[2] * entries

    def ordered(slot):
        side, which = slot // box_count, slot % box_count
        one_hot = (
            lax.broadcasted_iota(jnp.int32, (count, count), 0)
            == order_ref[side, pl.ds(which, 1), :]
        ).astype(jnp.float32).astype(jnp.bfloat16)
        raw[0:3, :] = points_ref[side, which]
        whole = raw[...]
        top = whole.astype(jnp.bfloat16).astype(jnp.float32)
        mid = (whole - top).astype(jnp.bfloat16).astype(jnp.float32)
        rows = jnp.concatenate([top, mid, whole - top - mid, jnp.zeros_like(top)], axis=0)
        picked = jnp.dot(rows.astype(jnp.bfloat16), one_hot, preferred_element_type=jnp.float32)
        return (picked[0:8] + picked[8:16]) + picked[16:24]

    axis_row = lax.broadcasted_iota(jnp.int32, (8, count), 0)
    srow[...] = 2.0 * ordered(box_count + box)
    for k in range(entries):
        slot = slot_of(nb_ref, where_ref, box, first + k, box_count, box_total)
        code = place_ref[box, first + k]
        code = jnp.where(code >= 13, code + 1, code)
        shift = [(code // 9 - 1), (code // 3) % 3 - 1, code % 3 - 1]
        move = jnp.where(
            axis_row == 0,
            shift[0].astype(jnp.float32),
            jnp.where(axis_row == 1, shift[1].astype(jnp.float32), shift[2].astype(jnp.float32)),
        )
        start = proxies + k * count
        tcol[start:start + count, 0:8] = jnp.transpose(2.0 * (ordered(slot) + move))
    for d in range(box_count):
        raw[0:3, 0:share] = 2.0 * (0.5 + proxy_radius * proxy_ref[d])
        tcol[d * share:(d + 1) * share, 0:8] = jnp.transpose(raw[:, 0:share])
    block = tiles.shape[1] // 2

    def evaluate(base, slot, keep=None):
        for i in range(block // ROWS):
            inner = slice(i * ROWS, (i + 1) * ROWS)
            lower = slice(block + i * ROWS, block + (i + 1) * ROWS)
            start = pl.multiple_of(base + i * ROWS, ROWS)
            tx = tcol[pl.ds(start, ROWS), 0:1]
            ty = tcol[pl.ds(start, ROWS), 1:2]
            tz = tcol[pl.ds(start, ROWS), 2:3]
            for c in range(0, count, 256):
                here = slice(c, c + 256)
                there = slice(count + c, count + c + 256)
                real, imag = kernel_values(tx, ty, tz, srow[0:1, here], srow[1:2, here],
                                           srow[2:3, here])
                if keep is not None:
                    kern_ref[keep, 0, inner, here] = real
                    kern_ref[keep, 1, inner, here] = imag
                real = real.astype(jnp.bfloat16)
                imag = imag.astype(jnp.bfloat16)
                tiles[slot, inner, here] = real
                tiles[slot, inner, there] = imag
                tiles[slot, lower, here] = imag
                tiles[slot, lower, there] = -real

    def gather(slot):
        total[...] += dot_tn(tiles[slot, :, 0:S], tiles[slot])

    total[...] = jnp.zeros_like(total)
    evaluate(0, 0)
    for i in range(1, proxies // block):
        gather((i + 1) % 2)
        evaluate(i * block, i % 2)
    parity = (proxies // block) % 2
    per = count // block

    @pl.loop(0, entries)
    def _(k):
        base = proxies + k * count
        for i in range(per):
            gather((parity + i + 1) % 2)
            evaluate(base + i * block, (parity + i) % 2, k if i == 0 else None)

    gather((parity + per - 1) % 2)
    cross_ref[0] = total[:, 0:count]
    cross_ref[1] = total[:, count:]


def exact(a, b, dims=((1,), (0,))):
    return lax.dot_general(a, b, (dims, ((), ())), precision=highest,
                           preferred_element_type=jnp.float32)


def solve_kernel(mine_ref, other_ref, x_ref, mat, low, high):
    n = x_ref.shape[1]
    wide = mine_ref.shape[2]
    nb = NBLK
    mat[...] = mine_ref[...] + other_ref[...]
    diagonal = lax.broadcasted_iota(jnp.int32, (n, n), 0) == lax.broadcasted_iota(
        jnp.int32, (n, n), 1
    )
    gram = mat[0, :, 0:n]
    ridge = ridge_share * jnp.sum(jnp.where(diagonal, gram, 0.0)) / n
    mat[0, :, 0:n] = gram + jnp.where(diagonal, ridge, 0.0)
    low[...] = jnp.zeros_like(low)
    high[...] = jnp.zeros_like(high)
    lane = lax.broadcasted_iota(jnp.int32, (nb, 128), 1)
    sub = lax.broadcasted_iota(jnp.int32, (nb, 128), 0)
    lane_all = lax.broadcasted_iota(jnp.int32, (n, 128), 1)

    def turned(block, shift):
        return pltpu.roll(block, shift, 1) if shift else block

    def inverse(block_re, block_im, back):
        re0, im0 = turned(block_re, back), turned(block_im, back)
        re1, im1 = turned(block_re, (back + nb) % 128), turned(block_im, (back + nb) % 128)
        zero = jnp.zeros_like(re0)
        m = jnp.where(lane < nb, re0, jnp.where(lane < 2 * nb, im1,
                                                jnp.where(lane - 2 * nb == sub, 1.0, zero)))
        w = jnp.where(lane < nb, -im0, jnp.where(lane < 2 * nb, re1,
                                                 jnp.where(lane - 3 * nb == sub, 1.0, zero)))

        def spread(block, k):
            return jnp.broadcast_to(block[:, k:k + 1], (nb, 128))

        for k in range(0, nb, 2):
            p0, p1 = spread(m, k), spread(m, k + 1)
            s0, s1 = spread(m, nb + k), spread(m, nb + k + 1)
            a, d = p0[k:k + 1], p1[k + 1:k + 2]
            br, bi = p1[k:k + 1], s1[k:k + 1]
            scale = 1.0 / (a * d - (br * br + bi * bi))
            m0, m1, w0, w1 = m[k:k + 1], m[k + 1:k + 2], w[k:k + 1], w[k + 1:k + 2]
            row_m0 = (d * m0 - (br * m1 + bi * w1)) * scale
            row_w0 = (d * w0 - (br * w1 - bi * m1)) * scale
            row_m1 = (a * m1 - (br * m0 - bi * w0)) * scale
            row_w1 = (a * w1 - (br * w0 + bi * m0)) * scale
            new_m = m - ((p0 * row_m0 + s0 * row_w0) + (p1 * row_m1 + s1 * row_w1))
            new_w = w - ((p0 * row_w0 - s0 * row_m0) + (p1 * row_w1 - s1 * row_m1))
            m = jnp.where(sub == k, row_m0, jnp.where(sub == k + 1, row_m1, new_m))
            w = jnp.where(sub == k, row_w0, jnp.where(sub == k + 1, row_w1, new_w))
        return m

    m = inverse(mat[0, 0:nb, 0:128], mat[1, 0:nb, 0:128], 0)
    for j in range(n // nb):
        rows = slice(j * nb, (j + 1) * nb)
        after = slice((j + 1) * nb, (j + 2) * nb)
        q = (j * nb) // 128 * 128
        back = (128 - (j * nb) % 128) % 128
        start = (j + 1) * nb // 128 * 128
        span = wide - start
        panel_re = mat[0, rows, start:]
        panel_im = mat[1, rows, start:]
        high[2 * nb:3 * nb, 0:span] = panel_re
        high[2 * nb:3 * nb, span:2 * span] = panel_im
        high[3 * nb:4 * nb, 0:span] = -panel_im
        high[3 * nb:4 * nb, span:2 * span] = panel_re
        solved = exact(m, high[:, 0:2 * span])
        low[0:nb, 0:2 * span] = solved
        low[nb:2 * nb, 0:span] = -solved[:, span:]
        low[nb:2 * nb, span:2 * span] = solved[:, 0:span]
        left = jnp.where(
            lane_all < nb,
            turned(mat[0, :, q:q + 128], back),
            jnp.where(lane_all < 2 * nb, turned(mat[1, :, q:q + 128], (back + nb) % 128), 0.0),
        )
        if (j + 1) * nb < n:
            ahead = left[after]
            next_re = mat[0, after, start:start + 128] - exact(ahead, low[:, 0:128])
            next_im = mat[1, after, start:start + 128] - exact(ahead, low[:, span:span + 128])
            m = inverse(next_re, next_im, (128 - ((j + 1) * nb) % 128) % 128)
        change = exact(left, low[:, 0:2 * span])
        mat[0, :, start:] = mat[0, :, start:] - change[:, 0:span]
        mat[1, :, start:] = mat[1, :, start:] - change[:, span:]
        mat[0, rows, start:] = solved[:, 0:span]
        mat[1, rows, start:] = solved[:, span:]
    x_ref[...] = mat[:, :, n:]


def split(x):
    high = x.astype(jnp.bfloat16)
    return high, (x - high.astype(jnp.float32)).astype(jnp.bfloat16)


def threefold(a, b, dims=((1,), (0,))):
    def one(x, y):
        return lax.dot_general(x, y, (dims, ((), ())), preferred_element_type=jnp.float32)

    return one(a[0], b[0]) + (one(a[0], b[1]) + one(a[1], b[0]))


def update_kernel(box_count, box_total, entries, where_ref, nb_ref, kern_ref, x_ref, pivot_ref,
                  out_ref):
    n = x_ref.shape[1]
    box = where_ref[1]
    first = where_ref[2] * entries
    out_ref[...] = jnp.zeros_like(out_ref)
    xr, xi = x_ref[0], x_ref[1]
    right = split(jnp.concatenate(
        [jnp.concatenate([xr, xi], axis=1), jnp.concatenate([-xi, xr], axis=1)], axis=0))
    pieces = range(pivot_ref.shape[0])
    qr = jnp.concatenate([pivot_ref[c, box, 0:1, :] for c in pieces], axis=1)
    qi = jnp.concatenate([pivot_ref[c, box, 1:2, :] for c in pieces], axis=1)
    nt = ((1,), (1,))
    for k in range(entries):
        slot = slot_of(nb_ref, where_ref, box, first + k, box_count, box_total)
        left = split(jnp.concatenate([kern_ref[k, 0, :, 0:n], kern_ref[k, 1, :, 0:n]], axis=1))
        both = threefold(left, right)
        br = kern_ref[k, 0, :, n:] - both[:, 0:n]
        bi = kern_ref[k, 1, :, n:] - both[:, n:]
        wr = split(br * qr - bi * qi)
        wi = split(br * qi + bi * qr)
        sr, si = split(br), split(bi)
        out_ref[slot, 0] = out_ref[slot, 0] - (threefold(wr, sr, nt) - threefold(wi, si, nt))
        out_ref[slot, 1] = out_ref[slot, 1] - (threefold(wr, si, nt) + threefold(wi, sr, nt))


MESH = pl.DeviceIdType.MESH


def meet(peers):
    barrier = pltpu.get_barrier_semaphore()
    for peer in peers:
        pl.semaphore_signal(barrier, inc=1, device_id=peer, device_id_type=MESH)
    pl.semaphore_wait(barrier, len(peers))


def exchange_kernel(box_total, col_count, group, points_ref, order_ref, proxy_ref, pivot_ref,
                    points_out, order_out, proxy_out, pivot_out, send, recv, local):
    me = lax.axis_index("col")
    place = lax.axis_index("box")
    after = {"box": lax.rem(place + 1, box_total)}
    before = {"box": lax.rem(place + box_total - 1, box_total)}
    peers = [{"col": lax.rem(me + d, col_count)} for d in range(1, col_count)]
    meet([before, after] + peers)
    jobs = [
        (points_ref, points_out.at[0], after),
        (points_ref, points_out.at[2], before),
        (order_ref, order_out.at[0], after),
        (order_ref, order_out.at[2], before),
    ]
    for d in range(1, col_count):
        jobs.append((pivot_ref, pivot_out.at[me], peers[d - 1]))
        if d % group == 0:
            jobs.append((proxy_ref, proxy_out.at[d // group], peers[d - 1]))
    copies = []
    for i, (source, target, peer) in enumerate(jobs):
        copy = pltpu.make_async_remote_copy(
            src_ref=source, dst_ref=target, send_sem=send.at[i], recv_sem=recv.at[i],
            device_id=peer, device_id_type=MESH)
        copy.start()
        copies.append(copy)
    own = ((points_ref, points_out.at[1]), (order_ref, order_out.at[1]),
           (proxy_ref, proxy_out.at[0]), (pivot_ref, pivot_out.at[me]))
    for i, (source, target) in enumerate(own):
        copy = pltpu.make_async_copy(source, target, local.at[i])
        copy.start()
        copies.append(copy)
    for copy in copies:
        copy.wait()


def swap_kernel(mine_ref, other_ref, send, recv):
    me = lax.axis_index("col")
    peer = {"col": me + 1 - 2 * lax.rem(me, 2)}
    meet([peer])
    copies = []
    for i in range(mine_ref.shape[0]):
        copy = pltpu.make_async_remote_copy(
            src_ref=mine_ref.at[i], dst_ref=other_ref.at[i], send_sem=send.at[i],
            recv_sem=recv.at[i], device_id=peer, device_id_type=MESH)
        copy.start()
        copies.append(copy)
    for copy in copies:
        copy.wait()


def reduce_kernel(box_total, col_count, group, buf_ref, out_ref, pair_in, cross_out, cross_in,
                  held, box_in, send, recv):
    me = lax.axis_index("col")
    place = lax.axis_index("box")
    partner = me + 1 - 2 * lax.rem(me, 2)
    across = lax.rem(me + group, col_count)
    far = lax.rem(partner + group, col_count)
    near_id, far_id = {"col": partner}, {"col": across}
    after = {"box": lax.rem(place + 1, box_total)}
    before = {"box": lax.rem(place + box_total - 1, box_total)}
    meet([near_id, far_id, before, after])
    width = out_ref.shape[0]

    def copy(index, source, target, peer):
        one = pltpu.make_async_remote_copy(
            src_ref=source, dst_ref=target, send_sem=send.at[index], recv_sem=recv.at[index],
            device_id=peer, device_id_type=MESH)
        one.start()
        return one

    box = me // group
    fed = 1 - box
    pairs = {}
    for kind, block in ((0, far), (1, partner)):
        for g in (0, 2):
            source = buf_ref.at[pl.ds(g * width, width), :, block]
            pairs[g, kind] = copy(2 * g + kind, source, pair_in.at[g, kind], near_id)
        pairs[1, kind] = copy(2 + kind, buf_ref.at[width + fed, :, block],
                              pair_in.at[1, kind, 0], near_id)
    cross = {}
    for g in (0, 2):
        pairs[g, 0].wait()
        cross_out[g] = buf_ref[g * width:(g + 1) * width, :, across] + pair_in[g, 0]
        cross[g] = copy(6 + g, cross_out.at[g], cross_in.at[g], far_id)
    pairs[1, 0].wait()
    cross_out[1, 0] = buf_ref[width + fed, :, across] + pair_in[1, 0, 0]
    cross[1] = copy(7, cross_out.at[1, 0], cross_in.at[1, 0], far_id)
    for g in (0, 2):
        pairs[g, 1].wait()
        held[g] = buf_ref[g * width:(g + 1) * width, :, me] + pair_in[g, 1]
    pairs[1, 1].wait()
    held[1, fed] = buf_ref[width + fed, :, me] + pair_in[1, 1, 0]
    moves = []
    for side, (g, peer) in enumerate(((0, before), (2, after))):
        cross[g].wait()
        held[g] = held[g] + cross_in[g]
        moves.append(copy(9 + side, held.at[g], box_in.at[side], peer))
    cross[1].wait()
    held[1, box] = cross_in[1, 0]
    moves[0].wait()
    held[1] = held[1] + box_in[0]
    moves[1].wait()
    out_ref[...] = held[1] + box_in[1]


def ring(count, step):
    return [(i, (i + step) % count) for i in range(count)]


def on_device(
    box_points, proxy_directions, point_order, neighbour_boxes, neighbour_places, pivot_inverse
):
    box_count, _, point_count = box_points.shape
    col_count = lax.axis_size("col")
    box_total = lax.axis_size("box")
    col_index = lax.axis_index("col")
    box_index = lax.axis_index("box")
    group = col_count // box_count
    box = col_index // group
    part = col_index % group
    entries = neighbour_boxes.shape[1] // group
    width = pivot_inverse.shape[2]
    where = jnp.stack([box_index, box, part]).astype(jnp.int32)

    jobs = 4 + col_count - 1 + box_count - 1
    points, order, proxies, pivots = pl.pallas_call(
        functools.partial(exchange_kernel, box_total, col_count, group),
        out_shape=(
            jax.ShapeDtypeStruct((3,) + box_points.shape, jnp.float32),
            jax.ShapeDtypeStruct((3,) + point_order.shape, jnp.int32),
            jax.ShapeDtypeStruct((box_count,) + proxy_directions.shape, jnp.float32),
            jax.ShapeDtypeStruct((col_count,) + pivot_inverse.shape, jnp.float32),
        ),
        in_specs=[pl.BlockSpec(memory_space=pl.ANY)] * 4,
        out_specs=(VMEM,) * 4,
        scratch_shapes=[pltpu.SemaphoreType.DMA((jobs,)), pltpu.SemaphoreType.DMA((jobs,)),
                        pltpu.SemaphoreType.DMA((4,))],
        compiler_params=params(collective_id=0, has_side_effects=True),
    )(box_points, point_order, proxy_directions, pivot_inverse)

    share = proxy_directions.shape[1]
    rows = box_count * share + entries * point_count
    cross, kern = pl.pallas_call(
        functools.partial(tile_kernel, box_count, box_total, entries),
        out_shape=(
            jax.ShapeDtypeStruct((2, S, point_count), jnp.float32),
            jax.ShapeDtypeStruct((entries, 2, S, point_count), jnp.float32),
        ),
        in_specs=[SMEM, SMEM, SMEM, VMEM, VMEM, VMEM],
        out_specs=(VMEM, VMEM),
        scratch_shapes=[
            pltpu.VMEM((rows, 128), jnp.float32),
            pltpu.VMEM((8, point_count), jnp.float32),
            pltpu.VMEM((8, point_count), jnp.float32),
            pltpu.VMEM((2, 2 * S, 2 * point_count), jnp.bfloat16),
            pltpu.VMEM((S, 2 * point_count), jnp.float32),
        ],
        compiler_params=params(),
    )(where, neighbour_boxes, neighbour_places, points, order, proxies)

    other = pl.pallas_call(
        swap_kernel,
        out_shape=jax.ShapeDtypeStruct(cross.shape, jnp.float32),
        in_specs=[VMEM],
        out_specs=VMEM,
        scratch_shapes=[pltpu.SemaphoreType.DMA((2,)), pltpu.SemaphoreType.DMA((2,))],
        compiler_params=params(collective_id=2, has_side_effects=True),
    )(cross)
    rest = point_count - S
    solved = pl.pallas_call(
        solve_kernel,
        out_shape=jax.ShapeDtypeStruct((2, S, rest), jnp.float32),
        in_specs=[VMEM, VMEM],
        out_specs=VMEM,
        scratch_shapes=[
            pltpu.VMEM((2, S, point_count), jnp.float32),
            pltpu.VMEM((128, 2 * point_count), jnp.float32),
            pltpu.VMEM((128, 2 * point_count), jnp.float32),
        ],
        compiler_params=params(),
    )(cross, other)

    mine = lax.dynamic_slice_in_dim(solved, col_index * width, width, 2)
    far = (col_index + group) % col_count
    sent = lax.dynamic_slice_in_dim(solved, far * width, width, 2)
    arrived = lax.ppermute(sent, "col", ring(col_count, group))
    interpolation = jnp.where(box == 0, jnp.stack([mine, arrived]), jnp.stack([arrived, mine]))

    buffer = pl.pallas_call(
        functools.partial(update_kernel, box_count, box_total, entries),
        out_shape=jax.ShapeDtypeStruct((3 * box_count, 2, S, S), jnp.float32),
        in_specs=[SMEM, SMEM, VMEM, VMEM, VMEM],
        out_specs=VMEM,
        compiler_params=params(),
    )(where, neighbour_boxes, kern, solved, pivots)

    strip = S // col_count
    block = (box_count, 2, strip, S)
    skeleton_update = pl.pallas_call(
        functools.partial(reduce_kernel, box_total, col_count, group),
        out_shape=jax.ShapeDtypeStruct(block, jnp.float32),
        in_specs=[VMEM],
        out_specs=VMEM,
        scratch_shapes=[
            pltpu.VMEM((3, 2) + block, jnp.float32),
            pltpu.VMEM((3,) + block, jnp.float32),
            pltpu.VMEM((3,) + block, jnp.float32),
            pltpu.VMEM((3,) + block, jnp.float32),
            pltpu.VMEM((2,) + block, jnp.float32),
            pltpu.SemaphoreType.DMA((11,)),
            pltpu.SemaphoreType.DMA((11,)),
        ],
        compiler_params=params(collective_id=1, has_side_effects=True),
    )(buffer.reshape(3 * box_count, 2, col_count, strip, S))
    return (interpolation, skeleton_update)


def solution(mesh):
    placed = (
        P("box", None, None),
        P(None, "col"),
        P("box", None),
        P("box", None),
        P("box", None),
        P("box", None, "col"),
    )
    return jax.shard_map(
        on_device,
        mesh=mesh,
        in_specs=placed,
        out_specs=(P("box", None, None, "col"), P("box", None, "col", None)),
        check_vma=False,
    )
```

profile of v0, /device:TPU:0, one launch (start us, length us, event | category | flops | bytes accessed | tf_op | source)
XLA Modules:
  0.0 84.3 jit_solution(15790618578099494919)
XLA Ops:
  0.6 0.0 copy-start.3
  0.7 0.7 copy.8.points_ref
  1.4 0.1 pad_add_fusion.where_ref
  1.5 0.0 copy-start.4
  1.5 0.7 copy-done.4
  2.1 0.0 copy-start.5
  2.1 0.7 copy-done.5
  2.8 0.0 copy-start.6
  2.8 0.7 copy-done.6
  3.5 9.5 %shard_map.77 = (f32[3,2,3,512]{3,2,1,0:T(4,128)S(1)}, s32[3,2,512]{2,1,0:T(2,128)S(1)}, f32[2,3,256]{2,1,0:T(4,128)S(1)}, f32[4,2,2,64]{3,2,1,0:T(2,128)S(1)}) custom-call(f32[2,3,512]{2,1,0:T(4,128)S(1)} %copy.8.points_ref, s32[2,512]{1,0:T(2,128)S(1)} %copy-done.4, f32[3,256]{1,0:T(4,128)S(1)} %copy-done.5, f32[2,2,64]{2,1,0:T(2,128)S(1)} %copy-done.6), custom_call_target="tpu_custom_call" | custom-call | tf_op jit(solution)/shard_map/pallas_call | solution.py:416
  13.0 0.0 copy-start.2
  13.0 0.7 copy-done.2
  13.7 0.0 copy-start.7
  13.7 0.7 copy-done.7
  14.4 11.0 %shard_map.78 = (f32[2,256,512]{2,1,0:T(8,128)S(1)}, f32[4,2,256,512]{3,2,1,0:T(8,128)S(1)}) custom-call(s32[3]{0:T(128)S(1)} %pad_add_fusion.where_ref, s32[2,8]{1,0:T(2,128)S(1)} %copy-done.2, s32[2,8]{1,0:T(2,128)S(1)} %copy-done.7, f32[3,2,3,512]{3,2,1,0:T(4,128)S(1)} %get-tuple-element.8.points_ref, s32[3,2,512]{2,1,0:T(2,128)S(1)} %get-tuple-element.9.order_ref, ...), custom_call_target="tpu_custom_call" | custom-call | tf_op jit(solution)/shard_map/pallas_call | solution.py:433
  25.4 0.0 copy-start
  25.4 1.9 %copy-done = f32[4,2,256,512]{3,2,1,0:T(8,128)} copy-done((f32[4,2,256,512]{3,2,1,0:T(8,128)}, f32[4,2,256,512]{3,2,1,0:T(8,128)S(1)}, u32[]{:S(2)}) %copy-start) | copy-done | bytes 4194328
  27.3 2.7 %shard_map.79.other_ref = f32[2,256,512]{2,1,0:T(8,128)S(1)} custom-call(f32[2,256,512]{2,1,0:T(8,128)S(1)} %get-tuple-element.11.mine_ref), custom_call_target="tpu_custom_call" | custom-call | tf_op jit(solution)/shard_map/pallas_call | solution.py:451
  30.0 18.0 %shard_map.80.x_ref = f32[2,256,256]{2,1,0:T(8,128)S(1)} custom-call(f32[2,256,512]{2,1,0:T(8,128)S(1)} %get-tuple-element.11.mine_ref, f32[2,256,512]{2,1,0:T(8,128)S(1)} %shard_map.79.other_ref), custom_call_target="tpu_custom_call" | custom-call | tf_op jit(solution)/shard_map/pallas_call | solution.py:460
  48.0 0.2 dynamic-slice_bitcast_fusion
  48.2 0.6 collective-permute-start
  48.8 0.0 copy-done.3
  48.8 0.0 copy-start.1
  48.8 2.2 %copy-done.1 = f32[4,2,256,512]{3,2,1,0:T(8,128)S(1)} copy-done((f32[4,2,256,512]{3,2,1,0:T(8,128)S(1)}, f32[4,2,256,512]{3,2,1,0:T(8,128)}, u32[]{:S(2)}) %copy-start.1) | copy-done | bytes 4194328
  51.0 5.2 %shard_map.81 = f32[6,2,256,256]{3,2,1,0:T(8,128)S(1)} custom-call(s32[3]{0:T(128)S(1)} %pad_add_fusion.where_ref, s32[2,8]{1,0:T(2,128)S(1)} %copy-done.3, f32[4,2,256,512]{3,2,1,0:T(8,128)S(1)} %copy-done.1, f32[2,256,256]{2,1,0:T(8,128)S(1)} %shard_map.80.x_ref, f32[4,2,2,64]{3,2,1,0:T(2,128)S(1)} %get-tuple-element.13.pivot_ref), custom_call_target="tpu_custom_call" | custom-call | tf_op jit(solution)/shard_map/pallas_call | solution.py:479
  56.3 26.4 %shard_map.82 = f32[2,2,64,256]{3,2,1,0:T(8,128)S(1)} custom-call(f32[6,2,4,64,256]{4,3,2,1,0:T(8,128)S(1)} %bitcast.7), custom_call_target="tpu_custom_call" | custom-call | tf_op jit(solution)/shard_map/pallas_call | solution.py:489
  82.7 0.0 collective-permute-done
  82.7 0.9 %copy.9 = f32[2,2,256,64]{2,3,1,0:T(8,128)} copy(f32[2,2,256,64]{3,2,1,0:T(8,128)S(1)} %maximum_select_fusion) | data formatting | bytes 524288
  83.6 0.7 copy.11
  (1 shorter events, 0.0 us)
Async XLA Ops:
  0.6 48.2 %copy-start.3 = (s32[2,8]{1,0:T(2,128)S(1)}, s32[2,8]{1,0:T(2,128)}, u32[]{:S(2)}) copy-start(s32[2,8]{1,0:T(2,128)} %nb_ref.3) | copy-start | bytes 196
  1.5 0.7 copy-start.4
  2.1 0.7 copy-start.5
  2.8 0.7 copy-start.6
  13.0 0.7 copy-start.2
  13.7 0.7 copy-start.7
  25.4 2.0 %copy-start = (f32[4,2,256,512]{3,2,1,0:T(8,128)}, f32[4,2,256,512]{3,2,1,0:T(8,128)S(1)}, u32[]{:S(2)}) copy-start(f32[4,2,256,512]{3,2,1,0:T(8,128)S(1)} %get-tuple-element.12.kern_ref) | copy-start | bytes 12582916
  48.2 34.4 %collective-permute-start = (f32[2,256,64]{2,1,0:T(8,128)S(1)}, f32[2,256,64]{2,1,0:T(8,128)S(1)}, u32[]{:S(2)}, u32[]{:S(2)}) collective-permute-start(f32[2,256,64]{2,1,0:T(8,128)S(1)} %get-tuple-element.17), channel_id=1, source_target_pairs={{0,2},{1,3},{2,0},{3,1},{4,6},{5,7},{6,4},{7,5},{8,10},{9,11},{10,... | collective-permute-start | bytes 393224 | tf_op jit(solution)/shard_map/ppermute | solution.py:476
  48.8 2.2 %copy-start.1 = (f32[4,2,256,512]{3,2,1,0:T(8,128)S(1)}, f32[4,2,256,512]{3,2,1,0:T(8,128)}, u32[]{:S(2)}) copy-start(f32[4,2,256,512]{3,2,1,0:T(8,128)} %copy-done) | copy-start | bytes 12582916
where the time goes:
time: 84.7 us; the launch traced here: 84.3 us
  Pallas kernels  72.8 us (86%)
  local copies, waits for them, and re-layouts  10.1 us (12%)
    pallas_call x1, Pallas kernels, on_device(): pl.pallas_call(functools.partial(reduce_kernel, box_total, col_count, gro...  26.4 us
    pallas_call x1, Pallas kernels, on_device(): pl.pallas_call(solve_kernel, out_shape=jax.ShapeDtypeStruct((2, S, rest),...  18 us
    pallas_call x1, Pallas kernels, on_device(): pl.pallas_call(functools.partial(tile_kernel, box_count, box_total, entri...  11 us
    unnamed x19, local copies, waits for them, and re-layouts  9.85 us
    pallas_call x1, Pallas kernels, on_device(): pl.pallas_call(functools.partial(exchange_kernel, box_total, col_count, g...  9.48 us
    pallas_call x1, Pallas kernels, on_device(): pl.pallas_call(functools.partial(update_kernel, box_count, box_total, ent...  5.24 us
    pallas_call x1, Pallas kernels, on_device(): pl.pallas_call(swap_kernel, out_shape=jax.ShapeDtypeStruct(cross.shape, j...  2.69 us
  transfers between devices with their start and end apart: 1, of which 0 were waited for; matrix products, arithmetic and copies ran while one was open for 0% of the time, Pallas kernels for 38%

commit v1 on v0

v1 whole, which is shorter than its diff:
```python
import functools
import math

import jax
import jax.numpy as jnp
from jax import lax
from jax.experimental import pallas as pl
from jax.experimental.pallas import tpu as pltpu
from jax.sharding import PartitionSpec as P

softening = 0.05
proxy_radius = 1.5
ridge_share = 0.05
highest = lax.Precision.HIGHEST
NBLK = 32
BLOCK = 256
ROWS = 16
DEPTH = 64

SIN = (4.44287959, -7.30781805, 3.59778873, -0.79123822)
COS_TILE = (1.41420408, -6.97764206, 5.7152384, -1.72834866)
COS = (1.4142135381698608, -6.978850841522217, 5.739460468292236, -1.883557915687561, 0.3106880187988281)

HBM = pl.BlockSpec(memory_space=pltpu.HBM)
VMEM = pl.BlockSpec(memory_space=pltpu.VMEM)
SMEM = pl.BlockSpec(memory_space=pltpu.SMEM)
MESH = pl.DeviceIdType.MESH
F32 = jnp.float32
BF16 = jnp.bfloat16


def params(**more):
    return pltpu.CompilerParams(vmem_limit_bytes=24 * 1024 * 1024, **more)


def horner(coefficients, z):
    total = coefficients[-1] * z + coefficients[-2]
    for one in coefficients[-3::-1]:
        total = total * z + one
    return total


def kernel_values(square, cosine):
    inverse = lax.rsqrt(square)
    turns = square * inverse
    part = turns - jnp.floor(turns + 0.5)
    z = part * part
    amplitude = inverse * (1.0 / (2.0 * math.pi))
    sine = part * horner(SIN, z)
    scaled = amplitude * sine
    return amplitude - scaled * sine, scaled * horner(cosine, z)


def three(x):
    high = x.astype(BF16).astype(F32)
    rest = x - high
    mid = rest.astype(BF16).astype(F32)
    return high, mid, rest - mid


def row_three(block, row):
    third = lax.broadcasted_iota(jnp.int32, block.shape, 0) == 3
    return jnp.where(third, row, block)


def norm_of(points):
    return jnp.sum(points * points, axis=0, keepdims=True)


def stacked(groups):
    zero = jnp.zeros_like(groups[0])
    return jnp.concatenate(groups + [zero] * (DEPTH // 8 - len(groups)), axis=0).astype(BF16)


def target_rows(points):
    high, mid, low = three(points)
    n_high, n_mid, n_low = three(norm_of(points))
    return stacked([row_three(high, n_high), row_three(high, n_mid), row_three(mid, n_low),
                    row_three(high, 1.0), row_three(mid, 1.0), row_three(low, 1.0)])


def source_rows(points):
    high, mid, low = three(points)
    norm = norm_of(points) + 4.0 * softening * softening
    n_high, n_mid, n_low = three(norm)
    return stacked([row_three(-2.0 * high, 1.0), row_three(-2.0 * mid, 1.0),
                    row_three(-2.0 * high, 1.0), row_three(-2.0 * low, n_high),
                    row_three(-2.0 * mid, n_mid), row_three(-2.0 * high, n_low)])


def three_rows(points):
    rows = lax.broadcasted_iota(jnp.int32, points.shape, 0)
    return jnp.where(rows < 3, points, 0.0)


def shifted(points, code):
    code = jnp.where(code >= 13, code + 1, code)
    axis_row = lax.broadcasted_iota(jnp.int32, points.shape, 0)
    move = jnp.where(
        axis_row == 0,
        (code // 9 - 1).astype(F32),
        jnp.where(axis_row == 1, ((code // 3) % 3 - 1).astype(F32), (code % 3 - 1).astype(F32)),
    )
    return three_rows(2.0 * (points + (move - 0.5)))


def centred(points):
    return three_rows(2.0 * (points - 0.5))


def slot_of(nb_ref, row, entry, box_count, box_total):
    owner_box = nb_ref[row, entry]
    step = owner_box // box_count - lax.axis_index("box") + 1
    step = jnp.where(step < 0, step + box_total, step)
    step = jnp.where(step >= box_total, step - box_total, step)
    return step * box_count + owner_box % box_count


def dot_tn(a, b):
    return lax.dot_general(a, b, (((0,), (0,)), ((), ())), preferred_element_type=F32)


def meet(peers):
    barrier = pltpu.get_barrier_semaphore()
    for peer in peers:
        pl.semaphore_signal(barrier, inc=1, device_id=peer, device_id_type=MESH)
    return lambda: pl.semaphore_wait(barrier, len(peers))


def send(source, target, sends, recvs, index, peer):
    one = pltpu.make_async_remote_copy(
        src_ref=source, dst_ref=target, send_sem=sends.at[index], recv_sem=recvs.at[index],
        device_id=peer, device_id_type=MESH)
    one.start()
    return one


def exchange_kernel(box_total, col_count, group, skeleton, points_ref, order_ref, proxy_ref,
                    pivot_ref, points_out, proxy_out, pivot_out, points, order, sends, recvs,
                    local):
    me = lax.axis_index("col")
    place = lax.axis_index("box")
    box_count, _, count = points_ref.shape
    after = {"box": lax.rem(place + 1, box_total)}
    before = {"box": lax.rem(place + box_total - 1, box_total)}
    across = {"col": lax.rem(me + group, col_count)}
    mine = me // group
    own = ((points_ref, points), (order_ref, order), (proxy_ref, proxy_out.at[0]),
           (pivot_ref, pivot_out.at[mine]))
    loads = []
    for i, (source, target) in enumerate(own):
        copy = pltpu.make_async_copy(source, target, local.at[i])
        copy.start()
        loads.append(copy)
    arrived = meet([before, after, across])
    for copy in loads:
        copy.wait()
    width = (count - skeleton) // col_count
    for box in range(box_count):
        row = order[box:box + 1, :]
        strips = [row[:, skeleton + s * width:skeleton + (s + 1) * width]
                  for c in range(group) for s in range(c, col_count, group)]
        row = jnp.concatenate([row[:, 0:skeleton]] + strips, axis=1)
        one_hot = (lax.broadcasted_iota(jnp.int32, (count, count), 0) == row).astype(F32)
        whole = jnp.concatenate([points[box], jnp.zeros((5, count), F32)], axis=0)
        rows = jnp.concatenate(list(three(whole)) + [jnp.zeros_like(whole)], axis=0)
        picked = jnp.dot(rows.astype(BF16), one_hot.astype(BF16), preferred_element_type=F32)
        points_out[1, box] = (picked[0:8] + picked[8:16]) + picked[16:24]
    arrived()
    jobs = [
        send(points_out.at[1], points_out.at[0], sends, recvs, 0, after),
        send(points_out.at[1], points_out.at[2], sends, recvs, 1, before),
        send(proxy_ref, proxy_out.at[1], sends, recvs, 2, across),
        send(pivot_ref, pivot_out.at[mine], sends, recvs, 3, across),
    ]
    for copy in jobs:
        copy.wait()


def tile_kernel(box_total, entries, group, skeleton, nb_hbm, place_hbm, points_ref, proxy_ref,
                gram_ref, rest_ref, nb_ref, place_ref, targets, sources, tiles, total, local):
    count = points_ref.shape[3]
    box_count, _, share = proxy_ref.shape
    proxies = box_count * share
    me = lax.axis_index("col")
    box = me // group
    first = lax.rem(me, group) * entries
    loads = [pltpu.make_async_copy(nb_hbm, nb_ref, local.at[0]),
             pltpu.make_async_copy(place_hbm, place_ref, local.at[1])]
    for copy in loads:
        copy.start()
    sources[...] = source_rows(centred(points_ref[1, box]))
    for d in range(box_count):
        directions = jnp.concatenate([proxy_ref[d], jnp.zeros((5, share), F32)], axis=0)
        targets[:, d * share:(d + 1) * share] = target_rows((2.0 * proxy_radius) * directions)
    for copy in loads:
        copy.wait()
    for k in range(entries):
        slot = slot_of(nb_ref, box, first + k, box_count, box_total)
        here = shifted(points_ref[slot // box_count, slot % box_count], place_ref[box, first + k])
        targets[:, proxies + k * count:proxies + (k + 1) * count] = target_rows(here)
    block = tiles.shape[1] // 2

    def evaluate(base, slot):
        squares = dot_tn(targets[:, pl.ds(pl.multiple_of(base, block), block)], sources[...])
        for i in range(block // ROWS):
            inner = slice(i * ROWS, (i + 1) * ROWS)
            lower = slice(block + i * ROWS, block + (i + 1) * ROWS)
            for c in range(0, count, 256):
                here = slice(c, c + 256)
                there = slice(count + c, count + c + 256)
                real, imag = kernel_values(squares[inner, here], COS_TILE)
                real = real.astype(BF16)
                imag = imag.astype(BF16)
                tiles[slot, inner, here] = real
                tiles[slot, inner, there] = imag
                tiles[slot, lower, here] = imag
                tiles[slot, lower, there] = -real

    def gather(slot):
        total[...] += dot_tn(tiles[slot, :, 0:skeleton], tiles[slot])

    total[...] = jnp.zeros_like(total)
    evaluate(0, 0)
    for i in range(1, proxies // block):
        gather((i + 1) % 2)
        evaluate(i * block, i % 2)
    parity = (proxies // block) % 2
    per = count // block

    @pl.loop(0, entries)
    def _(k):
        base = proxies + k * count
        for i in range(per):
            gather((parity + i + 1) % 2)
            evaluate(base + i * block, (parity + i) % 2)

    gather((parity + per - 1) % 2)
    half = (count - skeleton) // group
    for p in range(2):
        gram_ref[p] = total[:, p * count:p * count + skeleton]
        for c in range(group):
            start = p * count + skeleton + c * half
            rest_ref[c, p] = total[:, start:start + half]


def swap_kernel(gram_ref, rest_ref, gram_out, rest_out, sends, recvs):
    me = lax.axis_index("col")
    side = lax.rem(me, 2)
    peer = {"col": me + 1 - 2 * side}
    meet([peer])()
    copies = []
    for i in range(2):
        copies.append(send(gram_ref.at[i], gram_out.at[i], sends, recvs, i, peer))
    for i in range(2):
        copies.append(send(rest_ref.at[1 - side, i], rest_out.at[i], sends, recvs, 2 + i, peer))
    for copy in copies:
        copy.wait()


def exact(a, b, dims=((1,), (0,))):
    return lax.dot_general(a, b, (dims, ((), ())), precision=highest,
                           preferred_element_type=F32)


def solve_kernel(group, gram_ref, rest_ref, gram_in, rest_in, x_ref, mat, low, high):
    n = x_ref.shape[1]
    wide = mat.shape[2]
    nb = NBLK
    side = lax.rem(lax.axis_index("col"), group)
    mat[:, :, 0:n] = gram_ref[...] + gram_in[...]
    mat[:, :, n:] = rest_ref[side] + rest_in[...]
    diagonal = lax.broadcasted_iota(jnp.int32, (n, n), 0) == lax.broadcasted_iota(
        jnp.int32, (n, n), 1
    )
    gram = mat[0, :, 0:n]
    ridge = ridge_share * jnp.sum(jnp.where(diagonal, gram, 0.0)) / n
    mat[0, :, 0:n] = gram + jnp.where(diagonal, ridge, 0.0)
    low[...] = jnp.zeros_like(low)
    high[...] = jnp.zeros_like(high)
    lane = lax.broadcasted_iota(jnp.int32, (nb, 128), 1)
    sub = lax.broadcasted_iota(jnp.int32, (nb, 128), 0)
    lane_all = lax.broadcasted_iota(jnp.int32, (n, 128), 1)

    def turned(block, shift):
        return pltpu.roll(block, shift, 1) if shift else block

    def inverse(block_re, block_im, back):
        re0, im0 = turned(block_re, back), turned(block_im, back)
        re1, im1 = turned(block_re, (back + nb) % 128), turned(block_im, (back + nb) % 128)
        zero = jnp.zeros_like(re0)
        m = jnp.where(lane < nb, re0, jnp.where(lane < 2 * nb, im1,
                                                jnp.where(lane - 2 * nb == sub, 1.0, zero)))
        w = jnp.where(lane < nb, -im0, jnp.where(lane < 2 * nb, re1,
                                                 jnp.where(lane - 3 * nb == sub, 1.0, zero)))

        def spread(block, k):
            return jnp.broadcast_to(block[:, k:k + 1], (nb, 128))

        for k in range(0, nb, 2):
            p0, p1 = spread(m, k), spread(m, k + 1)
            s0, s1 = spread(m, nb + k), spread(m, nb + k + 1)
            a, d = p0[k:k + 1], p1[k + 1:k + 2]
            br, bi = p1[k:k + 1], s1[k:k + 1]
            scale = 1.0 / (a * d - (br * br + bi * bi))
            m0, m1, w0, w1 = m[k:k + 1], m[k + 1:k + 2], w[k:k + 1], w[k + 1:k + 2]
            row_m0 = (d * m0 - (br * m1 + bi * w1)) * scale
            row_w0 = (d * w0 - (br * w1 - bi * m1)) * scale
            row_m1 = (a * m1 - (br * m0 - bi * w0)) * scale
            row_w1 = (a * w1 - (br * w0 + bi * m0)) * scale
            new_m = m - ((p0 * row_m0 + s0 * row_w0) + (p1 * row_m1 + s1 * row_w1))
            new_w = w - ((p0 * row_w0 - s0 * row_m0) + (p1 * row_w1 - s1 * row_m1))
            m = jnp.where(sub == k, row_m0, jnp.where(sub == k + 1, row_m1, new_m))
            w = jnp.where(sub == k, row_w0, jnp.where(sub == k + 1, row_w1, new_w))
        return m

    m = inverse(mat[0, 0:nb, 0:128], mat[1, 0:nb, 0:128], 0)
    for j in range(n // nb):
        rows = slice(j * nb, (j + 1) * nb)
        after = slice((j + 1) * nb, (j + 2) * nb)
        q = (j * nb) // 128 * 128
        back = (128 - (j * nb) % 128) % 128
        start = (j + 1) * nb // 128 * 128
        span = wide - start
        panel_re = mat[0, rows, start:]
        panel_im = mat[1, rows, start:]
        high[2 * nb:3 * nb, 0:span] = panel_re
        high[2 * nb:3 * nb, span:2 * span] = panel_im
        high[3 * nb:4 * nb, 0:span] = -panel_im
        high[3 * nb:4 * nb, span:2 * span] = panel_re
        solved = exact(m, high[:, 0:2 * span])
        low[0:nb, 0:2 * span] = solved
        low[nb:2 * nb, 0:span] = -solved[:, span:]
        low[nb:2 * nb, span:2 * span] = solved[:, 0:span]
        left = jnp.where(
            lane_all < nb,
            turned(mat[0, :, q:q + 128], back),
            jnp.where(lane_all < 2 * nb, turned(mat[1, :, q:q + 128], (back + nb) % 128), 0.0),
        )
        if (j + 1) * nb < n:
            ahead = left[after]
            next_re = mat[0, after, start:start + 128] - exact(ahead, low[:, 0:128])
            next_im = mat[1, after, start:start + 128] - exact(ahead, low[:, span:span + 128])
            m = inverse(next_re, next_im, (128 - ((j + 1) * nb) % 128) % 128)
        change = exact(left, low[:, 0:2 * span])
        mat[0, :, start:] = mat[0, :, start:] - change[:, 0:span]
        mat[1, :, start:] = mat[1, :, start:] - change[:, span:]
        mat[0, rows, start:] = solved[:, 0:span]
        mat[1, rows, start:] = solved[:, span:]
    x_ref[...] = mat[:, :, n:]


def split(x):
    high = x.astype(BF16)
    return high, (x - high.astype(F32)).astype(BF16)


def threefold(a, b, dims=((1,), (0,))):
    def one(x, y):
        return lax.dot_general(x, y, (dims, ((), ())), preferred_element_type=F32)

    return one(a[0], b[0]) + (one(a[0], b[1]) + one(a[1], b[0]))


def right_side(x):
    xr, xi = x[0], x[1]
    return split(jnp.concatenate(
        [jnp.concatenate([xr, xi], axis=1), jnp.concatenate([-xi, xr], axis=1)], axis=0))


def pivot_rows(pivot_ref, box):
    pieces = range(pivot_ref.shape[0])
    return [jnp.concatenate([pivot_ref[c, box, p:p + 1, :] for c in pieces], axis=1)
            for p in range(2)]


def fold(left, rest, right, pivots, rows, weighted, out_ref, slot):
    qr, qi = pivots
    width = qr.shape[1]
    held = weighted.shape[1] // 2
    both = rest - threefold(left, right)
    br, bi = both[:, 0:width], both[:, width:]
    wr = br * qr - bi * qi
    wi = br * qi + bi * qr
    weighted[0] = jnp.concatenate([wr, -wi], axis=1)
    weighted[1] = jnp.concatenate([wi, wr], axis=1)
    upper = jnp.concatenate([weighted[0, rows, :], weighted[1, rows, :]], axis=0)
    update = threefold(split(upper), split(both), ((1,), (1,)))
    half = update.shape[0] // 2
    out_ref[slot, 0] = out_ref[slot, 0] - update[0:half]
    out_ref[slot, 1] = out_ref[slot, 1] - update[half:]


def row_half(col_count, group, n):
    count = n // (col_count // group)
    me = lax.axis_index("col")
    return pl.ds(pl.multiple_of((me // group) * count, count), count)


def spread(squares, keep):
    for i in range(0, squares.shape[0], ROWS):
        inner = slice(i, i + ROWS)
        for c in range(0, squares.shape[1], 128):
            real, imag = kernel_values(squares[inner, c:c + 128], COS)
            keep(inner, c, real, imag)


def near_kernel(box_total, col_count, group, nb_ref, place_ref, points_ref, x_ref, pivot_ref,
                out_ref, high_ref, low_ref, rest_ref, sources, left, rest, weighted):
    n = x_ref.shape[1]
    width = x_ref.shape[2]
    box_count, _, count = points_ref.shape[1:]
    entries = nb_ref.shape[1]
    me = lax.axis_index("col")
    side = lax.rem(me, group)
    box = me // group
    fed = 1 - box
    out_ref[...] = jnp.zeros_like(out_ref)
    for i, which in enumerate((box, fed)):
        whole = source_rows(centred(points_ref[1, which]))
        half = whole[:, n:n + width]
        for c in range(1, group):
            half = jnp.where(side == c, whole[:, n + c * width:n + (c + 1) * width], half)
        sources[i, :, 0:n] = whole[:, 0:n]
        sources[i, :, n:] = half
    right = right_side(x_ref)
    pivots = pivot_rows(pivot_ref, box)
    rows = row_half(col_count, group, n)

    def evaluate(i, which, k, high, low, rest_at):
        slot = slot_of(nb_ref, which, k, box_count, box_total)
        here = shifted(points_ref[slot // box_count, slot % box_count], place_ref[which, k])
        squares = dot_tn(target_rows(here[:, 0:n]), sources[i])

        def keep(inner, c, real, imag):
            for p, value in enumerate((real, imag)):
                if c < n:
                    top, bottom = split(value)
                    high[inner, p * n + c:p * n + c + 128] = top
                    low[inner, p * n + c:p * n + c + 128] = bottom
                else:
                    rest_at[inner, p * width + c - n:p * width + c - n + 128] = value

        spread(squares, keep)

    def own(k, slot):
        evaluate(0, box, k, left.at[slot, 0], left.at[slot, 1], rest.at[slot])

    def other(k):
        evaluate(1, fed, k, high_ref.at[k], low_ref.at[k], rest_ref.at[k])

    def use(k, slot):
        to = slot_of(nb_ref, box, k, box_count, box_total)
        fold((left[slot, 0], left[slot, 1]), rest[slot], right, pivots, rows, weighted, out_ref,
             to)

    own(0, 0)

    @pl.loop(0, entries // 2)
    def _(pair):
        k = 2 * pair
        own(k + 1, 1)
        other(k)
        use(k, 0)
        own(jnp.minimum(k + 2, entries - 1), 0)
        other(k + 1)
        use(k + 1, 1)


def far_kernel(box_total, col_count, group, nb_ref, buf_ref, high_ref, low_ref, rest_ref, x_ref,
               mine_ref, pivot_ref, out_ref, inter_ref, weighted):
    n = x_ref.shape[1]
    entries, _, _ = rest_ref.shape
    me = lax.axis_index("col")
    box = me // group
    fed = 1 - box
    box_count = pivot_ref.shape[1]
    out_ref[...] = buf_ref[...]
    right = right_side(x_ref)
    pivots = pivot_rows(pivot_ref, fed)
    rows = row_half(col_count, group, n)
    strip = inter_ref.shape[2]
    for p in range(2):
        for ref, where in ((mine_ref, box), (x_ref, fed)):
            block = jnp.transpose(ref[p])
            piece = block[0:strip]
            for c in range(1, block.shape[0] // strip):
                piece = jnp.where(box == c, block[c * strip:(c + 1) * strip], piece)
            inter_ref[where, p] = piece

    @pl.loop(0, entries // 2)
    def _(pair):
        for i in range(2):
            k = 2 * pair + i
            to = slot_of(nb_ref, fed, k, box_count, box_total)
            fold((high_ref[k], low_ref[k]), rest_ref[k], right, pivots, rows, weighted.at[i],
                 out_ref, to)


def reduce_kernel(box_total, buf_ref, out_ref, pair_in, line_out, line_in, side_out, side_in,
                  held, sends, recvs):
    me = lax.axis_index("col")
    place = lax.axis_index("box")
    side = lax.rem(me, 2)
    odd = lax.rem(place, 2)
    near = {"col": me + 1 - 2 * side}
    relay = {"box": lax.rem(place + box_total + 4 * odd - 2, box_total)}
    source = {"box": lax.rem(place + box_total + 2 - 4 * odd, box_total)}
    twin = {"box": place + 1 - 2 * odd}
    meet([near, relay, source, twin])()
    box_count = out_ref.shape[0]
    order = (2 * odd, 2 - 2 * odd, 1)
    chunks = [(d, p) for d in range(box_count) for p in range(2)]
    pairs = {}
    for g, at in enumerate(order):
        for i, (d, p) in enumerate(chunks):
            pairs[g, i] = send(buf_ref.at[at * box_count + d, p, 1 - side], pair_in.at[g, d, p],
                               sends, recvs, len(chunks) * g + i, near)
    base = 3 * len(chunks)
    lines, sides = [], []
    for i, (d, p) in enumerate(chunks):
        pairs[0, i].wait()
        line_out[d, p] = buf_ref[order[0] * box_count + d, p, side] + pair_in[0, d, p]
        lines.append(send(line_out.at[d, p], line_in.at[d, p], sends, recvs, base + i, relay))
    for i, (d, p) in enumerate(chunks):
        pairs[1, i].wait()
        held[d, p] = buf_ref[order[1] * box_count + d, p, side] + pair_in[1, d, p]
    for i, (d, p) in enumerate(chunks):
        lines[i].wait()
        side_out[d, p] = held[d, p] + line_in[d, p]
        sides.append(send(side_out.at[d, p], side_in.at[d, p], sends, recvs,
                          base + len(chunks) + i, twin))
    for i, (d, p) in enumerate(chunks):
        pairs[2, i].wait()
        held[d, p] = buf_ref[box_count + d, p, side] + pair_in[2, d, p]
    for i, (d, p) in enumerate(chunks):
        sides[i].wait()
        out_ref[d, p] = held[d, p] + side_in[d, p]


def ring(count, step):
    return [(i, (i + step) % count) for i in range(count)]


def on_device(
    box_points, proxy_directions, point_order, neighbour_boxes, neighbour_places, pivot_inverse
):
    box_count, _, point_count = box_points.shape
    col_count = lax.axis_size("col")
    box_total = lax.axis_size("box")
    group = col_count // box_count
    listed = neighbour_boxes.shape[1]
    entries = listed // group
    width = pivot_inverse.shape[2]
    rest = width * col_count
    skeleton = point_count - rest
    half = rest // group
    share = proxy_directions.shape[1]
    dma = pltpu.SemaphoreType.DMA

    points, proxies, pivots = pl.pallas_call(
        functools.partial(exchange_kernel, box_total, col_count, group, skeleton),
        out_shape=(
            jax.ShapeDtypeStruct((3, box_count, 8, point_count), F32),
            jax.ShapeDtypeStruct((box_count,) + proxy_directions.shape, F32),
            jax.ShapeDtypeStruct((box_count,) + pivot_inverse.shape, F32),
        ),
        in_specs=[HBM] * 4,
        out_specs=(VMEM,) * 3,
        scratch_shapes=[pltpu.VMEM(box_points.shape, F32),
                        pltpu.VMEM(point_order.shape, jnp.int32),
                        dma((4,)), dma((4,)), dma((4,))],
        compiler_params=params(collective_id=0, has_side_effects=True),
    )(box_points, point_order, proxy_directions, pivot_inverse)

    rows = box_count * share + entries * point_count
    gram, right = pl.pallas_call(
        functools.partial(tile_kernel, box_total, entries, group, skeleton),
        out_shape=(
            jax.ShapeDtypeStruct((2, skeleton, skeleton), F32),
            jax.ShapeDtypeStruct((group, 2, skeleton, half), F32),
        ),
        in_specs=[HBM, HBM, VMEM, VMEM],
        out_specs=(VMEM, VMEM),
        scratch_shapes=[
            pltpu.SMEM(neighbour_boxes.shape, jnp.int32),
            pltpu.SMEM(neighbour_places.shape, jnp.int32),
            pltpu.VMEM((DEPTH, rows), BF16),
            pltpu.VMEM((DEPTH, point_count), BF16),
            pltpu.VMEM((2, 2 * BLOCK, 2 * point_count), BF16),
            pltpu.VMEM((skeleton, 2 * point_count), F32),
            dma((2,)),
        ],
        compiler_params=params(),
    )(neighbour_boxes, neighbour_places, points, proxies)

    gram_in, right_in = pl.pallas_call(
        swap_kernel,
        out_shape=(jax.ShapeDtypeStruct(gram.shape, F32),
                   jax.ShapeDtypeStruct(right.shape[1:], F32)),
        in_specs=[VMEM, VMEM],
        out_specs=(VMEM, VMEM),
        scratch_shapes=[dma((4,)), dma((4,))],
        compiler_params=params(collective_id=2, has_side_effects=True),
    )(gram, right)
    solved = pl.pallas_call(
        functools.partial(solve_kernel, group),
        out_shape=jax.ShapeDtypeStruct((2, skeleton, half), F32),
        in_specs=[VMEM] * 4,
        out_specs=VMEM,
        scratch_shapes=[
            pltpu.VMEM((2, skeleton, skeleton + half), F32),
            pltpu.VMEM((128, 2 * (skeleton + half)), F32),
            pltpu.VMEM((128, 2 * (skeleton + half)), F32),
        ],
        compiler_params=params(),
    )(gram, right, gram_in, right_in)
    arrived = lax.ppermute(solved, "col", ring(col_count, group))

    strips = skeleton // box_count
    buffer, high, low, kept = pl.pallas_call(
        functools.partial(near_kernel, box_total, col_count, group),
        out_shape=(
            jax.ShapeDtypeStruct((3 * box_count, 2, strips, skeleton), F32),
            jax.ShapeDtypeStruct((listed, skeleton, 2 * skeleton), BF16),
            jax.ShapeDtypeStruct((listed, skeleton, 2 * skeleton), BF16),
            jax.ShapeDtypeStruct((listed, skeleton, 2 * half), F32),
        ),
        in_specs=[SMEM, SMEM, VMEM, VMEM, VMEM],
        out_specs=(VMEM,) * 4,
        scratch_shapes=[
            pltpu.VMEM((box_count, DEPTH, skeleton + half), BF16),
            pltpu.VMEM((2, 2, skeleton, 2 * skeleton), BF16),
            pltpu.VMEM((2, skeleton, 2 * half), F32),
            pltpu.VMEM((2, skeleton, 2 * half), F32),
        ],
        compiler_params=params(),
        cost_estimate=pl.CostEstimate(flops=4 * 10**9, bytes_accessed=8 * 10**6,
                                      transcendentals=0),
    )(neighbour_boxes, neighbour_places, points, solved, pivots)

    buffer, inter = pl.pallas_call(
        functools.partial(far_kernel, box_total, col_count, group),
        out_shape=(
            jax.ShapeDtypeStruct(buffer.shape, F32),
            jax.ShapeDtypeStruct((box_count, 2, width, skeleton), F32),
        ),
        in_specs=[SMEM] + [VMEM] * 7,
        out_specs=(VMEM, VMEM),
        scratch_shapes=[pltpu.VMEM((2, 2, skeleton, 2 * half), F32)],
        compiler_params=params(),
    )(neighbour_boxes, buffer, high, low, kept, arrived, solved, pivots)
    interpolation = jnp.swapaxes(inter, 2, 3)

    strip = skeleton // col_count
    block = (box_count, 2, strip, skeleton)
    jobs = 5 * 2 * box_count
    skeleton_update = pl.pallas_call(
        functools.partial(reduce_kernel, box_total),
        out_shape=jax.ShapeDtypeStruct(block, F32),
        in_specs=[VMEM],
        out_specs=VMEM,
        scratch_shapes=[
            pltpu.VMEM((3,) + block, F32),
            pltpu.VMEM(block, F32),
            pltpu.VMEM(block, F32),
            pltpu.VMEM(block, F32),
            pltpu.VMEM(block, F32),
            pltpu.VMEM(block, F32),
            dma((jobs,)),
            dma((jobs,)),
        ],
        compiler_params=params(collective_id=1, has_side_effects=True),
    )(buffer.reshape(3 * box_count, 2, group, strip, skeleton))
    return (interpolation, skeleton_update)


def solution(mesh):
    placed = (
        P("box", None, None),
        P(None, "col"),
        P("box", None),
        P("box", None),
        P("box", None),
        P("box", None, "col"),
    )
    return jax.shard_map(
        on_device,
        mesh=mesh,
        in_specs=placed,
        out_specs=(P("box", None, None, "col"), P("box", None, "col", None)),
        check_vma=False,
    )
```

time: 84.7 us -> 82.4 us (0.973)
  local copies, waits for them, and re-layouts: 10.1 us -> 4.85 us
  Pallas kernels: 72.8 us -> 75.9 us
    unnamed x19 -> x16, local copies, waits for them, and re-layouts: 9.85 us -> 4.85 us
    pallas_call x5 -> x6, Pallas kernels: 63.3 us -> 66.3 us  [the longest x1 17.5 us: on_device(): pl.pallas_call(functools.partial(solve_kernel, group), out_shape=jax.Shap...]
  transfers between devices with their start and end apart: 1 -> 1, of which waited for: 0 -> 0; matrix products, arithmetic and copies ran while one was open for 0% -> 0% of each run, Pallas kernels for 38% -> 15%
where the time goes in v1:
time: 82.4 us; the launch traced here: 82 us
  Pallas kernels  75.9 us (92%)
  local copies, waits for them, and re-layouts  4.85 us (6%)
    pallas_call x1, Pallas kernels, on_device(): pl.pallas_call(functools.partial(solve_kernel, group), out_shape=jax.Shap...  17.5 us
    pallas_call x1, Pallas kernels, on_device(): pl.pallas_call(functools.partial(reduce_kernel, box_total), out_shape=jax...  16 us
    pallas_call x1, Pallas kernels, on_device(): pl.pallas_call(functools.partial(near_kernel, box_total, col_count, group...  12.5 us
    pallas_call x1, Pallas kernels, on_device(): pl.pallas_call(functools.partial(tile_kernel, box_total, entries, group,...  10.1 us
    pallas_call x1, Pallas kernels, on_device(): pl.pallas_call(functools.partial(exchange_kernel, box_total, col_count, g...  9.54 us
    pallas_call x1, Pallas kernels, on_device(): pl.pallas_call(functools.partial(far_kernel, box_total, col_count, group)...  7.8 us
    unnamed x16, local copies, waits for them, and re-layouts  4.85 us
    pallas_call x1, Pallas kernels, on_device(): pl.pallas_call(swap_kernel, out_shape=(jax.ShapeDtypeStruct(gram.shape, F...  2.37 us
  transfers between devices with their start and end apart: 1, of which 0 were waited for; matrix products, arithmetic and copies ran while one was open for 0% of the time, Pallas kernels for 15%

profile of v1, /device:TPU:0, one launch (start us, length us, event | category | flops | bytes accessed | tf_op | source)
XLA Modules:
  0.0 82.0 jit_solution(4369138243764035404)
XLA Ops:
  0.6 0.0 copy-start.1
  0.6 0.0 copy-start.6
  0.7 0.7 copy.8.points_ref
  1.4 0.0 copy-start.2
  1.4 0.7 copy-done.2
  2.1 0.0 copy-start.3
  2.1 0.7 copy-done.3
  2.7 0.0 copy-start.4
  2.8 0.7 copy-done.4
  3.4 9.5 %shard_map.77 = (f32[3,2,8,512]{3,2,1,0:T(8,128)S(1)}, f32[2,3,256]{2,1,0:T(4,128)S(1)}, f32[2,2,2,64]{3,2,1,0:T(2,128)S(1)}) custom-call(f32[2,3,512]{2,1,0:T(4,128)S(1)} %copy.8.points_ref, s32[2,512]{1,0:T(2,128)S(1)} %copy-done.2, f32[3,256]{1,0:T(4,128)S(1)} %copy-done.3, f32[2,2,64]{2,1,0:T(2,128)S(1)} %copy-done.4), custom_call_target="tpu_custom_call" | custom-call | tf_op jit(solution)/shard_map/pallas_call | solution.py:561
  13.0 0.0 copy-start
  13.0 0.7 copy-done
  13.7 0.0 copy-start.5
  13.7 0.7 copy-done.5
  14.3 10.1 %shard_map.78 = (f32[2,256,256]{2,1,0:T(8,128)S(1)}, f32[2,2,256,128]{3,2,1,0:T(8,128)S(1)}) custom-call(s32[2,8]{1,0:T(2,128)S(1)} %copy-done, s32[2,8]{1,0:T(2,128)S(1)} %copy-done.5, f32[3,2,8,512]{3,2,1,0:T(8,128)S(1)} %get-tuple-element.15.points_ref, f32[2,3,256]{2,1,0:T(4,128)S(1)} %get-tuple-element.16.proxy_ref), custom_call_target="tpu_custom_call" | custom-call | tf_op jit(solution)/shard_map/pallas_call | solution.py:577
  24.5 2.4 %shard_map.79 = (f32[2,256,256]{2,1,0:T(8,128)S(1)}, f32[2,256,128]{2,1,0:T(8,128)S(1)}) custom-call(f32[2,256,256]{2,1,0:T(8,128)S(1)} %get-tuple-element.17.gram_ref, f32[2,2,256,128]{3,2,1,0:T(8,128)S(1)} %get-tuple-element.18.rest_ref), custom_call_target="tpu_custom_call" | custom-call | tf_op jit(solution)/shard_map/pallas_call | solution.py:597
  26.9 17.5 %shard_map.80.x_ref.mine_ref = f32[2,256,128]{2,1,0:T(8,128)S(1)} custom-call(f32[2,256,256]{2,1,0:T(8,128)S(1)} %get-tuple-element.17.gram_ref, f32[2,2,256,128]{3,2,1,0:T(8,128)S(1)} %get-tuple-element.18.rest_ref, f32[2,256,256]{2,1,0:T(8,128)S(1)} %get-tuple-element.19.gram_in, f32[2,256,128]{2,1,0:T(8,128)S(1)} %get-tuple-element.20.rest_in), custom_call_target="tpu_custom_call" | custom-call | tf_op jit(solution)/shard_map/pallas_call | solution.py:606
  44.4 0.6 collective-permute-start
  45.0 0.0 copy-done.1
  45.0 0.0 copy-done.6
  45.0 12.5 %shard_map.81 = (f32[6,2,128,256]{3,2,1,0:T(8,128)S(1)}, bf16[8,256,512]{2,1,0:T(8,128)(2,1)S(1)}, bf16[8,256,512]{2,1,0:T(8,128)(2,1)S(1)}, f32[8,256,256]{2,1,0:T(8,128)S(1)}) custom-call(s32[2,8]{1,0:T(2,128)S(1)} %copy-done.1, s32[2,8]{1,0:T(2,128)S(1)} %copy-done.6, f32[3,2,8,512]{3,2,1,0:T(8,128)S(1)} %get-tuple-element.15.points_ref, ...), custom_call_target="tpu_custom_call" | custom-call | flops 4000000000 | bytes 8000000 | tf_op jit(solution)/shard_map/pallas_call | solution.py:621
  57.5 0.0 collective-permute-done.x_ref
  57.5 7.8 %shard_map.82 = (f32[6,2,128,256]{3,2,1,0:T(8,128)S(1)}, f32[2,2,64,256]{3,2,1,0:T(8,128)}) custom-call(s32[2,8]{1,0:T(2,128)S(1)} %copy-done.1, f32[6,2,128,256]{3,2,1,0:T(8,128)S(1)} %get-tuple-element.22.buf_ref, bf16[8,256,512]{2,1,0:T(8,128)(2,1)S(1)} %get-tuple-element.23.high_ref, bf16[8,256,512]{2,1,0:T(8,128)(2,1)S(1)} %get-tuple-element.24.low_ref, ...), custom_call_target="tpu_custom_call" | custom-call | tf_op jit(solution)/shard_map/pallas_call | solution.py:642
  65.3 16.0 %shard_map.83 = f32[2,2,64,256]{3,2,1,0:T(8,128)S(1)} custom-call(f32[6,2,2,64,256]{4,3,2,1,0:T(8,128)S(1)} %bitcast.2), custom_call_target="tpu_custom_call" | custom-call | tf_op jit(solution)/shard_map/pallas_call | solution.py:658
  81.3 0.7 copy.10
Async XLA Ops:
  0.6 44.4 %copy-start.1 = (s32[2,8]{1,0:T(2,128)S(1)}, s32[2,8]{1,0:T(2,128)}, u32[]{:S(2)}) copy-start(s32[2,8]{1,0:T(2,128)} %nb_ref.3) | copy-start | bytes 196
  0.6 44.4 %copy-start.6 = (s32[2,8]{1,0:T(2,128)S(1)}, s32[2,8]{1,0:T(2,128)}, u32[]{:S(2)}) copy-start(s32[2,8]{1,0:T(2,128)} %place_ref.1) | copy-start | bytes 196
  1.4 0.7 copy-start.2
  2.1 0.7 copy-start.3
  2.7 0.7 copy-start.4
  13.0 0.7 copy-start
  13.7 0.7 copy-start.5
  44.4 13.1 %collective-permute-start = (f32[2,256,128]{2,1,0:T(8,128)S(1)}, f32[2,256,128]{2,1,0:T(8,128)S(1)}, u32[]{:S(2)}, u32[]{:S(2)}) collective-permute-start(f32[2,256,128]{2,1,0:T(8,128)S(1)} %shard_map.80.x_ref.mine_ref), channel_id=1, source_target_pairs={{0,2},{1,3},{2,0},{3,1},{4,6},{5,7},{6,4},{7,5},{8,10},{9,11},{10,... | collective-permute-start | bytes 786440 | tf_op jit(solution)/shard_map/ppermute | solution.py:618

commit v2 on v1

--- a/solution.py
+++ b/solution.py
@@ -11,7 +11,6 @@
 softening = 0.05
 proxy_radius = 1.5
 ridge_share = 0.05
-highest = lax.Precision.HIGHEST
 NBLK = 32
 BLOCK = 256
 ROWS = 16
@@ -258,36 +257,36 @@
         copy.wait()
 
 
-def exact(a, b, dims=((1,), (0,))):
-    return lax.dot_general(a, b, (dims, ((), ())), precision=highest,
-                           preferred_element_type=F32)
-
-
-def solve_kernel(group, gram_ref, rest_ref, gram_in, rest_in, x_ref, mat, low, high):
+def solve_kernel(group, gram_ref, rest_ref, gram_in, rest_in, x_ref, mat, head, tail):
     n = x_ref.shape[1]
-    wide = mat.shape[2]
     nb = NBLK
     side = lax.rem(lax.axis_index("col"), group)
-    mat[:, :, 0:n] = gram_ref[...] + gram_in[...]
     mat[:, :, n:] = rest_ref[side] + rest_in[...]
-    diagonal = lax.broadcasted_iota(jnp.int32, (n, n), 0) == lax.broadcasted_iota(
-        jnp.int32, (n, n), 1
+    ridge = 0.0
+    diagonal = lax.broadcasted_iota(jnp.int32, (128, 128), 0) == lax.broadcasted_iota(
+        jnp.int32, (128, 128), 1
     )
-    gram = mat[0, :, 0:n]
-    ridge = ridge_share * jnp.sum(jnp.where(diagonal, gram, 0.0)) / n
-    mat[0, :, 0:n] = gram + jnp.where(diagonal, ridge, 0.0)
-    low[...] = jnp.zeros_like(low)
-    high[...] = jnp.zeros_like(high)
+    gram = gram_ref[...] + gram_in[...]
+    for c in range(0, n, 128):
+        ridge = ridge + jnp.sum(jnp.where(diagonal, gram[0, c:c + 128, c:c + 128], 0.0))
+    ridge = ridge_share * ridge / n
+    mat[:, :, 0:n] = gram
+    for c in range(0, n, 128):
+        here = slice(c, c + 128)
+        mat[0, here, here] = gram[0, here, here] + jnp.where(diagonal, ridge, 0.0)
+    head[6 * nb:, :] = jnp.zeros_like(head[6 * nb:, :])
+    tail[6 * nb:, :] = jnp.zeros_like(tail[6 * nb:, :])
     lane = lax.broadcasted_iota(jnp.int32, (nb, 128), 1)
     sub = lax.broadcasted_iota(jnp.int32, (nb, 128), 0)
     lane_all = lax.broadcasted_iota(jnp.int32, (n, 128), 1)
 
     def turned(block, shift):
+        shift = shift % 128
         return pltpu.roll(block, shift, 1) if shift else block
 
     def inverse(block_re, block_im, back):
         re0, im0 = turned(block_re, back), turned(block_im, back)
-        re1, im1 = turned(block_re, (back + nb) % 128), turned(block_im, (back + nb) % 128)
+        re1, im1 = turned(block_re, back + nb), turned(block_im, back + nb)
         zero = jnp.zeros_like(re0)
         m = jnp.where(lane < nb, re0, jnp.where(lane < 2 * nb, im1,
                                                 jnp.where(lane - 2 * nb == sub, 1.0, zero)))
@@ -312,41 +311,81 @@
             new_w = w - ((p0 * row_w0 - s0 * row_m0) + (p1 * row_w1 - s1 * row_m1))
             m = jnp.where(sub == k, row_m0, jnp.where(sub == k + 1, row_m1, new_m))
             w = jnp.where(sub == k, row_w0, jnp.where(sub == k + 1, row_w1, new_w))
-        return m
-
-    m = inverse(mat[0, 0:nb, 0:128], mat[1, 0:nb, 0:128], 0)
+            yield m
+
+    def tripled(block):
+        high = block.astype(BF16)
+        return jnp.concatenate([high, (block - high.astype(F32)).astype(BF16)], axis=1)
+
+    def put(ref, w, re, im):
+        block = jnp.concatenate([jnp.concatenate([re, im], axis=1),
+                                 jnp.concatenate([-im, re], axis=1)], axis=0)
+        high, rest = split(block)
+        where = slice(256 * w, 256 * w + 256)
+        ref[0:2 * nb, where] = high
+        ref[2 * nb:4 * nb, where] = rest
+        ref[4 * nb:6 * nb, where] = high
+
+    def plain(a, b):
+        return jnp.dot(a, b, preferred_element_type=F32)
+
+    for m in inverse(mat[0, 0:nb, 0:128], mat[1, 0:nb, 0:128], 0):
+        pass
     for j in range(n // nb):
         rows = slice(j * nb, (j + 1) * nb)
         after = slice((j + 1) * nb, (j + 2) * nb)
         q = (j * nb) // 128 * 128
-        back = (128 - (j * nb) % 128) % 128
-        start = (j + 1) * nb // 128 * 128
-        span = wide - start
-        panel_re = mat[0, rows, start:]
-        panel_im = mat[1, rows, start:]
-        high[2 * nb:3 * nb, 0:span] = panel_re
-        high[2 * nb:3 * nb, span:2 * span] = panel_im
-        high[3 * nb:4 * nb, 0:span] = -panel_im
-        high[3 * nb:4 * nb, span:2 * span] = panel_re
-        solved = exact(m, high[:, 0:2 * span])
-        low[0:nb, 0:2 * span] = solved
-        low[nb:2 * nb, 0:span] = -solved[:, span:]
-        low[nb:2 * nb, span:2 * span] = solved[:, 0:span]
-        left = jnp.where(
-            lane_all < nb,
-            turned(mat[0, :, q:q + 128], back),
-            jnp.where(lane_all < 2 * nb, turned(mat[1, :, q:q + 128], (back + nb) % 128), 0.0),
-        )
+        back = -(j * nb)
+        windows = list(range((j + 1) * nb // 128, mat.shape[2] // 128))
+        window_re, window_im = mat[0, :, q:q + 128], mat[1, :, q:q + 128]
+        left = tripled(jnp.where(
+            lane_all < nb, turned(window_re, back),
+            jnp.where(lane_all < 2 * nb, turned(window_im, back + nb),
+                      jnp.where(lane_all < 3 * nb, turned(window_re, back + 2 * nb),
+                                turned(window_im, back + 3 * nb)))))
+        factor = tripled(jnp.where(lane < 2 * nb, turned(m, 64), m))
+        held = {}
+
+        def solve(w):
+            here = slice(128 * w, 128 * w + 128)
+            put(head, w, mat[0, rows, here], mat[1, rows, here])
+            held[w] = plain(factor, head[:, 256 * w:256 * w + 256])
+            put(tail, w, held[w][:, 0:128], held[w][:, 128:])
+
+        def change(w, part):
+            here = slice(128 * w, 128 * w + 128)
+            some = slice(part * 128, (part + 1) * 128)
+            less = plain(left[some], tail[:, 256 * w:256 * w + 256])
+            mat[0, some, here] = mat[0, some, here] - less[:, 0:128]
+            mat[1, some, here] = mat[1, some, here] - less[:, 128:]
+
+        def place(w):
+            here = slice(128 * w, 128 * w + 128)
+            mat[0, rows, here] = held[w][:, 0:128]
+            mat[1, rows, here] = held[w][:, 128:]
+
+        first = windows[0]
+        solve(first)
+        pivots = iter(())
         if (j + 1) * nb < n:
-            ahead = left[after]
-            next_re = mat[0, after, start:start + 128] - exact(ahead, low[:, 0:128])
-            next_im = mat[1, after, start:start + 128] - exact(ahead, low[:, span:span + 128])
-            m = inverse(next_re, next_im, (128 - ((j + 1) * nb) % 128) % 128)
-        change = exact(left, low[:, 0:2 * span])
-        mat[0, :, start:] = mat[0, :, start:] - change[:, 0:span]
-        mat[1, :, start:] = mat[1, :, start:] - change[:, span:]
-        mat[0, rows, start:] = solved[:, 0:span]
-        mat[1, rows, start:] = solved[:, span:]
+            here = slice(128 * first, 128 * first + 128)
+            less = plain(left[after], tail[:, 256 * first:256 * first + 256])
+            pivots = inverse(mat[0, after, here] - less[:, 0:128],
+                             mat[1, after, here] - less[:, 128:], -((j + 1) * nb))
+        tasks = [functools.partial(solve, w) for w in windows[1:]]
+        for w in windows:
+            tasks += [functools.partial(change, w, part) for part in range(n // 128)]
+            tasks.append(functools.partial(place, w))
+        steps = nb // 2
+        done = 0
+        for i, task in enumerate(tasks):
+            task()
+            upto = (i + 1) * steps // len(tasks)
+            for _ in range(upto - done):
+                m = next(pivots, m)
+            done = upto
+        for m in pivots:
+            pass
     x_ref[...] = mat[:, :, n:]
 
 
@@ -610,8 +649,8 @@
         out_specs=VMEM,
         scratch_shapes=[
             pltpu.VMEM((2, skeleton, skeleton + half), F32),
-            pltpu.VMEM((128, 2 * (skeleton + half)), F32),
-            pltpu.VMEM((128, 2 * (skeleton + half)), F32),
+            pltpu.VMEM((8 * NBLK, 2 * (skeleton + half)), BF16),
+            pltpu.VMEM((8 * NBLK, 2 * (skeleton + half)), BF16),
         ],
         compiler_params=params(),
     )(gram, right, gram_in, right_in)

time: 82.4 us -> 81.2 us (0.985)
  Pallas kernels: 75.9 us -> 74.7 us
    pallas_call x1, Pallas kernels: 17.5 us -> 16.6 us  [on_device(): pl.pallas_call(functools.partial(solve_kernel, group), out_shape=jax.Shap...]
where the time goes in v2:
time: 81.2 us; the launch traced here: 80.8 us
  Pallas kernels  74.7 us (92%)
  local copies, waits for them, and re-layouts  4.85 us (6%)
    pallas_call x1, Pallas kernels, on_device(): pl.pallas_call(functools.partial(solve_kernel, group), out_shape=jax.Shap...  16.6 us
    pallas_call x1, Pallas kernels, on_device(): pl.pallas_call(functools.partial(reduce_kernel, box_total), out_shape=jax...  16 us
    pallas_call x1, Pallas kernels, on_device(): pl.pallas_call(functools.partial(near_kernel, box_total, col_count, group...  12.3 us
    pallas_call x1, Pallas kernels, on_device(): pl.pallas_call(functools.partial(tile_kernel, box_total, entries, group,...  10.1 us
    pallas_call x1, Pallas kernels, on_device(): pl.pallas_call(functools.partial(exchange_kernel, box_total, col_count, g...  9.54 us
    pallas_call x1, Pallas kernels, on_device(): pl.pallas_call(functools.partial(far_kernel, box_total, col_count, group)...  7.8 us
    unnamed x16, local copies, waits for them, and re-layouts  4.85 us
    pallas_call x1, Pallas kernels, on_device(): pl.pallas_call(swap_kernel, out_shape=(jax.ShapeDtypeStruct(gram.shape, F...  2.37 us
  transfers between devices with their start and end apart: 1, of which 0 were waited for; matrix products, arithmetic and copies ran while one was open for 0% of the time, Pallas kernels for 15%

profile of v2, /device:TPU:0, one launch (start us, length us, event | category | flops | bytes accessed | tf_op | source)
XLA Modules:
  0.0 80.8 jit_solution(7546990630542883516)
XLA Ops:
  0.6 0.0 copy-start.1
  0.6 0.0 copy-start.6
  0.7 0.7 copy.8.points_ref
  1.4 0.0 copy-start.2
  1.4 0.7 copy-done.2
  2.1 0.0 copy-start.3
  2.1 0.7 copy-done.3
  2.7 0.0 copy-start.4
  2.8 0.7 copy-done.4
  3.4 9.5 %shard_map.77 = (f32[3,2,8,512]{3,2,1,0:T(8,128)S(1)}, f32[2,3,256]{2,1,0:T(4,128)S(1)}, f32[2,2,2,64]{3,2,1,0:T(2,128)S(1)}) custom-call(f32[2,3,512]{2,1,0:T(4,128)S(1)} %copy.8.points_ref, s32[2,512]{1,0:T(2,128)S(1)} %copy-done.2, f32[3,256]{1,0:T(4,128)S(1)} %copy-done.3, f32[2,2,64]{2,1,0:T(2,128)S(1)} %copy-done.4), custom_call_target="tpu_custom_call" | custom-call | tf_op jit(solution)/shard_map/pallas_call | solution.py:600
  13.0 0.0 copy-start
  13.0 0.7 copy-done
  13.7 0.0 copy-start.5
  13.7 0.7 copy-done.5
  14.3 10.1 %shard_map.78 = (f32[2,256,256]{2,1,0:T(8,128)S(1)}, f32[2,2,256,128]{3,2,1,0:T(8,128)S(1)}) custom-call(s32[2,8]{1,0:T(2,128)S(1)} %copy-done, s32[2,8]{1,0:T(2,128)S(1)} %copy-done.5, f32[3,2,8,512]{3,2,1,0:T(8,128)S(1)} %get-tuple-element.15.points_ref, f32[2,3,256]{2,1,0:T(4,128)S(1)} %get-tuple-element.16.proxy_ref), custom_call_target="tpu_custom_call" | custom-call | tf_op jit(solution)/shard_map/pallas_call | solution.py:616
  24.5 2.4 %shard_map.79 = (f32[2,256,256]{2,1,0:T(8,128)S(1)}, f32[2,256,128]{2,1,0:T(8,128)S(1)}) custom-call(f32[2,256,256]{2,1,0:T(8,128)S(1)} %get-tuple-element.17.gram_ref, f32[2,2,256,128]{3,2,1,0:T(8,128)S(1)} %get-tuple-element.18.rest_ref), custom_call_target="tpu_custom_call" | custom-call | tf_op jit(solution)/shard_map/pallas_call | solution.py:636
  26.9 16.6 %shard_map.80.x_ref.mine_ref = f32[2,256,128]{2,1,0:T(8,128)S(1)} custom-call(f32[2,256,256]{2,1,0:T(8,128)S(1)} %get-tuple-element.17.gram_ref, f32[2,2,256,128]{3,2,1,0:T(8,128)S(1)} %get-tuple-element.18.rest_ref, f32[2,256,256]{2,1,0:T(8,128)S(1)} %get-tuple-element.19.gram_in, f32[2,256,128]{2,1,0:T(8,128)S(1)} %get-tuple-element.20.rest_in), custom_call_target="tpu_custom_call" | custom-call | tf_op jit(solution)/shard_map/pallas_call | solution.py:645
  43.4 0.6 collective-permute-start
  44.0 0.0 copy-done.1
  44.0 0.0 copy-done.6
  44.0 12.3 %shard_map.81 = (f32[6,2,128,256]{3,2,1,0:T(8,128)S(1)}, bf16[8,256,512]{2,1,0:T(8,128)(2,1)S(1)}, bf16[8,256,512]{2,1,0:T(8,128)(2,1)S(1)}, f32[8,256,256]{2,1,0:T(8,128)S(1)}) custom-call(s32[2,8]{1,0:T(2,128)S(1)} %copy-done.1, s32[2,8]{1,0:T(2,128)S(1)} %copy-done.6, f32[3,2,8,512]{3,2,1,0:T(8,128)S(1)} %get-tuple-element.15.points_ref, ...), custom_call_target="tpu_custom_call" | custom-call | flops 4000000000 | bytes 8000000 | tf_op jit(solution)/shard_map/pallas_call | solution.py:660
  56.3 0.0 collective-permute-done.x_ref
  56.3 7.8 %shard_map.82 = (f32[6,2,128,256]{3,2,1,0:T(8,128)S(1)}, f32[2,2,64,256]{3,2,1,0:T(8,128)}) custom-call(s32[2,8]{1,0:T(2,128)S(1)} %copy-done.1, f32[6,2,128,256]{3,2,1,0:T(8,128)S(1)} %get-tuple-element.22.buf_ref, bf16[8,256,512]{2,1,0:T(8,128)(2,1)S(1)} %get-tuple-element.23.high_ref, bf16[8,256,512]{2,1,0:T(8,128)(2,1)S(1)} %get-tuple-element.24.low_ref, ...), custom_call_target="tpu_custom_call" | custom-call | tf_op jit(solution)/shard_map/pallas_call | solution.py:681
  64.1 16.0 %shard_map.83 = f32[2,2,64,256]{3,2,1,0:T(8,128)S(1)} custom-call(f32[6,2,2,64,256]{4,3,2,1,0:T(8,128)S(1)} %bitcast.2), custom_call_target="tpu_custom_call" | custom-call | tf_op jit(solution)/shard_map/pallas_call | solution.py:697
  80.1 0.7 copy.10
Async XLA Ops:
  0.6 43.4 %copy-start.1 = (s32[2,8]{1,0:T(2,128)S(1)}, s32[2,8]{1,0:T(2,128)}, u32[]{:S(2)}) copy-start(s32[2,8]{1,0:T(2,128)} %nb_ref.3) | copy-start | bytes 196
  0.6 43.4 %copy-start.6 = (s32[2,8]{1,0:T(2,128)S(1)}, s32[2,8]{1,0:T(2,128)}, u32[]{:S(2)}) copy-start(s32[2,8]{1,0:T(2,128)} %place_ref.1) | copy-start | bytes 196
  1.4 0.7 copy-start.2
  2.1 0.7 copy-start.3
  2.7 0.7 copy-start.4
  13.0 0.7 copy-start
  13.7 0.7 copy-start.5
  43.4 12.9 %collective-permute-start = (f32[2,256,128]{2,1,0:T(8,128)S(1)}, f32[2,256,128]{2,1,0:T(8,128)S(1)}, u32[]{:S(2)}, u32[]{:S(2)}) collective-permute-start(f32[2,256,128]{2,1,0:T(8,128)S(1)} %shard_map.80.x_ref.mine_ref), channel_id=1, source_target_pairs={{0,2},{1,3},{2,0},{3,1},{4,6},{5,7},{6,4},{7,5},{8,10},{9,11},{10,... | collective-permute-start | bytes 786440 | tf_op jit(solution)/shard_map/ppermute | solution.py:657

commit v3 on v2

--- a/solution.py
+++ b/solution.py
@@ -257,110 +257,141 @@
         copy.wait()
 
 
+def lanes(block, k):
+    return jnp.take_along_axis(block, jnp.full(block.shape, k, jnp.int32), axis=1)
+
+
+def across_rows(block, k):
+    return jnp.broadcast_to(block[k:k + 1, :], block.shape)
+
+
+def block_inverse(re, im, start, home):
+    count = len(re)
+    shape = re[0].shape
+    lane = lax.broadcasted_iota(jnp.int32, shape, 1)
+    sub = lax.broadcasted_iota(jnp.int32, shape, 0)
+    inside = (lane >= start) & (lane < start + 8 * count)
+    re = [jnp.where(inside, block, jnp.where(lane - home == sub + 8 * v, 1.0, 0.0))
+          for v, block in enumerate(re)]
+    im = [jnp.where(inside, block, 0.0) for block in im]
+    for r in range(count):
+        order = [r] + [v for v in range(count) if v > r] + list(range(r))
+        spread = {}
+        for v in order:
+            for j in range(8):
+                k = start + 8 * r + j
+                spread[v, j] = (lanes(re[v], k), lanes(im[v], k))
+        cols = {j: spread[r, j] for j in range(8)}
+        cols["row"] = (re[r], im[r])
+        for t in range(0, 8, 2):
+            (ar, ai), (cr, ci) = cols.pop(t), cols.pop(t + 1)
+            a, d = across_rows(ar, t), across_rows(cr, t + 1)
+            br, bi = across_rows(cr, t), across_rows(ci, t)
+            scale = 1.0 / (a * d - (br * br + bi * bi))
+            a, d, br, bi = a * scale, d * scale, br * scale, bi * scale
+            at, on = sub == t, sub == t + 1
+            here = at | on
+            e0r = jnp.where(at, -d, jnp.where(on, br, ar * d - (cr * br + ci * bi)))
+            e0i = jnp.where(at, 0.0, jnp.where(on, -bi, ai * d - (ci * br - cr * bi)))
+            e1r = jnp.where(at, br, jnp.where(on, -a, cr * a - (ar * br - ai * bi)))
+            e1i = jnp.where(at, bi, jnp.where(on, 0.0, ci * a - (ar * bi + ai * br)))
+            for key, (xr, xi) in cols.items():
+                x0r, x0i = across_rows(xr, t), across_rows(xi, t)
+                x1r, x1i = across_rows(xr, t + 1), across_rows(xi, t + 1)
+                lessr = (e0r * x0r - e0i * x0i) + (e1r * x1r - e1i * x1i)
+                lessi = (e0r * x0i + e0i * x0r) + (e1r * x1i + e1i * x1r)
+                cols[key] = (jnp.where(here, 0.0, xr) - lessr, jnp.where(here, 0.0, xi) - lessi)
+            if t < 6:
+                yield None
+        re[r], im[r] = cols["row"]
+        rows = [(across_rows(re[r], j), across_rows(im[r], j)) for j in range(8)]
+        for v in order[1:]:
+            lessr = [spread[v, j][0] * rows[j][0] - spread[v, j][1] * rows[j][1]
+                     for j in range(8)]
+            lessi = [spread[v, j][0] * rows[j][1] + spread[v, j][1] * rows[j][0]
+                     for j in range(8)]
+            re[v] = re[v] - summed(lessr)
+            im[v] = im[v] - summed(lessi)
+        yield jnp.concatenate(re, axis=0), jnp.concatenate(im, axis=0)
+
+
+def summed(terms):
+    while len(terms) > 1:
+        terms = [terms[i] + terms[i + 1] for i in range(0, len(terms), 2)]
+    return terms[0]
+
+
+def plain(a, b):
+    return jnp.dot(a, b, preferred_element_type=F32)
+
+
 def solve_kernel(group, gram_ref, rest_ref, gram_in, rest_in, x_ref, mat, head, tail):
     n = x_ref.shape[1]
     nb = NBLK
     side = lax.rem(lax.axis_index("col"), group)
-    mat[:, :, n:] = rest_ref[side] + rest_in[...]
-    ridge = 0.0
     diagonal = lax.broadcasted_iota(jnp.int32, (128, 128), 0) == lax.broadcasted_iota(
         jnp.int32, (128, 128), 1
     )
     gram = gram_ref[...] + gram_in[...]
+    ridge = 0.0
     for c in range(0, n, 128):
-        ridge = ridge + jnp.sum(jnp.where(diagonal, gram[0, c:c + 128, c:c + 128], 0.0))
-    ridge = ridge_share * ridge / n
+        ridge = ridge + jnp.where(diagonal, gram[0, c:c + 128, c:c + 128], 0.0)
+    ridge = ridge_share * jnp.sum(ridge) / n
     mat[:, :, 0:n] = gram
     for c in range(0, n, 128):
         here = slice(c, c + 128)
         mat[0, here, here] = gram[0, here, here] + jnp.where(diagonal, ridge, 0.0)
-    head[6 * nb:, :] = jnp.zeros_like(head[6 * nb:, :])
-    tail[6 * nb:, :] = jnp.zeros_like(tail[6 * nb:, :])
-    lane = lax.broadcasted_iota(jnp.int32, (nb, 128), 1)
-    sub = lax.broadcasted_iota(jnp.int32, (nb, 128), 0)
-    lane_all = lax.broadcasted_iota(jnp.int32, (n, 128), 1)
-
-    def turned(block, shift):
-        shift = shift % 128
-        return pltpu.roll(block, shift, 1) if shift else block
-
-    def inverse(block_re, block_im, back):
-        re0, im0 = turned(block_re, back), turned(block_im, back)
-        re1, im1 = turned(block_re, back + nb), turned(block_im, back + nb)
-        zero = jnp.zeros_like(re0)
-        m = jnp.where(lane < nb, re0, jnp.where(lane < 2 * nb, im1,
-                                                jnp.where(lane - 2 * nb == sub, 1.0, zero)))
-        w = jnp.where(lane < nb, -im0, jnp.where(lane < 2 * nb, re1,
-                                                 jnp.where(lane - 3 * nb == sub, 1.0, zero)))
-
-        def spread(block, k):
-            return jnp.broadcast_to(block[:, k:k + 1], (nb, 128))
-
-        for k in range(0, nb, 2):
-            p0, p1 = spread(m, k), spread(m, k + 1)
-            s0, s1 = spread(m, nb + k), spread(m, nb + k + 1)
-            a, d = p0[k:k + 1], p1[k + 1:k + 2]
-            br, bi = p1[k:k + 1], s1[k:k + 1]
-            scale = 1.0 / (a * d - (br * br + bi * bi))
-            m0, m1, w0, w1 = m[k:k + 1], m[k + 1:k + 2], w[k:k + 1], w[k + 1:k + 2]
-            row_m0 = (d * m0 - (br * m1 + bi * w1)) * scale
-            row_w0 = (d * w0 - (br * w1 - bi * m1)) * scale
-            row_m1 = (a * m1 - (br * m0 - bi * w0)) * scale
-            row_w1 = (a * w1 - (br * w0 + bi * m0)) * scale
-            new_m = m - ((p0 * row_m0 + s0 * row_w0) + (p1 * row_m1 + s1 * row_w1))
-            new_w = w - ((p0 * row_w0 - s0 * row_m0) + (p1 * row_w1 - s1 * row_m1))
-            m = jnp.where(sub == k, row_m0, jnp.where(sub == k + 1, row_m1, new_m))
-            w = jnp.where(sub == k, row_w0, jnp.where(sub == k + 1, row_w1, new_w))
-            yield m
-
-    def tripled(block):
-        high = block.astype(BF16)
-        return jnp.concatenate([high, (block - high.astype(F32)).astype(BF16)], axis=1)
-
-    def put(ref, w, re, im):
-        block = jnp.concatenate([jnp.concatenate([re, im], axis=1),
-                                 jnp.concatenate([-im, re], axis=1)], axis=0)
-        high, rest = split(block)
+    mat[:, :, n:] = rest_ref[side] + rest_in[...]
+    head[...] = jnp.zeros_like(head)
+    tail[...] = jnp.zeros_like(tail)
+
+    def pick(block):
+        return [block[8 * v:8 * v + 8] for v in range(nb // 8)]
+
+    def put(ref, at, w, re, im):
         where = slice(256 * w, 256 * w + 256)
-        ref[0:2 * nb, where] = high
-        ref[2 * nb:4 * nb, where] = rest
-        ref[4 * nb:6 * nb, where] = high
-
-    def plain(a, b):
-        return jnp.dot(a, b, preferred_element_type=F32)
-
-    for m in inverse(mat[0, 0:nb, 0:128], mat[1, 0:nb, 0:128], 0):
-        pass
+        for base, block in ((at, [re, im]), (128 + at, [-im, re])):
+            high, rest = split(jnp.concatenate(block, axis=1))
+            ref[0, base:base + nb, where] = high
+            ref[1, base:base + nb, where] = rest
+
+    def clear(ref, at):
+        for base in (at, 128 + at):
+            ref[:, base:base + nb, :] = jnp.zeros((2, nb, ref.shape[2]), BF16)
+
+    def doubled(re, im):
+        return jnp.concatenate(split(jnp.concatenate([re, im], axis=1)), axis=0)
+
+    def product(left, ref, w):
+        where = slice(256 * w, 256 * w + 256)
+        half = left.shape[0] // 2
+        both = plain(left, ref[0, :, where])
+        return both[0:half] + (both[half:] + plain(left[0:half], ref[1, :, where]))
+
+    for step in block_inverse(pick(mat[0, 0:nb, 0:128]), pick(mat[1, 0:nb, 0:128]), 0, nb):
+        found = step or None
     for j in range(n // nb):
         rows = slice(j * nb, (j + 1) * nb)
         after = slice((j + 1) * nb, (j + 2) * nb)
         q = (j * nb) // 128 * 128
-        back = -(j * nb)
+        at = j * nb - q
+        home = (at + nb) % 128
         windows = list(range((j + 1) * nb // 128, mat.shape[2] // 128))
-        window_re, window_im = mat[0, :, q:q + 128], mat[1, :, q:q + 128]
-        left = tripled(jnp.where(
-            lane_all < nb, turned(window_re, back),
-            jnp.where(lane_all < 2 * nb, turned(window_im, back + nb),
-                      jnp.where(lane_all < 3 * nb, turned(window_re, back + 2 * nb),
-                                turned(window_im, back + 3 * nb)))))
-        factor = tripled(jnp.where(lane < 2 * nb, turned(m, 64), m))
+        factor = doubled(*found)
+        left = doubled(mat[0, :, q:q + 128], mat[1, :, q:q + 128])
         held = {}
 
         def solve(w):
             here = slice(128 * w, 128 * w + 128)
-            put(head, w, mat[0, rows, here], mat[1, rows, here])
-            held[w] = plain(factor, head[:, 256 * w:256 * w + 256])
-            put(tail, w, held[w][:, 0:128], held[w][:, 128:])
-
-        def change(w, part):
+            put(head, home, w, mat[0, rows, here], mat[1, rows, here])
+            held[w] = product(factor, head, w)
+            put(tail, at, w, held[w][:, 0:128], held[w][:, 128:])
+
+        def change(w):
             here = slice(128 * w, 128 * w + 128)
-            some = slice(part * 128, (part + 1) * 128)
-            less = plain(left[some], tail[:, 256 * w:256 * w + 256])
-            mat[0, some, here] = mat[0, some, here] - less[:, 0:128]
-            mat[1, some, here] = mat[1, some, here] - less[:, 128:]
-
-        def place(w):
-            here = slice(128 * w, 128 * w + 128)
+            less = product(left, tail, w)
+            mat[0, :, here] = mat[0, :, here] - less[:, 0:128]
+            mat[1, :, here] = mat[1, :, here] - less[:, 128:]
             mat[0, rows, here] = held[w][:, 0:128]
             mat[1, rows, here] = held[w][:, 128:]
 
@@ -369,23 +400,26 @@
         pivots = iter(())
         if (j + 1) * nb < n:
             here = slice(128 * first, 128 * first + 128)
-            less = plain(left[after], tail[:, 256 * first:256 * first + 256])
-            pivots = inverse(mat[0, after, here] - less[:, 0:128],
-                             mat[1, after, here] - less[:, 128:], -((j + 1) * nb))
+            ahead = jnp.concatenate([left[after], left[n + (j + 1) * nb:n + (j + 2) * nb]], axis=0)
+            less = product(ahead, tail, first)
+            to = (j + 1) * nb % 128
+            pivots = block_inverse(pick(mat[0, after, here] - less[:, 0:128]),
+                                   pick(mat[1, after, here] - less[:, 128:]),
+                                   to, (to + nb) % 128)
         tasks = [functools.partial(solve, w) for w in windows[1:]]
-        for w in windows:
-            tasks += [functools.partial(change, w, part) for part in range(n // 128)]
-            tasks.append(functools.partial(place, w))
+        tasks += [functools.partial(change, w) for w in windows]
+        tasks.append(functools.partial(clear, head, home))
+        tasks.append(functools.partial(clear, tail, at))
         steps = nb // 2
         done = 0
         for i, task in enumerate(tasks):
             task()
             upto = (i + 1) * steps // len(tasks)
             for _ in range(upto - done):
-                m = next(pivots, m)
+                found = next(pivots, None) or found
             done = upto
-        for m in pivots:
-            pass
+        for step in pivots:
+            found = step or found
     x_ref[...] = mat[:, :, n:]
 
 
@@ -649,8 +683,8 @@
         out_specs=VMEM,
         scratch_shapes=[
             pltpu.VMEM((2, skeleton, skeleton + half), F32),
-            pltpu.VMEM((8 * NBLK, 2 * (skeleton + half)), BF16),
-            pltpu.VMEM((8 * NBLK, 2 * (skeleton + half)), BF16),
+            pltpu.VMEM((2, 256, 2 * (skeleton + half)), BF16),
+            pltpu.VMEM((2, 256, 2 * (skeleton + half)), BF16),
         ],
         compiler_params=params(),
     )(gram, right, gram_in, right_in)

time: 81.2 us -> 74.8 us (0.921)
  Pallas kernels: 74.7 us -> 68.3 us
    pallas_call x1, Pallas kernels: 16.6 us -> 10.3 us  [on_device(): pl.pallas_call(functools.partial(solve_kernel, group), out_shape=jax.Shap...]
  transfers between devices with their start and end apart: 1 -> 1, of which waited for: 0 -> 0; matrix products, arithmetic and copies ran while one was open for 0% -> 0% of each run, Pallas kernels for 15% -> 16%
where the time goes in v3:
time: 74.8 us; the launch traced here: 74.5 us
  Pallas kernels  68.3 us (91%)
  local copies, waits for them, and re-layouts  4.85 us (6%)
    pallas_call x1, Pallas kernels, on_device(): pl.pallas_call(functools.partial(reduce_kernel, box_total), out_shape=jax...  16 us
    pallas_call x1, Pallas kernels, on_device(): pl.pallas_call(functools.partial(near_kernel, box_total, col_count, group...  12.3 us
    pallas_call x1, Pallas kernels, on_device(): pl.pallas_call(functools.partial(solve_kernel, group), out_shape=jax.Shap...  10.3 us
    pallas_call x1, Pallas kernels, on_device(): pl.pallas_call(functools.partial(tile_kernel, box_total, entries, group,...  10.1 us
    pallas_call x1, Pallas kernels, on_device(): pl.pallas_call(functools.partial(exchange_kernel, box_total, col_count, g...  9.54 us
    pallas_call x1, Pallas kernels, on_device(): pl.pallas_call(functools.partial(far_kernel, box_total, col_count, group)...  7.8 us
    unnamed x16, local copies, waits for them, and re-layouts  4.85 us
    pallas_call x1, Pallas kernels, on_device(): pl.pallas_call(swap_kernel, out_shape=(jax.ShapeDtypeStruct(gram.shape, F...  2.37 us
  transfers between devices with their start and end apart: 1, of which 0 were waited for; matrix products, arithmetic and copies ran while one was open for 0% of the time, Pallas kernels for 16%

profile of v3, /device:TPU:0, one launch (start us, length us, event | category | flops | bytes accessed | tf_op | source)
XLA Modules:
  0.0 74.5 jit_solution(7386382939914052474)
XLA Ops:
  0.6 0.0 copy-start.1
  0.6 0.0 copy-start.6
  0.7 0.7 copy.8.points_ref
  1.4 0.0 copy-start.2
  1.4 0.7 copy-done.2
  2.1 0.0 copy-start.3
  2.1 0.7 copy-done.3
  2.7 0.0 copy-start.4
  2.8 0.7 copy-done.4
  3.4 9.5 %shard_map.77 = (f32[3,2,8,512]{3,2,1,0:T(8,128)S(1)}, f32[2,3,256]{2,1,0:T(4,128)S(1)}, f32[2,2,2,64]{3,2,1,0:T(2,128)S(1)}) custom-call(f32[2,3,512]{2,1,0:T(4,128)S(1)} %copy.8.points_ref, s32[2,512]{1,0:T(2,128)S(1)} %copy-done.2, f32[3,256]{1,0:T(4,128)S(1)} %copy-done.3, f32[2,2,64]{2,1,0:T(2,128)S(1)} %copy-done.4), custom_call_target="tpu_custom_call" | custom-call | tf_op jit(solution)/shard_map/pallas_call | solution.py:634
  13.0 0.0 copy-start
  13.0 0.7 copy-done
  13.7 0.0 copy-start.5
  13.7 0.7 copy-done.5
  14.3 10.1 %shard_map.78 = (f32[2,256,256]{2,1,0:T(8,128)S(1)}, f32[2,2,256,128]{3,2,1,0:T(8,128)S(1)}) custom-call(s32[2,8]{1,0:T(2,128)S(1)} %copy-done, s32[2,8]{1,0:T(2,128)S(1)} %copy-done.5, f32[3,2,8,512]{3,2,1,0:T(8,128)S(1)} %get-tuple-element.15.points_ref, f32[2,3,256]{2,1,0:T(4,128)S(1)} %get-tuple-element.16.proxy_ref), custom_call_target="tpu_custom_call" | custom-call | tf_op jit(solution)/shard_map/pallas_call | solution.py:650
  24.5 2.4 %shard_map.79 = (f32[2,256,256]{2,1,0:T(8,128)S(1)}, f32[2,256,128]{2,1,0:T(8,128)S(1)}) custom-call(f32[2,256,256]{2,1,0:T(8,128)S(1)} %get-tuple-element.17.gram_ref, f32[2,2,256,128]{3,2,1,0:T(8,128)S(1)} %get-tuple-element.18.rest_ref), custom_call_target="tpu_custom_call" | custom-call | tf_op jit(solution)/shard_map/pallas_call | solution.py:670
  26.9 10.3 %shard_map.80.x_ref.mine_ref = f32[2,256,128]{2,1,0:T(8,128)S(1)} custom-call(f32[2,256,256]{2,1,0:T(8,128)S(1)} %get-tuple-element.17.gram_ref, f32[2,2,256,128]{3,2,1,0:T(8,128)S(1)} %get-tuple-element.18.rest_ref, f32[2,256,256]{2,1,0:T(8,128)S(1)} %get-tuple-element.19.gram_in, f32[2,256,128]{2,1,0:T(8,128)S(1)} %get-tuple-element.20.rest_in), custom_call_target="tpu_custom_call" | custom-call | tf_op jit(solution)/shard_map/pallas_call | solution.py:679
  37.1 0.6 collective-permute-start
  37.7 0.0 copy-done.1
  37.7 0.0 copy-done.6
  37.7 12.3 %shard_map.81 = (f32[6,2,128,256]{3,2,1,0:T(8,128)S(1)}, bf16[8,256,512]{2,1,0:T(8,128)(2,1)S(1)}, bf16[8,256,512]{2,1,0:T(8,128)(2,1)S(1)}, f32[8,256,256]{2,1,0:T(8,128)S(1)}) custom-call(s32[2,8]{1,0:T(2,128)S(1)} %copy-done.1, s32[2,8]{1,0:T(2,128)S(1)} %copy-done.6, f32[3,2,8,512]{3,2,1,0:T(8,128)S(1)} %get-tuple-element.15.points_ref, ...), custom_call_target="tpu_custom_call" | custom-call | flops 4000000000 | bytes 8000000 | tf_op jit(solution)/shard_map/pallas_call | solution.py:694
  50.0 0.0 collective-permute-done.x_ref
  50.0 7.8 %shard_map.82 = (f32[6,2,128,256]{3,2,1,0:T(8,128)S(1)}, f32[2,2,64,256]{3,2,1,0:T(8,128)}) custom-call(s32[2,8]{1,0:T(2,128)S(1)} %copy-done.1, f32[6,2,128,256]{3,2,1,0:T(8,128)S(1)} %get-tuple-element.22.buf_ref, bf16[8,256,512]{2,1,0:T(8,128)(2,1)S(1)} %get-tuple-element.23.high_ref, bf16[8,256,512]{2,1,0:T(8,128)(2,1)S(1)} %get-tuple-element.24.low_ref, ...), custom_call_target="tpu_custom_call" | custom-call | tf_op jit(solution)/shard_map/pallas_call | solution.py:715
  57.8 16.0 %shard_map.83 = f32[2,2,64,256]{3,2,1,0:T(8,128)S(1)} custom-call(f32[6,2,2,64,256]{4,3,2,1,0:T(8,128)S(1)} %bitcast.2), custom_call_target="tpu_custom_call" | custom-call | tf_op jit(solution)/shard_map/pallas_call | solution.py:731
  73.8 0.7 copy.10
Async XLA Ops:
  0.6 37.1 %copy-start.1 = (s32[2,8]{1,0:T(2,128)S(1)}, s32[2,8]{1,0:T(2,128)}, u32[]{:S(2)}) copy-start(s32[2,8]{1,0:T(2,128)} %nb_ref.3) | copy-start | bytes 196
  0.6 37.1 %copy-start.6 = (s32[2,8]{1,0:T(2,128)S(1)}, s32[2,8]{1,0:T(2,128)}, u32[]{:S(2)}) copy-start(s32[2,8]{1,0:T(2,128)} %place_ref.1) | copy-start | bytes 196
  1.4 0.7 copy-start.2
  2.1 0.7 copy-start.3
  2.7 0.7 copy-start.4
  13.0 0.7 copy-start
  13.7 0.7 copy-start.5
  37.1 12.9 %collective-permute-start = (f32[2,256,128]{2,1,0:T(8,128)S(1)}, f32[2,256,128]{2,1,0:T(8,128)S(1)}, u32[]{:S(2)}, u32[]{:S(2)}) collective-permute-start(f32[2,256,128]{2,1,0:T(8,128)S(1)} %shard_map.80.x_ref.mine_ref), channel_id=1, source_target_pairs={{0,2},{1,3},{2,0},{3,1},{4,6},{5,7},{6,4},{7,5},{8,10},{9,11},{10,... | collective-permute-start | bytes 786440 | tf_op jit(solution)/shard_map/ppermute | solution.py:691

commit v4 on v3

--- a/solution.py
+++ b/solution.py
@@ -139,7 +139,7 @@
                     local):
     me = lax.axis_index("col")
     place = lax.axis_index("box")
-    box_count, _, count = points_ref.shape
+    _, box_count, count = points_ref.shape
     after = {"box": lax.rem(place + 1, box_total)}
     before = {"box": lax.rem(place + box_total - 1, box_total)}
     across = {"col": lax.rem(me + group, col_count)}
@@ -161,7 +161,8 @@
                   for c in range(group) for s in range(c, col_count, group)]
         row = jnp.concatenate([row[:, 0:skeleton]] + strips, axis=1)
         one_hot = (lax.broadcasted_iota(jnp.int32, (count, count), 0) == row).astype(F32)
-        whole = jnp.concatenate([points[box], jnp.zeros((5, count), F32)], axis=0)
+        whole = jnp.concatenate([points[axis, box:box + 1, :] for axis in range(3)]
+                                + [jnp.zeros((5, count), F32)], axis=0)
         rows = jnp.concatenate(list(three(whole)) + [jnp.zeros_like(whole)], axis=0)
         picked = jnp.dot(rows.astype(BF16), one_hot.astype(BF16), preferred_element_type=F32)
         points_out[1, box] = (picked[0:8] + picked[8:16]) + picked[16:24]
@@ -176,85 +177,77 @@
         copy.wait()
 
 
-def tile_kernel(box_total, entries, group, skeleton, nb_hbm, place_hbm, points_ref, proxy_ref,
-                gram_ref, rest_ref, nb_ref, place_ref, targets, sources, tiles, total, local):
+def tile_kernel(box_total, entries, group, skeleton, nb_ref, place_ref, points_ref, proxy_ref,
+                cross_ref, targets, sources, squares, tiles, total):
     count = points_ref.shape[3]
     box_count, _, share = proxy_ref.shape
     proxies = box_count * share
     me = lax.axis_index("col")
     box = me // group
     first = lax.rem(me, group) * entries
-    loads = [pltpu.make_async_copy(nb_hbm, nb_ref, local.at[0]),
-             pltpu.make_async_copy(place_hbm, place_ref, local.at[1])]
-    for copy in loads:
-        copy.start()
     sources[...] = source_rows(centred(points_ref[1, box]))
     for d in range(box_count):
         directions = jnp.concatenate([proxy_ref[d], jnp.zeros((5, share), F32)], axis=0)
         targets[:, d * share:(d + 1) * share] = target_rows((2.0 * proxy_radius) * directions)
-    for copy in loads:
-        copy.wait()
     for k in range(entries):
         slot = slot_of(nb_ref, box, first + k, box_count, box_total)
         here = shifted(points_ref[slot // box_count, slot % box_count], place_ref[box, first + k])
         targets[:, proxies + k * count:proxies + (k + 1) * count] = target_rows(here)
     block = tiles.shape[1] // 2
 
-    def evaluate(base, slot):
-        squares = dot_tn(targets[:, pl.ds(pl.multiple_of(base, block), block)], sources[...])
-        for i in range(block // ROWS):
-            inner = slice(i * ROWS, (i + 1) * ROWS)
-            lower = slice(block + i * ROWS, block + (i + 1) * ROWS)
-            for c in range(0, count, 256):
-                here = slice(c, c + 256)
-                there = slice(count + c, count + c + 256)
-                real, imag = kernel_values(squares[inner, here], COS_TILE)
-                real = real.astype(BF16)
-                imag = imag.astype(BF16)
-                tiles[slot, inner, here] = real
-                tiles[slot, inner, there] = imag
-                tiles[slot, lower, here] = imag
-                tiles[slot, lower, there] = -real
-
-    def gather(slot):
-        total[...] += dot_tn(tiles[slot, :, 0:skeleton], tiles[slot])
+    def measure(base, slot):
+        squares[slot] = dot_tn(targets[:, pl.ds(pl.multiple_of(base, block), block)],
+                               sources[...])
+
+    def evaluate(slot, i):
+        inner = slice(i * ROWS, (i + 1) * ROWS)
+        lower = slice(block + i * ROWS, block + (i + 1) * ROWS)
+        for c in range(0, count, 256):
+            here = slice(c, c + 256)
+            there = slice(count + c, count + c + 256)
+            real, imag = kernel_values(squares[slot, inner, here], COS_TILE)
+            real = real.astype(BF16)
+            imag = imag.astype(BF16)
+            tiles[slot, inner, here] = real
+            tiles[slot, inner, there] = imag
+            tiles[slot, lower, here] = imag
+            tiles[slot, lower, there] = -real
+
+    def gather(slot, left, c):
+        here = slice(c, c + 256)
+        total[:, here] += plain(left, tiles[slot, :, here])
+
+    def stage(ahead, now, before):
+        measure(*ahead)
+        steps = block // ROWS
+        pieces = 2 * count // 256
+        left = None if before is None else jnp.transpose(tiles[before, :, 0:skeleton])
+        for i in range(steps):
+            if left is not None and i % (steps // pieces) == 0:
+                gather(before, left, i // (steps // pieces) * 256)
+            evaluate(now, i)
 
     total[...] = jnp.zeros_like(total)
-    evaluate(0, 0)
-    for i in range(1, proxies // block):
-        gather((i + 1) % 2)
-        evaluate(i * block, i % 2)
-    parity = (proxies // block) % 2
+    blocks = proxies // block
+    measure(0, 0)
+    for i in range(blocks):
+        stage(((i + 1) * block, (i + 1) % 2), i % 2, (i + 1) % 2 if i else None)
     per = count // block
+    last = proxies + (entries * per - 1) * block
 
     @pl.loop(0, entries)
     def _(k):
         base = proxies + k * count
         for i in range(per):
-            gather((parity + i + 1) % 2)
-            evaluate(base + i * block, (parity + i) % 2)
-
-    gather((parity + per - 1) % 2)
-    half = (count - skeleton) // group
+            now = (blocks + i) % 2
+            stage((jnp.minimum(base + (i + 1) * block, last), 1 - now), now, 1 - now)
+
+    end = (blocks + per - 1) % 2
+    left = jnp.transpose(tiles[end, :, 0:skeleton])
+    for c in range(0, 2 * count, 256):
+        gather(end, left, c)
     for p in range(2):
-        gram_ref[p] = total[:, p * count:p * count + skeleton]
-        for c in range(group):
-            start = p * count + skeleton + c * half
-            rest_ref[c, p] = total[:, start:start + half]
-
-
-def swap_kernel(gram_ref, rest_ref, gram_out, rest_out, sends, recvs):
-    me = lax.axis_index("col")
-    side = lax.rem(me, 2)
-    peer = {"col": me + 1 - 2 * side}
-    meet([peer])()
-    copies = []
-    for i in range(2):
-        copies.append(send(gram_ref.at[i], gram_out.at[i], sends, recvs, i, peer))
-    for i in range(2):
-        copies.append(send(rest_ref.at[1 - side, i], rest_out.at[i], sends, recvs, 2 + i, peer))
-    for copy in copies:
-        copy.wait()
+        cross_ref[p] = total[:, p * count:(p + 1) * count]
 
 
 def lanes(block, k):
@@ -325,14 +318,15 @@
     return jnp.dot(a, b, preferred_element_type=F32)
 
 
-def solve_kernel(group, gram_ref, rest_ref, gram_in, rest_in, x_ref, mat, head, tail):
+def solve_kernel(group, cross_ref, cross_in, x_ref, mat, head, tail):
     n = x_ref.shape[1]
+    width = x_ref.shape[2]
     nb = NBLK
     side = lax.rem(lax.axis_index("col"), group)
     diagonal = lax.broadcasted_iota(jnp.int32, (128, 128), 0) == lax.broadcasted_iota(
         jnp.int32, (128, 128), 1
     )
-    gram = gram_ref[...] + gram_in[...]
+    gram = cross_ref[:, :, 0:n] + cross_in[:, :, 0:n]
     ridge = 0.0
     for c in range(0, n, 128):
         ridge = ridge + jnp.where(diagonal, gram[0, c:c + 128, c:c + 128], 0.0)
@@ -341,7 +335,8 @@
     for c in range(0, n, 128):
         here = slice(c, c + 128)
         mat[0, here, here] = gram[0, here, here] + jnp.where(diagonal, ridge, 0.0)
-    mat[:, :, n:] = rest_ref[side] + rest_in[...]
+    mine = pl.ds(pl.multiple_of(n + side * width, 128), width)
+    mat[:, :, n:] = cross_ref[:, :, mine] + cross_in[:, :, mine]
     head[...] = jnp.zeros_like(head)
     tail[...] = jnp.zeros_like(tail)
 
@@ -428,17 +423,10 @@
     return high, (x - high.astype(F32)).astype(BF16)
 
 
-def threefold(a, b, dims=((1,), (0,))):
-    def one(x, y):
-        return lax.dot_general(x, y, (dims, ((), ())), preferred_element_type=F32)
-
-    return one(a[0], b[0]) + (one(a[0], b[1]) + one(a[1], b[0]))
-
-
 def right_side(x):
     xr, xi = x[0], x[1]
-    return split(jnp.concatenate(
-        [jnp.concatenate([xr, xi], axis=1), jnp.concatenate([-xi, xr], axis=1)], axis=0))
+    return jnp.concatenate(split(jnp.concatenate(
+        [jnp.concatenate([xr, xi], axis=1), jnp.concatenate([-xi, xr], axis=1)], axis=0)), axis=1)
 
 
 def pivot_rows(pivot_ref, box):
@@ -447,21 +435,31 @@
             for p in range(2)]
 
 
-def fold(left, rest, right, pivots, rows, weighted, out_ref, slot):
+def quarters(product):
+    rows, cols = product.shape[0] // 2, product.shape[1] // 2
+    return ((product[:rows, :cols] + product[:rows, cols:])
+            + (product[rows:, :cols] + product[rows:, cols:]))
+
+
+def form(left, rest, right, blocks, slot):
+    blocks[slot] = rest - quarters(plain(left, right[...]))
+
+
+def fold(blocks, slot, rows, pivots, out_ref, to):
     qr, qi = pivots
     width = qr.shape[1]
-    held = weighted.shape[1] // 2
-    both = rest - threefold(left, right)
-    br, bi = both[:, 0:width], both[:, width:]
+    mine = blocks[slot, rows, :]
+    br, bi = mine[:, 0:width], mine[:, width:]
     wr = br * qr - bi * qi
     wi = br * qi + bi * qr
-    weighted[0] = jnp.concatenate([wr, -wi], axis=1)
-    weighted[1] = jnp.concatenate([wi, wr], axis=1)
-    upper = jnp.concatenate([weighted[0, rows, :], weighted[1, rows, :]], axis=0)
-    update = threefold(split(upper), split(both), ((1,), (1,)))
+    upper = jnp.concatenate([jnp.concatenate([wr, -wi], axis=1),
+                             jnp.concatenate([wi, wr], axis=1)], axis=0)
+    update = quarters(lax.dot_general(
+        jnp.concatenate(split(upper), axis=0), jnp.concatenate(split(blocks[slot]), axis=0),
+        (((1,), (1,)), ((), ())), preferred_element_type=F32))
     half = update.shape[0] // 2
-    out_ref[slot, 0] = out_ref[slot, 0] - update[0:half]
-    out_ref[slot, 1] = out_ref[slot, 1] - update[half:]
+    out_ref[to, 0] = out_ref[to, 0] - update[0:half]
+    out_ref[to, 1] = out_ref[to, 1] - update[half:]
 
 
 def row_half(col_count, group, n):
@@ -470,88 +468,110 @@
     return pl.ds(pl.multiple_of((me // group) * count, count), count)
 
 
-def spread(squares, keep):
-    for i in range(0, squares.shape[0], ROWS):
+def entry_squares(box_total, nb_ref, place_ref, points_ref, which, k, n, sources):
+    box_count = points_ref.shape[1]
+    place = slot_of(nb_ref, which, k, box_count, box_total)
+    here = shifted(points_ref[place // box_count, place % box_count], place_ref[which, k])
+    return dot_tn(target_rows(here[:, 0:n]), sources[...])
+
+
+def evaluate(squares, n, width, left_at, rest_at):
+    for i in range(0, n, ROWS):
         inner = slice(i, i + ROWS)
-        for c in range(0, squares.shape[1], 128):
-            real, imag = kernel_values(squares[inner, c:c + 128], COS)
-            keep(inner, c, real, imag)
+        under = slice(n + i, n + i + ROWS)
+        for c in range(0, n + width, 128):
+            values = kernel_values(squares[inner, c:c + 128], COS)
+            for p, value in enumerate(values):
+                if c < n:
+                    here = slice(p * n + c, p * n + c + 128)
+                    left_at[inner, here], left_at[under, here] = split(value)
+                else:
+                    start = p * width + c - n
+                    rest_at[inner, start:start + 128] = value
+
+
+def half_sources(points, side, group, n, width):
+    whole = source_rows(centred(points))
+    half = whole[:, n:n + width]
+    for c in range(1, group):
+        half = jnp.where(side == c, whole[:, n + c * width:n + (c + 1) * width], half)
+    return jnp.concatenate([whole[:, 0:n], half], axis=1)
+
+
+def kernel_kernel(box_total, group, nb_ref, place_ref, points_ref, left_ref, rest_ref, sources,
+                  squares):
+    entries, n, width = rest_ref.shape
+    width //= 2
+    me = lax.axis_index("col")
+    fed = 1 - me // group
+    sources[...] = half_sources(points_ref[1, fed], lax.rem(me, group), group, n, width)
+
+    def measure(k, slot):
+        squares[slot] = entry_squares(box_total, nb_ref, place_ref, points_ref, fed, k, n, sources)
+
+    measure(0, 0)
+
+    @pl.loop(0, entries // 2)
+    def _(pair):
+        for i in range(2):
+            k = 2 * pair + i
+            measure(jnp.minimum(k + 1, entries - 1), 1 - i)
+            evaluate(squares.at[i], n, width, left_ref.at[k], rest_ref.at[k])
 
 
 def near_kernel(box_total, col_count, group, nb_ref, place_ref, points_ref, x_ref, pivot_ref,
-                out_ref, high_ref, low_ref, rest_ref, sources, left, rest, weighted):
+                out_ref, sources, squares, left, rest, right, blocks):
     n = x_ref.shape[1]
     width = x_ref.shape[2]
-    box_count, _, count = points_ref.shape[1:]
+    box_count = points_ref.shape[1]
     entries = nb_ref.shape[1]
     me = lax.axis_index("col")
-    side = lax.rem(me, group)
     box = me // group
-    fed = 1 - box
-    out_ref[...] = jnp.zeros_like(out_ref)
-    for i, which in enumerate((box, fed)):
-        whole = source_rows(centred(points_ref[1, which]))
-        half = whole[:, n:n + width]
-        for c in range(1, group):
-            half = jnp.where(side == c, whole[:, n + c * width:n + (c + 1) * width], half)
-        sources[i, :, 0:n] = whole[:, 0:n]
-        sources[i, :, n:] = half
-    right = right_side(x_ref)
+    sources[...] = half_sources(points_ref[1, box], lax.rem(me, group), group, n, width)
     pivots = pivot_rows(pivot_ref, box)
     rows = row_half(col_count, group, n)
 
-    def evaluate(i, which, k, high, low, rest_at):
-        slot = slot_of(nb_ref, which, k, box_count, box_total)
-        here = shifted(points_ref[slot // box_count, slot % box_count], place_ref[which, k])
-        squares = dot_tn(target_rows(here[:, 0:n]), sources[i])
-
-        def keep(inner, c, real, imag):
-            for p, value in enumerate((real, imag)):
-                if c < n:
-                    top, bottom = split(value)
-                    high[inner, p * n + c:p * n + c + 128] = top
-                    low[inner, p * n + c:p * n + c + 128] = bottom
-                else:
-                    rest_at[inner, p * width + c - n:p * width + c - n + 128] = value
-
-        spread(squares, keep)
-
-    def own(k, slot):
-        evaluate(0, box, k, left.at[slot, 0], left.at[slot, 1], rest.at[slot])
-
-    def other(k):
-        evaluate(1, fed, k, high_ref.at[k], low_ref.at[k], rest_ref.at[k])
-
-    def use(k, slot):
-        to = slot_of(nb_ref, box, k, box_count, box_total)
-        fold((left[slot, 0], left[slot, 1]), rest[slot], right, pivots, rows, weighted, out_ref,
-             to)
-
-    own(0, 0)
+    def measure(k, slot):
+        squares[slot] = entry_squares(box_total, nb_ref, place_ref, points_ref, box, k, n, sources)
+
+    def finish(k, slot):
+        fold(blocks, slot, rows, pivots, out_ref,
+             slot_of(nb_ref, box, k, box_count, box_total))
+
+    measure(0, 0)
+    measure(1, 1)
+    right[...] = right_side(x_ref)
+    out_ref[...] = jnp.zeros_like(out_ref)
+    evaluate(squares.at[0], n, width, left.at[0], rest.at[0])
 
     @pl.loop(0, entries // 2)
     def _(pair):
-        k = 2 * pair
-        own(k + 1, 1)
-        other(k)
-        use(k, 0)
-        own(jnp.minimum(k + 2, entries - 1), 0)
-        other(k + 1)
-        use(k + 1, 1)
-
-
-def far_kernel(box_total, col_count, group, nb_ref, buf_ref, high_ref, low_ref, rest_ref, x_ref,
-               mine_ref, pivot_ref, out_ref, inter_ref, weighted):
+        for i in range(2):
+            k = 2 * pair + i
+            measure(jnp.minimum(k + 2, entries - 1), i)
+            form(left[i], rest[i], right, blocks, i)
+            evaluate(squares.at[1 - i], n, width, left.at[1 - i], rest.at[1 - i])
+            finish(k, i)
+
+
+def far_kernel(box_total, col_count, group, nb_ref, buf_ref, left_ref, rest_ref, x_ref,
+               mine_ref, pivot_ref, out_ref, inter_ref, right, blocks):
     n = x_ref.shape[1]
     entries, _, _ = rest_ref.shape
     me = lax.axis_index("col")
     box = me // group
     fed = 1 - box
     box_count = pivot_ref.shape[1]
-    out_ref[...] = buf_ref[...]
-    right = right_side(x_ref)
+    right[...] = right_side(x_ref)
     pivots = pivot_rows(pivot_ref, fed)
     rows = row_half(col_count, group, n)
+    form(left_ref[0], rest_ref[0], right, blocks, 0)
+    out_ref[...] = buf_ref[...]
+    for k in range(entries):
+        if k + 1 < entries:
+            form(left_ref[k + 1], rest_ref[k + 1], right, blocks, (k + 1) % 2)
+        fold(blocks, k % 2, rows, pivots, out_ref,
+             slot_of(nb_ref, fed, k, box_count, box_total))
     strip = inter_ref.shape[2]
     for p in range(2):
         for ref, where in ((mine_ref, box), (x_ref, fed)):
@@ -560,14 +580,6 @@
             for c in range(1, block.shape[0] // strip):
                 piece = jnp.where(box == c, block[c * strip:(c + 1) * strip], piece)
             inter_ref[where, p] = piece
-
-    @pl.loop(0, entries // 2)
-    def _(pair):
-        for i in range(2):
-            k = 2 * pair + i
-            to = slot_of(nb_ref, fed, k, box_count, box_total)
-            fold((high_ref[k], low_ref[k]), rest_ref[k], right, pivots, rows, weighted.at[i],
-                 out_ref, to)
 
 
 def reduce_kernel(box_total, buf_ref, out_ref, pair_in, line_out, line_in, side_out, side_in,
@@ -640,46 +652,54 @@
         ),
         in_specs=[HBM] * 4,
         out_specs=(VMEM,) * 3,
-        scratch_shapes=[pltpu.VMEM(box_points.shape, F32),
+        scratch_shapes=[pltpu.VMEM((3, box_count, point_count), F32),
                         pltpu.VMEM(point_order.shape, jnp.int32),
                         dma((4,)), dma((4,)), dma((4,))],
         compiler_params=params(collective_id=0, has_side_effects=True),
-    )(box_points, point_order, proxy_directions, pivot_inverse)
+        cost_estimate=pl.CostEstimate(flops=4 * 10**9, bytes_accessed=16 * 10**6,
+                                      transcendentals=0),
+    )(*(pltpu.with_memory_space_constraint(one, pltpu.HBM) for one in (
+        jnp.transpose(box_points, (1, 0, 2)), point_order, proxy_directions, pivot_inverse)))
 
     rows = box_count * share + entries * point_count
-    gram, right = pl.pallas_call(
+    cross = pl.pallas_call(
         functools.partial(tile_kernel, box_total, entries, group, skeleton),
-        out_shape=(
-            jax.ShapeDtypeStruct((2, skeleton, skeleton), F32),
-            jax.ShapeDtypeStruct((group, 2, skeleton, half), F32),
-        ),
-        in_specs=[HBM, HBM, VMEM, VMEM],
-        out_specs=(VMEM, VMEM),
+        out_shape=jax.ShapeDtypeStruct((2, skeleton, point_count), F32),
+        in_specs=[SMEM, SMEM, VMEM, VMEM],
+        out_specs=VMEM,
         scratch_shapes=[
-            pltpu.SMEM(neighbour_boxes.shape, jnp.int32),
-            pltpu.SMEM(neighbour_places.shape, jnp.int32),
             pltpu.VMEM((DEPTH, rows), BF16),
             pltpu.VMEM((DEPTH, point_count), BF16),
+            pltpu.VMEM((2, BLOCK, point_count), F32),
             pltpu.VMEM((2, 2 * BLOCK, 2 * point_count), BF16),
             pltpu.VMEM((skeleton, 2 * point_count), F32),
-            dma((2,)),
         ],
         compiler_params=params(),
     )(neighbour_boxes, neighbour_places, points, proxies)
-
-    gram_in, right_in = pl.pallas_call(
-        swap_kernel,
-        out_shape=(jax.ShapeDtypeStruct(gram.shape, F32),
-                   jax.ShapeDtypeStruct(right.shape[1:], F32)),
-        in_specs=[VMEM, VMEM],
+    pairs = [(i, i + 1 - 2 * (i % 2)) for i in range(col_count)]
+    cross_in = lax.ppermute(cross, "col", pairs)
+
+    cover = pl.CostEstimate(flops=8 * 10**9, bytes_accessed=16 * 10**6, transcendentals=0)
+    left, kept = pl.pallas_call(
+        functools.partial(kernel_kernel, box_total, group),
+        out_shape=(
+            jax.ShapeDtypeStruct((listed, 2 * skeleton, 2 * skeleton), BF16),
+            jax.ShapeDtypeStruct((listed, skeleton, 2 * half), F32),
+        ),
+        in_specs=[SMEM, SMEM, VMEM],
         out_specs=(VMEM, VMEM),
-        scratch_shapes=[dma((4,)), dma((4,))],
-        compiler_params=params(collective_id=2, has_side_effects=True),
-    )(gram, right)
+        scratch_shapes=[
+            pltpu.VMEM((DEPTH, skeleton + half), BF16),
+            pltpu.VMEM((2, skeleton, skeleton + half), F32),
+        ],
+        compiler_params=params(),
+        cost_estimate=cover,
+    )(neighbour_boxes, neighbour_places, points)
+
     solved = pl.pallas_call(
         functools.partial(solve_kernel, group),
         out_shape=jax.ShapeDtypeStruct((2, skeleton, half), F32),
-        in_specs=[VMEM] * 4,
+        in_specs=[VMEM] * 2,
         out_specs=VMEM,
         scratch_shapes=[
             pltpu.VMEM((2, skeleton, skeleton + half), F32),
@@ -687,29 +707,25 @@
             pltpu.VMEM((2, 256, 2 * (skeleton + half)), BF16),
         ],
         compiler_params=params(),
-    )(gram, right, gram_in, right_in)
+    )(cross, cross_in)
     arrived = lax.ppermute(solved, "col", ring(col_count, group))
 
     strips = skeleton // box_count
-    buffer, high, low, kept = pl.pallas_call(
+    buffer = pl.pallas_call(
         functools.partial(near_kernel, box_total, col_count, group),
-        out_shape=(
-            jax.ShapeDtypeStruct((3 * box_count, 2, strips, skeleton), F32),
-            jax.ShapeDtypeStruct((listed, skeleton, 2 * skeleton), BF16),
-            jax.ShapeDtypeStruct((listed, skeleton, 2 * skeleton), BF16),
-            jax.ShapeDtypeStruct((listed, skeleton, 2 * half), F32),
-        ),
+        out_shape=jax.ShapeDtypeStruct((3 * box_count, 2, strips, skeleton), F32),
         in_specs=[SMEM, SMEM, VMEM, VMEM, VMEM],
-        out_specs=(VMEM,) * 4,
+        out_specs=VMEM,
         scratch_shapes=[
-            pltpu.VMEM((box_count, DEPTH, skeleton + half), BF16),
-            pltpu.VMEM((2, 2, skeleton, 2 * skeleton), BF16),
+            pltpu.VMEM((DEPTH, skeleton + half), BF16),
+            pltpu.VMEM((2, skeleton, skeleton + half), F32),
+            pltpu.VMEM((2, 2 * skeleton, 2 * skeleton), BF16),
             pltpu.VMEM((2, skeleton, 2 * half), F32),
+            pltpu.VMEM((2 * skeleton, 4 * half), BF16),
             pltpu.VMEM((2, skeleton, 2 * half), F32),
         ],
         compiler_params=params(),
-        cost_estimate=pl.CostEstimate(flops=4 * 10**9, bytes_accessed=8 * 10**6,
-                                      transcendentals=0),
+        cost_estimate=cover,
     )(neighbour_boxes, neighbour_places, points, solved, pivots)
 
     buffer, inter = pl.pallas_call(
@@ -718,11 +734,14 @@
             jax.ShapeDtypeStruct(buffer.shape, F32),
             jax.ShapeDtypeStruct((box_count, 2, width, skeleton), F32),
         ),
-        in_specs=[SMEM] + [VMEM] * 7,
+        in_specs=[SMEM] + [VMEM] * 6,
         out_specs=(VMEM, VMEM),
-        scratch_shapes=[pltpu.VMEM((2, 2, skeleton, 2 * half), F32)],
+        scratch_shapes=[
+            pltpu.VMEM((2 * skeleton, 4 * half), BF16),
+            pltpu.VMEM((2, skeleton, 2 * half), F32),
+        ],
         compiler_params=params(),
-    )(neighbour_boxes, buffer, high, low, kept, arrived, solved, pivots)
+    )(neighbour_boxes, buffer, left, kept, arrived, solved, pivots)
     interpolation = jnp.swapaxes(inter, 2, 3)
 
     strip = skeleton // col_count

time: 74.8 us -> 72 us (0.963)
  local copies, waits for them, and re-layouts: 4.85 us -> 0.71 us
  Pallas kernels: 68.3 us -> 69.2 us
    unnamed x16 -> x5, local copies, waits for them, and re-layouts: 4.85 us -> 0.71 us
    pallas_call x1, Pallas kernels: 2.37 us -> 5.14 us  [on_device(): pl.pallas_call(functools.partial(kernel_kernel, box_total, group), out_sh...]
    pallas_call x1, Pallas kernels: 10.1 us -> 8.87 us  [on_device(): pl.pallas_call(functools.partial(tile_kernel, box_total, entries, group,...]
  transfers between devices with their start and end apart: 1 -> 2, of which waited for: 0 -> 0; matrix products, arithmetic and copies ran while one was open for 0% -> 0% of each run, Pallas kernels for 16% -> 24%
where the time goes in v4:
time: 72 us; the launch traced here: 71.8 us
  Pallas kernels  69.2 us (96%)
  starting transfers between devices  1.19 us (2%)
  between operations  0.74 us (1%)
    pallas_call x1, Pallas kernels, on_device(): pl.pallas_call(functools.partial(reduce_kernel, box_total), out_shape=jax...  15.5 us
    pallas_call x1, Pallas kernels, on_device(): pl.pallas_call(functools.partial(near_kernel, box_total, col_count, group...  12.1 us
    pallas_call x1, Pallas kernels, on_device(): pl.pallas_call(functools.partial(solve_kernel, group), out_shape=jax.Shap...  10.3 us
    pallas_call x1, Pallas kernels, on_device(): pl.pallas_call(functools.partial(exchange_kernel, box_total, col_count, g...  9.56 us
    pallas_call x1, Pallas kernels, on_device(): pl.pallas_call(functools.partial(tile_kernel, box_total, entries, group,...  8.87 us
    pallas_call x1, Pallas kernels, on_device(): pl.pallas_call(functools.partial(far_kernel, box_total, col_count, group)...  7.8 us
    pallas_call x1, Pallas kernels, on_device(): pl.pallas_call(functools.partial(kernel_kernel, box_total, group), out_sh...  5.14 us
  transfers between devices with their start and end apart: 2, of which 0 were waited for; matrix products, arithmetic and copies ran while one was open for 0% of the time, Pallas kernels for 24%

profile of v4, /device:TPU:0, one launch (start us, length us, event | category | flops | bytes accessed | tf_op | source)
XLA Modules:
  0.0 71.8 jit_solution(6078733503766040179)
XLA Ops:
  0.6 0.0 copy-start
  0.6 0.0 copy-start.1
  0.7 9.6 %shard_map.77 = (f32[3,2,8,512]{3,2,1,0:T(8,128)S(1)}, f32[2,3,256]{2,1,0:T(4,128)S(1)}, f32[2,2,2,64]{3,2,1,0:T(2,128)S(1)}) custom-call(f32[3,2,512]{2,1,0:T(2,128)} %bitcast.5, s32[2,512]{1,0:T(2,128)} %order_ref.1, f32[3,256]{1,0:T(4,128)} %proxy_ref.1, f32[2,2,64]{2,1,0:T(2,128)} %pivot_ref.1), custom_call_target="tpu_custom_call" | custom-call | flops 4000000000 | bytes 16000000 | tf_op jit(solution)/shard_map/pallas_call | solution.py:646
  10.2 0.0 copy-done
  10.2 0.0 copy-done.1
  10.2 8.9 %shard_map.78.cross_ref = f32[2,256,512]{2,1,0:T(8,128)S(1)} custom-call(s32[2,8]{1,0:T(2,128)S(1)} %copy-done, s32[2,8]{1,0:T(2,128)S(1)} %copy-done.1, f32[3,2,8,512]{3,2,1,0:T(8,128)S(1)} %get-tuple-element.9.points_ref, f32[2,3,256]{2,1,0:T(4,128)S(1)} %get-tuple-element.10.proxy_ref), custom_call_target="tpu_custom_call" | custom-call | tf_op jit(solution)/shard_map/pallas_call | solution.py:665
  19.1 0.1 collective-permute-start
  19.2 5.1 %shard_map.81 = (bf16[8,512,512]{2,1,0:T(8,128)(2,1)S(1)}, f32[8,256,256]{2,1,0:T(8,128)S(1)}) custom-call(s32[2,8]{1,0:T(2,128)S(1)} %copy-done, s32[2,8]{1,0:T(2,128)S(1)} %copy-done.1, f32[3,2,8,512]{3,2,1,0:T(8,128)S(1)} %get-tuple-element.9.points_ref), custom_call_target="tpu_custom_call" | custom-call | flops 8000000000 | bytes 16000000 | tf_op jit(solution)/shard_map/pallas_call | solution.py:683
  24.3 0.0 collective-permute-done.cross_in
  24.4 10.3 %shard_map.79.x_ref.mine_ref = f32[2,256,128]{2,1,0:T(8,128)S(1)} custom-call(f32[2,256,512]{2,1,0:T(8,128)S(1)} %shard_map.78.cross_ref, f32[2,256,512]{2,1,0:T(8,128)S(1)} %collective-permute-done.cross_in), custom_call_target="tpu_custom_call" | custom-call | tf_op jit(solution)/shard_map/pallas_call | solution.py:699
  34.6 1.1 %collective-permute-start.1 = (f32[2,256,128]{2,1,0:T(8,128)S(1)}, f32[2,256,128]{2,1,0:T(8,128)S(1)}, u32[]{:S(2)}, u32[]{:S(2)}) collective-permute-start(f32[2,256,128]{2,1,0:T(8,128)S(1)} %shard_map.79.x_ref.mine_ref), channel_id=1, source_target_pairs={{0,2},{1,3},{2,0},{3,1},{4,6},{5,7},{6,4},{7,5},{8,10},{9,11},{10,... | collective-permute-start | bytes 786440 | tf_op jit(solution)/shard_map/ppermute | solution.py:711
  35.7 12.1 %shard_map.80.buf_ref = f32[6,2,128,256]{3,2,1,0:T(8,128)S(1)} custom-call(s32[2,8]{1,0:T(2,128)S(1)} %copy-done, s32[2,8]{1,0:T(2,128)S(1)} %copy-done.1, f32[3,2,8,512]{3,2,1,0:T(8,128)S(1)} %get-tuple-element.9.points_ref, f32[2,256,128]{2,1,0:T(8,128)S(1)} %shard_map.79.x_ref.mine_ref, f32[2,2,2,64]{3,2,1,0:T(2,128)S(1)} %get-tuple-element.11.pivot_ref), custom_call_target="tpu_custom_call" | custom-call | flops 8000000000 | bytes 16000000 | tf_op jit(solution)/shard_map/pallas_call | solution.py:714
  47.8 0.0 collective-permute-done.1.x_ref
  47.8 7.8 %shard_map.82 = (f32[6,2,128,256]{3,2,1,0:T(8,128)S(1)}, f32[2,2,64,256]{3,2,1,0:T(8,128)}) custom-call(s32[2,8]{1,0:T(2,128)S(1)} %copy-done, f32[6,2,128,256]{3,2,1,0:T(8,128)S(1)} %shard_map.80.buf_ref, bf16[8,512,512]{2,1,0:T(8,128)(2,1)S(1)} %get-tuple-element.12.left_ref, f32[8,256,256]{2,1,0:T(8,128)S(1)} %get-tuple-element.13.rest_ref, ...), custom_call_target="tpu_custom_call" | custom-call | tf_op jit(solution)/shard_map/pallas_call | solution.py:731
  55.6 15.5 %shard_map.83 = f32[2,2,64,256]{3,2,1,0:T(8,128)S(1)} custom-call(f32[6,2,2,64,256]{4,3,2,1,0:T(8,128)S(1)} %bitcast.3), custom_call_target="tpu_custom_call" | custom-call | tf_op jit(solution)/shard_map/pallas_call | solution.py:750
  71.1 0.7 copy.9
Async XLA Ops:
  0.6 9.6 %copy-start = (s32[2,8]{1,0:T(2,128)S(1)}, s32[2,8]{1,0:T(2,128)}, u32[]{:S(2)}) copy-start(s32[2,8]{1,0:T(2,128)} %nb_ref.7) | copy-start | bytes 196
  0.6 9.6 %copy-start.1 = (s32[2,8]{1,0:T(2,128)S(1)}, s32[2,8]{1,0:T(2,128)}, u32[]{:S(2)}) copy-start(s32[2,8]{1,0:T(2,128)} %place_ref.5) | copy-start | bytes 196
  19.1 5.2 %collective-permute-start = (f32[2,256,512]{2,1,0:T(8,128)S(1)}, f32[2,256,512]{2,1,0:T(8,128)S(1)}, u32[]{:S(2)}, u32[]{:S(2)}) collective-permute-start(f32[2,256,512]{2,1,0:T(8,128)S(1)} %shard_map.78.cross_ref), channel_id=1, source_target_pairs={{0,1},{1,0},{2,3},{3,2},{4,5},{5,4},{6,7},{7,6},{8,9},{9,8},{10,11... | collective-permute-start | bytes 3145736 | tf_op jit(solution)/shard_map/ppermute | solution.py:680
  34.6 13.2 %collective-permute-start.1 = (f32[2,256,128]{2,1,0:T(8,128)S(1)}, f32[2,256,128]{2,1,0:T(8,128)S(1)}, u32[]{:S(2)}, u32[]{:S(2)}) collective-permute-start(f32[2,256,128]{2,1,0:T(8,128)S(1)} %shard_map.79.x_ref.mine_ref), channel_id=1, source_target_pairs={{0,2},{1,3},{2,0},{3,1},{4,6},{5,7},{6,4},{7,5},{8,10},{9,11},{10,... | collective-permute-start | bytes 786440 | tf_op jit(solution)/shard_map/ppermute | solution.py:711

commit v5 on v4

--- a/solution.py
+++ b/solution.py
@@ -15,10 +15,10 @@
 BLOCK = 256
 ROWS = 16
 DEPTH = 64
+PIECES = 2
 
 SIN = (4.44287959, -7.30781805, 3.59778873, -0.79123822)
-COS_TILE = (1.41420408, -6.97764206, 5.7152384, -1.72834866)
-COS = (1.4142135381698608, -6.978850841522217, 5.739460468292236, -1.883557915687561, 0.3106880187988281)
+COS = (1.41420408, -6.97764206, 5.7152384, -1.72834866)
 
 HBM = pl.BlockSpec(memory_space=pltpu.HBM)
 VMEM = pl.BlockSpec(memory_space=pltpu.VMEM)
@@ -39,7 +39,7 @@
     return total
 
 
-def kernel_values(square, cosine):
+def kernel_values(square):
     inverse = lax.rsqrt(square)
     turns = square * inverse
     part = turns - jnp.floor(turns + 0.5)
@@ -47,7 +47,7 @@
     amplitude = inverse * (1.0 / (2.0 * math.pi))
     sine = part * horner(SIN, z)
     scaled = amplitude * sine
-    return amplitude - scaled * sine, scaled * horner(cosine, z)
+    return amplitude - scaled * sine, scaled * horner(COS, z)
 
 
 def three(x):
@@ -205,7 +205,7 @@
         for c in range(0, count, 256):
             here = slice(c, c + 256)
             there = slice(count + c, count + c + 256)
-            real, imag = kernel_values(squares[slot, inner, here], COS_TILE)
+            real, imag = kernel_values(squares[slot, inner, here])
             real = real.astype(BF16)
             imag = imag.astype(BF16)
             tiles[slot, inner, here] = real
@@ -475,12 +475,12 @@
     return dot_tn(target_rows(here[:, 0:n]), sources[...])
 
 
-def evaluate(squares, n, width, left_at, rest_at):
-    for i in range(0, n, ROWS):
+def evaluate(squares, n, width, left_at, rest_at, part=0, parts=1):
+    for i in range(part * n // parts, (part + 1) * n // parts, ROWS):
         inner = slice(i, i + ROWS)
         under = slice(n + i, n + i + ROWS)
         for c in range(0, n + width, 128):
-            values = kernel_values(squares[inner, c:c + 128], COS)
+            values = kernel_values(squares[inner, c:c + 128])
             for p, value in enumerate(values):
                 if c < n:
                     here = slice(p * n + c, p * n + c + 128)
@@ -538,20 +538,25 @@
         fold(blocks, slot, rows, pivots, out_ref,
              slot_of(nb_ref, box, k, box_count, box_total))
 
+    def values(k, part):
+        if k < entries:
+            evaluate(squares.at[k % 3], n, width, left.at[k % 2], rest.at[k % 2], part, 2)
+
     measure(0, 0)
     measure(1, 1)
     right[...] = right_side(x_ref)
     out_ref[...] = jnp.zeros_like(out_ref)
-    evaluate(squares.at[0], n, width, left.at[0], rest.at[0])
-
-    @pl.loop(0, entries // 2)
-    def _(pair):
-        for i in range(2):
-            k = 2 * pair + i
-            measure(jnp.minimum(k + 2, entries - 1), i)
-            form(left[i], rest[i], right, blocks, i)
-            evaluate(squares.at[1 - i], n, width, left.at[1 - i], rest.at[1 - i])
-            finish(k, i)
+    for part in range(2):
+        values(0, part)
+    for k in range(entries + 1):
+        if k + 2 < entries:
+            measure(k + 2, (k + 2) % 3)
+        if k < entries:
+            form(left[k % 2], rest[k % 2], right, blocks, k)
+        values(k + 1, 0)
+        if k:
+            finish(k - 1, k - 1)
+        values(k + 1, 1)
 
 
 def far_kernel(box_total, col_count, group, nb_ref, buf_ref, left_ref, rest_ref, x_ref,
@@ -565,13 +570,13 @@
     right[...] = right_side(x_ref)
     pivots = pivot_rows(pivot_ref, fed)
     rows = row_half(col_count, group, n)
-    form(left_ref[0], rest_ref[0], right, blocks, 0)
     out_ref[...] = buf_ref[...]
-    for k in range(entries):
-        if k + 1 < entries:
-            form(left_ref[k + 1], rest_ref[k + 1], right, blocks, (k + 1) % 2)
-        fold(blocks, k % 2, rows, pivots, out_ref,
-             slot_of(nb_ref, fed, k, box_count, box_total))
+    for k in range(entries + 2):
+        if k < entries:
+            form(left_ref[k], rest_ref[k], right, blocks, k)
+        if k > 1:
+            fold(blocks, k - 2, rows, pivots, out_ref,
+                 slot_of(nb_ref, fed, k - 2, box_count, box_total))
     strip = inter_ref.shape[2]
     for p in range(2):
         for ref, where in ((mine_ref, box), (x_ref, fed)):
@@ -593,34 +598,43 @@
     source = {"box": lax.rem(place + box_total + 2 - 4 * odd, box_total)}
     twin = {"box": place + 1 - 2 * odd}
     meet([near, relay, source, twin])()
-    box_count = out_ref.shape[0]
+    box_count, _, strip, _ = out_ref.shape
     order = (2 * odd, 2 - 2 * odd, 1)
-    chunks = [(d, p) for d in range(box_count) for p in range(2)]
+    piece = strip // PIECES
+    chunks = [(d, p, pl.ds(i * piece, piece)) for d in range(box_count) for p in range(2)
+              for i in range(PIECES)]
+    wholes = [(d, p) for d in range(box_count) for p in range(2)]
     pairs = {}
-    for g, at in enumerate(order):
-        for i, (d, p) in enumerate(chunks):
-            pairs[g, i] = send(buf_ref.at[at * box_count + d, p, 1 - side], pair_in.at[g, d, p],
-                               sends, recvs, len(chunks) * g + i, near)
-    base = 3 * len(chunks)
+    base = 0
+    for g, parts in enumerate((chunks, wholes, wholes)):
+        for i, part in enumerate(parts):
+            d, p = part[:2]
+            source_at = (order[g] * box_count + d, p, 1 - side) + part[2:]
+            pairs[g, i] = send(buf_ref.at[source_at], pair_in.at[(g,) + part], sends, recvs,
+                               base + i, near)
+        base += len(parts)
     lines, sides = [], []
-    for i, (d, p) in enumerate(chunks):
+    for i, (d, p, some) in enumerate(chunks):
         pairs[0, i].wait()
-        line_out[d, p] = buf_ref[order[0] * box_count + d, p, side] + pair_in[0, d, p]
-        lines.append(send(line_out.at[d, p], line_in.at[d, p], sends, recvs, base + i, relay))
-    for i, (d, p) in enumerate(chunks):
+        line_out[d, p, some] = (buf_ref[order[0] * box_count + d, p, side, some]
+                                + pair_in[0, d, p, some])
+        lines.append(send(line_out.at[d, p, some], line_in.at[d, p, some], sends, recvs,
+                          base + i, relay))
+    base += len(chunks)
+    for i, (d, p) in enumerate(wholes):
         pairs[1, i].wait()
         held[d, p] = buf_ref[order[1] * box_count + d, p, side] + pair_in[1, d, p]
-    for i, (d, p) in enumerate(chunks):
+    for i, (d, p, some) in enumerate(chunks):
         lines[i].wait()
-        side_out[d, p] = held[d, p] + line_in[d, p]
-        sides.append(send(side_out.at[d, p], side_in.at[d, p], sends, recvs,
-                          base + len(chunks) + i, twin))
-    for i, (d, p) in enumerate(chunks):
+        side_out[d, p, some] = held[d, p, some] + line_in[d, p, some]
+        sides.append(send(side_out.at[d, p, some], side_in.at[d, p, some], sends, recvs,
+                          base + i, twin))
+    for i, (d, p) in enumerate(wholes):
         pairs[2, i].wait()
         held[d, p] = buf_ref[box_count + d, p, side] + pair_in[2, d, p]
-    for i, (d, p) in enumerate(chunks):
+    for i, (d, p, some) in enumerate(chunks):
         sides[i].wait()
-        out_ref[d, p] = held[d, p] + side_in[d, p]
+        out_ref[d, p, some] = held[d, p, some] + side_in[d, p, some]
 
 
 def ring(count, step):
@@ -718,11 +732,11 @@
         out_specs=VMEM,
         scratch_shapes=[
             pltpu.VMEM((DEPTH, skeleton + half), BF16),
-            pltpu.VMEM((2, skeleton, skeleton + half), F32),
+            pltpu.VMEM((3, skeleton, skeleton + half), F32),
             pltpu.VMEM((2, 2 * skeleton, 2 * skeleton), BF16),
             pltpu.VMEM((2, skeleton, 2 * half), F32),
             pltpu.VMEM((2 * skeleton, 4 * half), BF16),
-            pltpu.VMEM((2, skeleton, 2 * half), F32),
+            pltpu.VMEM((listed, skeleton, 2 * half), F32),
         ],
         compiler_params=params(),
         cost_estimate=cover,
@@ -738,7 +752,7 @@
         out_specs=(VMEM, VMEM),
         scratch_shapes=[
             pltpu.VMEM((2 * skeleton, 4 * half), BF16),
-            pltpu.VMEM((2, skeleton, 2 * half), F32),
+            pltpu.VMEM((listed, skeleton, 2 * half), F32),
         ],
         compiler_params=params(),
     )(neighbour_boxes, buffer, left, kept, arrived, solved, pivots)
@@ -746,7 +760,7 @@
 
     strip = skeleton // col_count
     block = (box_count, 2, strip, skeleton)
-    jobs = 5 * 2 * box_count
+    jobs = (2 + 3 * PIECES) * 2 * box_count
     skeleton_update = pl.pallas_call(
         functools.partial(reduce_kernel, box_total),
         out_shape=jax.ShapeDtypeStruct(block, F32),

time: 72 us -> 68.8 us (0.956)
  Pallas kernels: 69.2 us -> 65.9 us
    pallas_call x1, Pallas kernels: 12.1 us -> 9.29 us  [on_device(): pl.pallas_call(functools.partial(near_kernel, box_total, col_count, group...]
  transfers between devices with their start and end apart: 2 -> 2, of which waited for: 0 -> 0; matrix products, arithmetic and copies ran while one was open for 0% -> 0% of each run, Pallas kernels for 24% -> 21%
where the time goes in v5:
time: 68.8 us; the launch traced here: 68.6 us
  Pallas kernels  65.9 us (96%)
  starting transfers between devices  1.19 us (2%)
  between operations  0.74 us (1%)
  local copies, waits for them, and re-layouts  0.71 us (1%)
    pallas_call x1, Pallas kernels, on_device(): pl.pallas_call(functools.partial(reduce_kernel, box_total), out_shape=jax...  14.9 us
    pallas_call x1, Pallas kernels, on_device(): pl.pallas_call(functools.partial(solve_kernel, group), out_shape=jax.Shap...  10.2 us
    pallas_call x1, Pallas kernels, on_device(): pl.pallas_call(functools.partial(exchange_kernel, box_total, col_count, g...  9.56 us
    pallas_call x1, Pallas kernels, on_device(): pl.pallas_call(functools.partial(near_kernel, box_total, col_count, group...  9.29 us
    pallas_call x1, Pallas kernels, on_device(): pl.pallas_call(functools.partial(tile_kernel, box_total, entries, group,...  8.87 us
    pallas_call x1, Pallas kernels, on_device(): pl.pallas_call(functools.partial(far_kernel, box_total, col_count, group)...  7.91 us
    pallas_call x1, Pallas kernels, on_device(): pl.pallas_call(functools.partial(kernel_kernel, box_total, group), out_sh...  5.12 us
  transfers between devices with their start and end apart: 2, of which 0 were waited for; matrix products, arithmetic and copies ran while one was open for 0% of the time, Pallas kernels for 21%

profile of v5, /device:TPU:0, one launch (start us, length us, event | category | flops | bytes accessed | tf_op | source)
XLA Modules:
  0.0 68.6 jit_solution(7745545922235961870)
XLA Ops:
  0.6 0.0 copy-start
  0.6 0.0 copy-start.1
  0.7 9.6 %shard_map.77 = (f32[3,2,8,512]{3,2,1,0:T(8,128)S(1)}, f32[2,3,256]{2,1,0:T(4,128)S(1)}, f32[2,2,2,64]{3,2,1,0:T(2,128)S(1)}) custom-call(f32[3,2,512]{2,1,0:T(2,128)} %bitcast.5, s32[2,512]{1,0:T(2,128)} %order_ref.1, f32[3,256]{1,0:T(4,128)} %proxy_ref.1, f32[2,2,64]{2,1,0:T(2,128)} %pivot_ref.1), custom_call_target="tpu_custom_call" | custom-call | flops 4000000000 | bytes 16000000 | tf_op jit(solution)/shard_map/pallas_call | solution.py:660
  10.2 0.0 copy-done
  10.2 0.0 copy-done.1
  10.2 8.9 %shard_map.78.cross_ref = f32[2,256,512]{2,1,0:T(8,128)S(1)} custom-call(s32[2,8]{1,0:T(2,128)S(1)} %copy-done, s32[2,8]{1,0:T(2,128)S(1)} %copy-done.1, f32[3,2,8,512]{3,2,1,0:T(8,128)S(1)} %get-tuple-element.9.points_ref, f32[2,3,256]{2,1,0:T(4,128)S(1)} %get-tuple-element.10.proxy_ref), custom_call_target="tpu_custom_call" | custom-call | tf_op jit(solution)/shard_map/pallas_call | solution.py:679
  19.1 0.1 collective-permute-start
  19.2 5.1 %shard_map.81 = (bf16[8,512,512]{2,1,0:T(8,128)(2,1)S(1)}, f32[8,256,256]{2,1,0:T(8,128)S(1)}) custom-call(s32[2,8]{1,0:T(2,128)S(1)} %copy-done, s32[2,8]{1,0:T(2,128)S(1)} %copy-done.1, f32[3,2,8,512]{3,2,1,0:T(8,128)S(1)} %get-tuple-element.9.points_ref), custom_call_target="tpu_custom_call" | custom-call | flops 8000000000 | bytes 16000000 | tf_op jit(solution)/shard_map/pallas_call | solution.py:697
  24.3 0.0 collective-permute-done.cross_in
  24.3 10.2 %shard_map.79.x_ref.mine_ref = f32[2,256,128]{2,1,0:T(8,128)S(1)} custom-call(f32[2,256,512]{2,1,0:T(8,128)S(1)} %shard_map.78.cross_ref, f32[2,256,512]{2,1,0:T(8,128)S(1)} %collective-permute-done.cross_in), custom_call_target="tpu_custom_call" | custom-call | tf_op jit(solution)/shard_map/pallas_call | solution.py:713
  34.6 1.1 %collective-permute-start.1 = (f32[2,256,128]{2,1,0:T(8,128)S(1)}, f32[2,256,128]{2,1,0:T(8,128)S(1)}, u32[]{:S(2)}, u32[]{:S(2)}) collective-permute-start(f32[2,256,128]{2,1,0:T(8,128)S(1)} %shard_map.79.x_ref.mine_ref), channel_id=1, source_target_pairs={{0,2},{1,3},{2,0},{3,1},{4,6},{5,7},{6,4},{7,5},{8,10},{9,11},{10,... | collective-permute-start | bytes 786440 | tf_op jit(solution)/shard_map/ppermute | solution.py:725
  35.7 9.3 %shard_map.80.buf_ref = f32[6,2,128,256]{3,2,1,0:T(8,128)S(1)} custom-call(s32[2,8]{1,0:T(2,128)S(1)} %copy-done, s32[2,8]{1,0:T(2,128)S(1)} %copy-done.1, f32[3,2,8,512]{3,2,1,0:T(8,128)S(1)} %get-tuple-element.9.points_ref, f32[2,256,128]{2,1,0:T(8,128)S(1)} %shard_map.79.x_ref.mine_ref, f32[2,2,2,64]{3,2,1,0:T(2,128)S(1)} %get-tuple-element.11.pivot_ref), custom_call_target="tpu_custom_call" | custom-call | flops 8000000000 | bytes 16000000 | tf_op jit(solution)/shard_map/pallas_call | solution.py:728
  45.0 0.0 collective-permute-done.1.x_ref
  45.0 7.9 %shard_map.82 = (f32[6,2,128,256]{3,2,1,0:T(8,128)S(1)}, f32[2,2,64,256]{3,2,1,0:T(8,128)}) custom-call(s32[2,8]{1,0:T(2,128)S(1)} %copy-done, f32[6,2,128,256]{3,2,1,0:T(8,128)S(1)} %shard_map.80.buf_ref, bf16[8,512,512]{2,1,0:T(8,128)(2,1)S(1)} %get-tuple-element.12.left_ref, f32[8,256,256]{2,1,0:T(8,128)S(1)} %get-tuple-element.13.rest_ref, ...), custom_call_target="tpu_custom_call" | custom-call | tf_op jit(solution)/shard_map/pallas_call | solution.py:745
  52.9 14.9 %shard_map.83 = f32[2,2,64,256]{3,2,1,0:T(8,128)S(1)} custom-call(f32[6,2,2,64,256]{4,3,2,1,0:T(8,128)S(1)} %bitcast.3), custom_call_target="tpu_custom_call" | custom-call | tf_op jit(solution)/shard_map/pallas_call | solution.py:764
  67.9 0.7 %copy.9 = f32[2,2,64,256]{3,2,1,0:T(8,128)} copy(f32[2,2,64,256]{3,2,1,0:T(8,128)S(1)} %shard_map.83) | data formatting | bytes 524288
Async XLA Ops:
  0.6 9.6 %copy-start = (s32[2,8]{1,0:T(2,128)S(1)}, s32[2,8]{1,0:T(2,128)}, u32[]{:S(2)}) copy-start(s32[2,8]{1,0:T(2,128)} %nb_ref.7) | copy-start | bytes 196
  0.6 9.6 %copy-start.1 = (s32[2,8]{1,0:T(2,128)S(1)}, s32[2,8]{1,0:T(2,128)}, u32[]{:S(2)}) copy-start(s32[2,8]{1,0:T(2,128)} %place_ref.5) | copy-start | bytes 196
  19.1 5.2 %collective-permute-start = (f32[2,256,512]{2,1,0:T(8,128)S(1)}, f32[2,256,512]{2,1,0:T(8,128)S(1)}, u32[]{:S(2)}, u32[]{:S(2)}) collective-permute-start(f32[2,256,512]{2,1,0:T(8,128)S(1)} %shard_map.78.cross_ref), channel_id=1, source_target_pairs={{0,1},{1,0},{2,3},{3,2},{4,5},{5,4},{6,7},{7,6},{8,9},{9,8},{10,11... | collective-permute-start | bytes 3145736 | tf_op jit(solution)/shard_map/ppermute | solution.py:694
  34.6 10.4 %collective-permute-start.1 = (f32[2,256,128]{2,1,0:T(8,128)S(1)}, f32[2,256,128]{2,1,0:T(8,128)S(1)}, u32[]{:S(2)}, u32[]{:S(2)}) collective-permute-start(f32[2,256,128]{2,1,0:T(8,128)S(1)} %shard_map.79.x_ref.mine_ref), channel_id=1, source_target_pairs={{0,2},{1,3},{2,0},{3,1},{4,6},{5,7},{6,4},{7,5},{8,10},{9,11},{10,... | collective-permute-start | bytes 786440 | tf_op jit(solution)/shard_map/ppermute | solution.py:725

commit v6 on v5

--- a/solution.py
+++ b/solution.py
@@ -423,16 +423,16 @@
     return high, (x - high.astype(F32)).astype(BF16)
 
 
-def right_side(x):
-    xr, xi = x[0], x[1]
+def left_side(xr, xi):
     return jnp.concatenate(split(jnp.concatenate(
-        [jnp.concatenate([xr, xi], axis=1), jnp.concatenate([-xi, xr], axis=1)], axis=0)), axis=1)
-
-
-def pivot_rows(pivot_ref, box):
+        [jnp.concatenate([xr, -xi], axis=1), jnp.concatenate([xi, xr], axis=1)], axis=0)), axis=0)
+
+
+def pivot_columns(pivot_ref, box):
     pieces = range(pivot_ref.shape[0])
-    return [jnp.concatenate([pivot_ref[c, box, p:p + 1, :] for c in pieces], axis=1)
+    rows = [jnp.concatenate([pivot_ref[c, box, p:p + 1, :] for c in pieces], axis=1)
             for p in range(2)]
+    return [jnp.transpose(jnp.broadcast_to(row, (128, row.shape[1]))) for row in rows]
 
 
 def quarters(product):
@@ -441,53 +441,51 @@
             + (product[rows:, :cols] + product[rows:, cols:]))
 
 
-def form(left, rest, right, blocks, slot):
-    blocks[slot] = rest - quarters(plain(left, right[...]))
-
-
-def fold(blocks, slot, rows, pivots, out_ref, to):
+def form(turned, right, rest, blocks, pair):
+    half = turned.shape[0] // 2
+    both = plain(turned[...], right[0])
+    blocks[pair] = rest - (both[0:half] + (both[half:] + plain(turned[0:half, :], right[1])))
+
+
+def fold(blocks, pair, i, row, pivots, out_ref, to):
     qr, qi = pivots
-    width = qr.shape[1]
-    mine = blocks[slot, rows, :]
-    br, bi = mine[:, 0:width], mine[:, width:]
-    wr = br * qr - bi * qi
-    wi = br * qi + bi * qr
+    width = qr.shape[0]
+    n = blocks.shape[2] // 2
+    mine = blocks[pair, :, pl.ds(pl.multiple_of(i * n + row, 128), qr.shape[1])]
+    br, bi = mine[0:width], mine[width:]
+    wr = jnp.transpose(br * qr - bi * qi)
+    wi = jnp.transpose(br * qi + bi * qr)
     upper = jnp.concatenate([jnp.concatenate([wr, -wi], axis=1),
                              jnp.concatenate([wi, wr], axis=1)], axis=0)
-    update = quarters(lax.dot_general(
-        jnp.concatenate(split(upper), axis=0), jnp.concatenate(split(blocks[slot]), axis=0),
-        (((1,), (1,)), ((), ())), preferred_element_type=F32))
+    whole = jnp.concatenate(split(blocks[pair, :, i * n:(i + 1) * n]), axis=1)
+    update = quarters(plain(jnp.concatenate(split(upper), axis=0), whole))
     half = update.shape[0] // 2
     out_ref[to, 0] = out_ref[to, 0] - update[0:half]
     out_ref[to, 1] = out_ref[to, 1] - update[half:]
 
 
-def row_half(col_count, group, n):
-    count = n // (col_count // group)
-    me = lax.axis_index("col")
-    return pl.ds(pl.multiple_of((me // group) * count, count), count)
+def first_row(group, count):
+    return lax.axis_index("col") // group * count
 
 
 def entry_squares(box_total, nb_ref, place_ref, points_ref, which, k, n, sources):
     box_count = points_ref.shape[1]
     place = slot_of(nb_ref, which, k, box_count, box_total)
     here = shifted(points_ref[place // box_count, place % box_count], place_ref[which, k])
-    return dot_tn(target_rows(here[:, 0:n]), sources[...])
-
-
-def evaluate(squares, n, width, left_at, rest_at, part=0, parts=1):
-    for i in range(part * n // parts, (part + 1) * n // parts, ROWS):
-        inner = slice(i, i + ROWS)
-        under = slice(n + i, n + i + ROWS)
-        for c in range(0, n + width, 128):
-            values = kernel_values(squares[inner, c:c + 128])
-            for p, value in enumerate(values):
-                if c < n:
-                    here = slice(p * n + c, p * n + c + 128)
-                    left_at[inner, here], left_at[under, here] = split(value)
+    return dot_tn(sources[...], target_rows(here[:, 0:n]))
+
+
+def evaluate(squares, n, width, right_at, rest_at, i, part=0, parts=1):
+    rows = n + width
+    for r in range(part * rows // parts, (part + 1) * rows // parts, ROWS):
+        for c in range(0, n, 128):
+            here = slice(i * n + c, i * n + c + 128)
+            for p, value in enumerate(kernel_values(squares[r:r + ROWS, c:c + 128])):
+                if r < n:
+                    at = slice(p * n + r, p * n + r + ROWS)
+                    right_at[0, at, here], right_at[1, at, here] = split(value)
                 else:
-                    start = p * width + c - n
-                    rest_at[inner, start:start + 128] = value
+                    rest_at[p * width + r - n:p * width + r - n + ROWS, here] = value
 
 
 def half_sources(points, side, group, n, width):
@@ -498,10 +496,10 @@
     return jnp.concatenate([whole[:, 0:n], half], axis=1)
 
 
-def kernel_kernel(box_total, group, nb_ref, place_ref, points_ref, left_ref, rest_ref, sources,
+def kernel_kernel(box_total, group, nb_ref, place_ref, points_ref, right_ref, rest_ref, sources,
                   squares):
-    entries, n, width = rest_ref.shape
-    width //= 2
+    pairs, width, n = rest_ref.shape
+    width, n = width // 2, n // 2
     me = lax.axis_index("col")
     fed = 1 - me // group
     sources[...] = half_sources(points_ref[1, fed], lax.rem(me, group), group, n, width)
@@ -511,16 +509,15 @@
 
     measure(0, 0)
 
-    @pl.loop(0, entries // 2)
+    @pl.loop(0, pairs)
     def _(pair):
         for i in range(2):
-            k = 2 * pair + i
-            measure(jnp.minimum(k + 1, entries - 1), 1 - i)
-            evaluate(squares.at[i], n, width, left_ref.at[k], rest_ref.at[k])
-
-
-def near_kernel(box_total, col_count, group, nb_ref, place_ref, points_ref, x_ref, pivot_ref,
-                out_ref, sources, squares, left, rest, right, blocks):
+            measure(jnp.minimum(2 * pair + i + 1, 2 * pairs - 1), 1 - i)
+            evaluate(squares.at[i], n, width, right_ref.at[pair], rest_ref.at[pair], i)
+
+
+def near_kernel(box_total, group, nb_ref, place_ref, points_ref, x_ref, pivot_ref,
+                out_ref, sources, squares, right, rest, turned, blocks):
     n = x_ref.shape[1]
     width = x_ref.shape[2]
     box_count = points_ref.shape[1]
@@ -528,59 +525,63 @@
     me = lax.axis_index("col")
     box = me // group
     sources[...] = half_sources(points_ref[1, box], lax.rem(me, group), group, n, width)
-    pivots = pivot_rows(pivot_ref, box)
-    rows = row_half(col_count, group, n)
-
-    def measure(k, slot):
-        squares[slot] = entry_squares(box_total, nb_ref, place_ref, points_ref, box, k, n, sources)
-
-    def finish(k, slot):
-        fold(blocks, slot, rows, pivots, out_ref,
-             slot_of(nb_ref, box, k, box_count, box_total))
-
-    def values(k, part):
+
+    def measure(k):
         if k < entries:
-            evaluate(squares.at[k % 3], n, width, left.at[k % 2], rest.at[k % 2], part, 2)
-
-    measure(0, 0)
-    measure(1, 1)
-    right[...] = right_side(x_ref)
+            squares[k % 4] = entry_squares(box_total, nb_ref, place_ref, points_ref, box, k, n,
+                                           sources)
+
+    def values(k, part, parts):
+        if k < entries:
+            at = k // 2 % 2
+            evaluate(squares.at[k % 4], n, width, right.at[at], rest.at[at], k % 2, part, parts)
+
+    for k in range(4):
+        measure(k)
     out_ref[...] = jnp.zeros_like(out_ref)
-    for part in range(2):
-        values(0, part)
-    for k in range(entries + 1):
-        if k + 2 < entries:
-            measure(k + 2, (k + 2) % 3)
-        if k < entries:
-            form(left[k % 2], rest[k % 2], right, blocks, k)
-        values(k + 1, 0)
-        if k:
-            finish(k - 1, k - 1)
-        values(k + 1, 1)
-
-
-def far_kernel(box_total, col_count, group, nb_ref, buf_ref, left_ref, rest_ref, x_ref,
-               mine_ref, pivot_ref, out_ref, inter_ref, right, blocks):
-    n = x_ref.shape[1]
-    entries, _, _ = rest_ref.shape
+    values(0, 0, 1)
+    turned[...] = left_side(jnp.transpose(x_ref[0]), jnp.transpose(x_ref[1]))
+    pivots = pivot_columns(pivot_ref, box)
+    row = first_row(group, out_ref.shape[2])
+    values(1, 0, 1)
+    pairs = entries // 2
+    for pair in range(pairs + 1):
+        if pair < pairs:
+            form(turned, right.at[pair % 2], rest[pair % 2], blocks, pair)
+        for i in range(2):
+            k = 2 * pair + 2 + i
+            values(k, 0, 2)
+            if pair:
+                done = 2 * pair - 2 + i
+                fold(blocks, pair - 1, i, row, pivots, out_ref,
+                     slot_of(nb_ref, box, done, box_count, box_total))
+            values(k, 1, 2)
+            measure(k + 2)
+
+
+def far_kernel(box_total, group, nb_ref, buf_ref, right_ref, rest_ref, x_ref,
+               mine_ref, pivot_ref, out_ref, inter_ref, turned, blocks):
+    pairs = rest_ref.shape[0]
     me = lax.axis_index("col")
     box = me // group
     fed = 1 - box
     box_count = pivot_ref.shape[1]
-    right[...] = right_side(x_ref)
-    pivots = pivot_rows(pivot_ref, fed)
-    rows = row_half(col_count, group, n)
-    out_ref[...] = buf_ref[...]
-    for k in range(entries + 2):
-        if k < entries:
-            form(left_ref[k], rest_ref[k], right, blocks, k)
-        if k > 1:
-            fold(blocks, k - 2, rows, pivots, out_ref,
-                 slot_of(nb_ref, fed, k - 2, box_count, box_total))
     strip = inter_ref.shape[2]
+    theirs = [jnp.transpose(x_ref[p]) for p in range(2)]
+    turned[...] = left_side(*theirs)
+    pivots = pivot_columns(pivot_ref, fed)
+    row = first_row(group, out_ref.shape[2])
+    for pair in range(pairs + 1):
+        if pair < pairs:
+            form(turned, right_ref.at[pair], rest_ref[pair], blocks, pair)
+        if not pair:
+            out_ref[...] = buf_ref[...]
+        for i in range(2):
+            if pair:
+                fold(blocks, pair - 1, i, row, pivots, out_ref,
+                     slot_of(nb_ref, fed, 2 * pair - 2 + i, box_count, box_total))
     for p in range(2):
-        for ref, where in ((mine_ref, box), (x_ref, fed)):
-            block = jnp.transpose(ref[p])
+        for block, where in ((jnp.transpose(mine_ref[p]), box), (theirs[p], fed)):
             piece = block[0:strip]
             for c in range(1, block.shape[0] // strip):
                 piece = jnp.where(box == c, block[c * strip:(c + 1) * strip], piece)
@@ -694,17 +695,17 @@
     cross_in = lax.ppermute(cross, "col", pairs)
 
     cover = pl.CostEstimate(flops=8 * 10**9, bytes_accessed=16 * 10**6, transcendentals=0)
-    left, kept = pl.pallas_call(
+    right, kept = pl.pallas_call(
         functools.partial(kernel_kernel, box_total, group),
         out_shape=(
-            jax.ShapeDtypeStruct((listed, 2 * skeleton, 2 * skeleton), BF16),
-            jax.ShapeDtypeStruct((listed, skeleton, 2 * half), F32),
+            jax.ShapeDtypeStruct((listed // 2, 2, 2 * skeleton, 2 * skeleton), BF16),
+            jax.ShapeDtypeStruct((listed // 2, 2 * half, 2 * skeleton), F32),
         ),
         in_specs=[SMEM, SMEM, VMEM],
         out_specs=(VMEM, VMEM),
         scratch_shapes=[
             pltpu.VMEM((DEPTH, skeleton + half), BF16),
-            pltpu.VMEM((2, skeleton, skeleton + half), F32),
+            pltpu.VMEM((2, skeleton + half, skeleton), F32),
         ],
         compiler_params=params(),
         cost_estimate=cover,
@@ -726,24 +727,24 @@
 
     strips = skeleton // box_count
     buffer = pl.pallas_call(
-        functools.partial(near_kernel, box_total, col_count, group),
+        functools.partial(near_kernel, box_total, group),
         out_shape=jax.ShapeDtypeStruct((3 * box_count, 2, strips, skeleton), F32),
         in_specs=[SMEM, SMEM, VMEM, VMEM, VMEM],
         out_specs=VMEM,
         scratch_shapes=[
             pltpu.VMEM((DEPTH, skeleton + half), BF16),
-            pltpu.VMEM((3, skeleton, skeleton + half), F32),
-            pltpu.VMEM((2, 2 * skeleton, 2 * skeleton), BF16),
-            pltpu.VMEM((2, skeleton, 2 * half), F32),
-            pltpu.VMEM((2 * skeleton, 4 * half), BF16),
-            pltpu.VMEM((listed, skeleton, 2 * half), F32),
+            pltpu.VMEM((4, skeleton + half, skeleton), F32),
+            pltpu.VMEM((2, 2, 2 * skeleton, 2 * skeleton), BF16),
+            pltpu.VMEM((2, 2 * half, 2 * skeleton), F32),
+            pltpu.VMEM((4 * half, 2 * skeleton), BF16),
+            pltpu.VMEM((listed // 2, 2 * half, 2 * skeleton), F32),
         ],
         compiler_params=params(),
         cost_estimate=cover,
     )(neighbour_boxes, neighbour_places, points, solved, pivots)
 
     buffer, inter = pl.pallas_call(
-        functools.partial(far_kernel, box_total, col_count, group),
+        functools.partial(far_kernel, box_total, group),
         out_shape=(
             jax.ShapeDtypeStruct(buffer.shape, F32),
             jax.ShapeDtypeStruct((box_count, 2, width, skeleton), F32),
@@ -751,11 +752,11 @@
         in_specs=[SMEM] + [VMEM] * 6,
         out_specs=(VMEM, VMEM),
         scratch_shapes=[
-            pltpu.VMEM((2 * skeleton, 4 * half), BF16),
-            pltpu.VMEM((listed, skeleton, 2 * half), F32),
+            pltpu.VMEM((4 * half, 2 * skeleton), BF16),
+            pltpu.VMEM((listed // 2, 2 * half, 2 * skeleton), F32),
         ],
         compiler_params=params(),
-    )(neighbour_boxes, buffer, left, kept, arrived, solved, pivots)
+    )(neighbour_boxes, buffer, right, kept, arrived, solved, pivots)
     interpolation = jnp.swapaxes(inter, 2, 3)
 
     strip = skeleton // col_count

time: 68.8 us -> 63.2 us (0.919)
  Pallas kernels: 65.9 us -> 59.4 us
  waiting for transfers between devices: 0.01 us -> 1.01 us
    pallas_call x2, Pallas kernels: 17.2 us -> 11.3 us  [the longest x1 6.64 us: on_device(): pl.pallas_call(functools.partial(near_kernel, box_total, group), out_shap...]
    ppermute x1, waiting for transfers between devices: 0.01 us -> 1.01 us  [on_device(): arrived = lax.ppermute(solved, 'col', ring(col_count, group))]
  transfers between devices with their start and end apart: 2 -> 2, of which waited for: 0 -> 1; matrix products, arithmetic and copies ran while one was open for 0% -> 0% of each run, Pallas kernels for 21% -> 18%
where the time goes in v6:
time: 63.2 us; the launch traced here: 63 us
  Pallas kernels  59.4 us (94%)
  starting transfers between devices  1.17 us (2%)
  waiting for transfers between devices  1.01 us (2%)
  between operations  0.73 us (1%)
  local copies, waits for them, and re-layouts  0.71 us (1%)
    pallas_call x1, Pallas kernels, on_device(): pl.pallas_call(functools.partial(reduce_kernel, box_total), out_shape=jax...  14.5 us
    pallas_call x1, Pallas kernels, on_device(): pl.pallas_call(functools.partial(solve_kernel, group), out_shape=jax.Shap...  10.3 us
    pallas_call x1, Pallas kernels, on_device(): pl.pallas_call(functools.partial(exchange_kernel, box_total, col_count, g...  9.56 us
    pallas_call x1, Pallas kernels, on_device(): pl.pallas_call(functools.partial(tile_kernel, box_total, entries, group,...  8.87 us
    pallas_call x1, Pallas kernels, on_device(): pl.pallas_call(functools.partial(near_kernel, box_total, group), out_shap...  6.64 us
    pallas_call x1, Pallas kernels, on_device(): pl.pallas_call(functools.partial(kernel_kernel, box_total, group), out_sh...  4.92 us
    pallas_call x1, Pallas kernels, on_device(): pl.pallas_call(functools.partial(far_kernel, box_total, group), out_shape...  4.67 us
  transfers between devices with their start and end apart: 2, of which 1 were waited for; matrix products, arithmetic and copies ran while one was open for 0% of the time, Pallas kernels for 18%

profile of v6, /device:TPU:0, one launch (start us, length us, event | category | flops | bytes accessed | tf_op | source)
XLA Modules:
  0.0 63.0 jit_solution(3872490016192034143)
XLA Ops:
  0.6 0.0 copy-start
  0.6 0.0 copy-start.1
  0.7 9.6 %shard_map.77 = (f32[3,2,8,512]{3,2,1,0:T(8,128)S(1)}, f32[2,3,256]{2,1,0:T(4,128)S(1)}, f32[2,2,2,64]{3,2,1,0:T(2,128)S(1)}) custom-call(f32[3,2,512]{2,1,0:T(2,128)} %bitcast.5, s32[2,512]{1,0:T(2,128)} %order_ref.1, f32[3,256]{1,0:T(4,128)} %proxy_ref.1, f32[2,2,64]{2,1,0:T(2,128)} %pivot_ref.1), custom_call_target="tpu_custom_call" | custom-call | flops 4000000000 | bytes 16000000 | tf_op jit(solution)/shard_map/pallas_call | solution.py:661
  10.2 0.0 copy-done
  10.2 0.0 copy-done.1
  10.2 8.9 %shard_map.78.cross_ref = f32[2,256,512]{2,1,0:T(8,128)S(1)} custom-call(s32[2,8]{1,0:T(2,128)S(1)} %copy-done, s32[2,8]{1,0:T(2,128)S(1)} %copy-done.1, f32[3,2,8,512]{3,2,1,0:T(8,128)S(1)} %get-tuple-element.9.points_ref, f32[2,3,256]{2,1,0:T(4,128)S(1)} %get-tuple-element.10.proxy_ref), custom_call_target="tpu_custom_call" | custom-call | tf_op jit(solution)/shard_map/pallas_call | solution.py:680
  19.1 0.1 collective-permute-start
  19.2 4.9 %shard_map.81 = (bf16[4,2,512,512]{3,2,1,0:T(8,128)(2,1)S(1)}, f32[4,256,512]{2,1,0:T(8,128)S(1)}) custom-call(s32[2,8]{1,0:T(2,128)S(1)} %copy-done, s32[2,8]{1,0:T(2,128)S(1)} %copy-done.1, f32[3,2,8,512]{3,2,1,0:T(8,128)S(1)} %get-tuple-element.9.points_ref), custom_call_target="tpu_custom_call" | custom-call | flops 8000000000 | bytes 16000000 | tf_op jit(solution)/shard_map/pallas_call | solution.py:698
  24.1 0.0 collective-permute-done.cross_in
  24.1 10.3 %shard_map.79.x_ref.mine_ref = f32[2,256,128]{2,1,0:T(8,128)S(1)} custom-call(f32[2,256,512]{2,1,0:T(8,128)S(1)} %shard_map.78.cross_ref, f32[2,256,512]{2,1,0:T(8,128)S(1)} %collective-permute-done.cross_in), custom_call_target="tpu_custom_call" | custom-call | tf_op jit(solution)/shard_map/pallas_call | solution.py:714
  34.4 1.1 %collective-permute-start.1 = (f32[2,256,128]{2,1,0:T(8,128)S(1)}, f32[2,256,128]{2,1,0:T(8,128)S(1)}, u32[]{:S(2)}, u32[]{:S(2)}) collective-permute-start(f32[2,256,128]{2,1,0:T(8,128)S(1)} %shard_map.79.x_ref.mine_ref), channel_id=1, source_target_pairs={{0,2},{1,3},{2,0},{3,1},{4,6},{5,7},{6,4},{7,5},{8,10},{9,11},{10,... | collective-permute-start | bytes 786440 | tf_op jit(solution)/shard_map/ppermute | solution.py:726
  35.5 6.6 %shard_map.80.buf_ref = f32[6,2,128,256]{3,2,1,0:T(8,128)S(1)} custom-call(s32[2,8]{1,0:T(2,128)S(1)} %copy-done, s32[2,8]{1,0:T(2,128)S(1)} %copy-done.1, f32[3,2,8,512]{3,2,1,0:T(8,128)S(1)} %get-tuple-element.9.points_ref, f32[2,256,128]{2,1,0:T(8,128)S(1)} %shard_map.79.x_ref.mine_ref, f32[2,2,2,64]{3,2,1,0:T(2,128)S(1)} %get-tuple-element.11.pivot_ref), custom_call_target="tpu_custom_call" | custom-call | flops 8000000000 | bytes 16000000 | tf_op jit(solution)/shard_map/pallas_call | solution.py:729
  42.2 1.0 %collective-permute-done.1.x_ref = f32[2,256,128]{2,1,0:T(8,128)S(1)} collective-permute-done((f32[2,256,128]{2,1,0:T(8,128)S(1)}, f32[2,256,128]{2,1,0:T(8,128)S(1)}, u32[]{:S(2)}, u32[]{:S(2)}) %collective-permute-start.1) | collective-permute-done | bytes 262176 | tf_op jit(solution)/shard_map/ppermute | solution.py:726
  43.2 4.7 %shard_map.82 = (f32[6,2,128,256]{3,2,1,0:T(8,128)S(1)}, f32[2,2,64,256]{3,2,1,0:T(8,128)}) custom-call(s32[2,8]{1,0:T(2,128)S(1)} %copy-done, f32[6,2,128,256]{3,2,1,0:T(8,128)S(1)} %shard_map.80.buf_ref, bf16[4,2,512,512]{3,2,1,0:T(8,128)(2,1)S(1)} %get-tuple-element.12.right_ref, f32[4,256,512]{2,1,0:T(8,128)S(1)} %get-tuple-element.13.rest_ref, ...), custom_call_target="tpu_custom_call" | custom-call | tf_op jit(solution)/shard_map/pallas_call | solution.py:746
  47.8 14.5 %shard_map.83 = f32[2,2,64,256]{3,2,1,0:T(8,128)S(1)} custom-call(f32[6,2,2,64,256]{4,3,2,1,0:T(8,128)S(1)} %bitcast.3), custom_call_target="tpu_custom_call" | custom-call | tf_op jit(solution)/shard_map/pallas_call | solution.py:765
  62.3 0.7 %copy.9 = f32[2,2,64,256]{3,2,1,0:T(8,128)} copy(f32[2,2,64,256]{3,2,1,0:T(8,128)S(1)} %shard_map.83) | data formatting | bytes 524288
Async XLA Ops:
  0.6 9.6 %copy-start = (s32[2,8]{1,0:T(2,128)S(1)}, s32[2,8]{1,0:T(2,128)}, u32[]{:S(2)}) copy-start(s32[2,8]{1,0:T(2,128)} %nb_ref.7) | copy-start | bytes 196
  0.6 9.6 %copy-start.1 = (s32[2,8]{1,0:T(2,128)S(1)}, s32[2,8]{1,0:T(2,128)}, u32[]{:S(2)}) copy-start(s32[2,8]{1,0:T(2,128)} %place_ref.5) | copy-start | bytes 196
  19.1 5.0 %collective-permute-start = (f32[2,256,512]{2,1,0:T(8,128)S(1)}, f32[2,256,512]{2,1,0:T(8,128)S(1)}, u32[]{:S(2)}, u32[]{:S(2)}) collective-permute-start(f32[2,256,512]{2,1,0:T(8,128)S(1)} %shard_map.78.cross_ref), channel_id=1, source_target_pairs={{0,1},{1,0},{2,3},{3,2},{4,5},{5,4},{6,7},{7,6},{8,9},{9,8},{10,11... | collective-permute-start | bytes 3145736 | tf_op jit(solution)/shard_map/ppermute | solution.py:695
  34.4 8.8 %collective-permute-start.1 = (f32[2,256,128]{2,1,0:T(8,128)S(1)}, f32[2,256,128]{2,1,0:T(8,128)S(1)}, u32[]{:S(2)}, u32[]{:S(2)}) collective-permute-start(f32[2,256,128]{2,1,0:T(8,128)S(1)} %shard_map.79.x_ref.mine_ref), channel_id=1, source_target_pairs={{0,2},{1,3},{2,0},{3,1},{4,6},{5,7},{6,4},{7,5},{8,10},{9,11},{10,... | collective-permute-start | bytes 786440 | tf_op jit(solution)/shard_map/ppermute | solution.py:726

commit v7 on v6

--- a/solution.py
+++ b/solution.py
@@ -16,6 +16,7 @@
 ROWS = 16
 DEPTH = 64
 PIECES = 2
+EARLY = 2
 
 SIN = (4.44287959, -7.30781805, 3.59778873, -0.79123822)
 COS = (1.41420408, -6.97764206, 5.7152384, -1.72834866)
@@ -196,8 +197,7 @@
     block = tiles.shape[1] // 2
 
     def measure(base, slot):
-        squares[slot] = dot_tn(targets[:, pl.ds(pl.multiple_of(base, block), block)],
-                               sources[...])
+        squares[slot] = dot_tn(targets[:, base:base + block], sources[...])
 
     def evaluate(slot, i):
         inner = slice(i * ROWS, (i + 1) * ROWS)
@@ -232,17 +232,10 @@
     measure(0, 0)
     for i in range(blocks):
         stage(((i + 1) * block, (i + 1) % 2), i % 2, (i + 1) % 2 if i else None)
-    per = count // block
-    last = proxies + (entries * per - 1) * block
-
-    @pl.loop(0, entries)
-    def _(k):
-        base = proxies + k * count
-        for i in range(per):
-            now = (blocks + i) % 2
-            stage((jnp.minimum(base + (i + 1) * block, last), 1 - now), now, 1 - now)
-
-    end = (blocks + per - 1) % 2
+    last = blocks + entries * (count // block) - 1
+    for i in range(blocks, last + 1):
+        stage((min(i + 1, last) * block, (i + 1) % 2), i % 2, (i + 1) % 2)
+    end = last % 2
     left = jnp.transpose(tiles[end, :, 0:skeleton])
     for c in range(0, 2 * count, 256):
         gather(end, left, c)
@@ -517,24 +510,27 @@
 
 
 def near_kernel(box_total, group, nb_ref, place_ref, points_ref, x_ref, pivot_ref,
-                out_ref, sources, squares, right, rest, turned, blocks):
+                out_ref, right_ref, rest_ref, sources, squares, right, rest, turned, blocks):
     n = x_ref.shape[1]
     width = x_ref.shape[2]
     box_count = points_ref.shape[1]
     entries = nb_ref.shape[1]
     me = lax.axis_index("col")
     box = me // group
-    sources[...] = half_sources(points_ref[1, box], lax.rem(me, group), group, n, width)
+    for i, which in enumerate((box, 1 - box)):
+        sources[i] = half_sources(points_ref[1, which], lax.rem(me, group), group, n, width)
 
     def measure(k):
-        if k < entries:
-            squares[k % 4] = entry_squares(box_total, nb_ref, place_ref, points_ref, box, k, n,
-                                           sources)
+        if k < entries + 2:
+            other = k >= entries
+            squares[k % 4] = entry_squares(box_total, nb_ref, place_ref, points_ref,
+                                           1 - box if other else box, k - 2 if other else k, n,
+                                           sources.at[int(other)])
 
     def values(k, part, parts):
-        if k < entries:
-            at = k // 2 % 2
-            evaluate(squares.at[k % 4], n, width, right.at[at], rest.at[at], k % 2, part, parts)
+        at = k // 2 % 2
+        into = (right.at[at], rest.at[at]) if k < entries else (right_ref, rest_ref)
+        evaluate(squares.at[k % 4], n, width, *into, k % 2, part, parts)
 
     for k in range(4):
         measure(k)
@@ -550,18 +546,20 @@
             form(turned, right.at[pair % 2], rest[pair % 2], blocks, pair)
         for i in range(2):
             k = 2 * pair + 2 + i
-            values(k, 0, 2)
+            if k < entries + 2:
+                values(k, 0, 2)
             if pair:
                 done = 2 * pair - 2 + i
                 fold(blocks, pair - 1, i, row, pivots, out_ref,
                      slot_of(nb_ref, box, done, box_count, box_total))
-            values(k, 1, 2)
+            if k < entries + 2:
+                values(k, 1, 2)
             measure(k + 2)
 
 
-def far_kernel(box_total, group, nb_ref, buf_ref, right_ref, rest_ref, x_ref,
-               mine_ref, pivot_ref, out_ref, inter_ref, turned, blocks):
-    pairs = rest_ref.shape[0]
+def far_kernel(box_total, group, nb_ref, buf_ref, right_ref, rest_ref, right_last, rest_last,
+               x_ref, mine_ref, pivot_ref, out_ref, inter_ref, turned, blocks):
+    pairs = rest_ref.shape[0] + 1
     me = lax.axis_index("col")
     box = me // group
     fed = 1 - box
@@ -572,8 +570,10 @@
     pivots = pivot_columns(pivot_ref, fed)
     row = first_row(group, out_ref.shape[2])
     for pair in range(pairs + 1):
-        if pair < pairs:
+        if pair < pairs - 1:
             form(turned, right_ref.at[pair], rest_ref[pair], blocks, pair)
+        elif pair < pairs:
+            form(turned, right_last, rest_last[...], blocks, pair)
         if not pair:
             out_ref[...] = buf_ref[...]
         for i in range(2):
@@ -589,7 +589,7 @@
 
 
 def reduce_kernel(box_total, buf_ref, out_ref, pair_in, line_out, line_in, side_out, side_in,
-                  held, sends, recvs):
+                  last_in, held, sends, recvs):
     me = lax.axis_index("col")
     place = lax.axis_index("box")
     side = lax.rem(me, 2)
@@ -604,38 +604,56 @@
     piece = strip // PIECES
     chunks = [(d, p, pl.ds(i * piece, piece)) for d in range(box_count) for p in range(2)
               for i in range(PIECES)]
-    wholes = [(d, p) for d in range(box_count) for p in range(2)]
-    pairs = {}
-    base = 0
-    for g, parts in enumerate((chunks, wholes, wholes)):
-        for i, part in enumerate(parts):
-            d, p = part[:2]
-            source_at = (order[g] * box_count + d, p, 1 - side) + part[2:]
-            pairs[g, i] = send(buf_ref.at[source_at], pair_in.at[(g,) + part], sends, recvs,
-                               base + i, near)
-        base += len(parts)
-    lines, sides = [], []
-    for i, (d, p, some) in enumerate(chunks):
-        pairs[0, i].wait()
-        line_out[d, p, some] = (buf_ref[order[0] * box_count + d, p, side, some]
-                                + pair_in[0, d, p, some])
-        lines.append(send(line_out.at[d, p, some], line_in.at[d, p, some], sends, recvs,
-                          base + i, relay))
-    base += len(chunks)
-    for i, (d, p) in enumerate(wholes):
-        pairs[1, i].wait()
-        held[d, p] = buf_ref[order[1] * box_count + d, p, side] + pair_in[1, d, p]
-    for i, (d, p, some) in enumerate(chunks):
-        lines[i].wait()
-        side_out[d, p, some] = held[d, p, some] + line_in[d, p, some]
-        sides.append(send(side_out.at[d, p, some], side_in.at[d, p, some], sends, recvs,
-                          base + i, twin))
-    for i, (d, p) in enumerate(wholes):
-        pairs[2, i].wait()
-        held[d, p] = buf_ref[box_count + d, p, side] + pair_in[2, d, p]
-    for i, (d, p, some) in enumerate(chunks):
-        sides[i].wait()
-        out_ref[d, p, some] = held[d, p, some] + side_in[d, p, some]
+    late, early = chunks[:-EARLY], chunks[-EARLY:]
+    count = iter(range(sends.shape[0]))
+
+    def pair(g, parts):
+        return [send(buf_ref.at[(order[g] * box_count + part[0], part[1], 1 - side) + part[2:]],
+                     pair_in.at[(g,) + part], sends, recvs, next(count), near) for part in parts]
+
+    def both(g, part):
+        return (buf_ref[(order[g] * box_count + part[0], part[1], side) + part[2:]]
+                + pair_in[(g,) + part])
+
+    def forward(source_ref, target_ref, part, peer):
+        return send(source_ref.at[part], target_ref.at[part], sends, recvs, next(count), peer)
+
+    line_pairs, line_early = pair(0, late), pair(0, early)
+    side_early, side_pairs = pair(1, early), pair(1, late)
+    own_pairs = pair(2, chunks)
+    lines, sides, turns, directs, onward = [], [], [], [], []
+    for part, copy in zip(late, line_pairs):
+        copy.wait()
+        line_out[part] = both(0, part)
+        lines.append(forward(line_out, line_in, part, relay))
+    for part, copy, other in zip(early, line_early, side_early):
+        copy.wait()
+        line_out[part] = both(0, part)
+        turns.append(forward(line_out, line_in, part, twin))
+        other.wait()
+        side_out[part] = both(1, part)
+        directs.append(forward(side_out, side_in, part, twin))
+    for part, copy in zip(late, side_pairs):
+        copy.wait()
+        held[part] = both(1, part)
+    for i, (part, copy) in enumerate(zip(late, lines)):
+        copy.wait()
+        side_out[part] = held[part] + line_in[part]
+        sides.append(forward(side_out, side_in, part, twin))
+        if i == 1:
+            for some, turn in zip(early, turns):
+                turn.wait()
+                onward.append(forward(line_in, last_in, some, source))
+    for part, copy in zip(chunks, own_pairs):
+        copy.wait()
+        held[part] = both(2, part)
+    for part, direct, copy in zip(early, directs, onward):
+        direct.wait()
+        copy.wait()
+        out_ref[part] = (held[part] + side_in[part]) + last_in[part]
+    for part, copy in zip(late, sides):
+        copy.wait()
+        out_ref[part] = held[part] + side_in[part]
 
 
 def ring(count, step):
@@ -698,8 +716,8 @@
     right, kept = pl.pallas_call(
         functools.partial(kernel_kernel, box_total, group),
         out_shape=(
-            jax.ShapeDtypeStruct((listed // 2, 2, 2 * skeleton, 2 * skeleton), BF16),
-            jax.ShapeDtypeStruct((listed // 2, 2 * half, 2 * skeleton), F32),
+            jax.ShapeDtypeStruct((listed // 2 - 1, 2, 2 * skeleton, 2 * skeleton), BF16),
+            jax.ShapeDtypeStruct((listed // 2 - 1, 2 * half, 2 * skeleton), F32),
         ),
         in_specs=[SMEM, SMEM, VMEM],
         out_specs=(VMEM, VMEM),
@@ -726,13 +744,17 @@
     arrived = lax.ppermute(solved, "col", ring(col_count, group))
 
     strips = skeleton // box_count
-    buffer = pl.pallas_call(
+    buffer, right_last, kept_last = pl.pallas_call(
         functools.partial(near_kernel, box_total, group),
-        out_shape=jax.ShapeDtypeStruct((3 * box_count, 2, strips, skeleton), F32),
+        out_shape=(
+            jax.ShapeDtypeStruct((3 * box_count, 2, strips, skeleton), F32),
+            jax.ShapeDtypeStruct((2, 2 * skeleton, 2 * skeleton), BF16),
+            jax.ShapeDtypeStruct((2 * half, 2 * skeleton), F32),
+        ),
         in_specs=[SMEM, SMEM, VMEM, VMEM, VMEM],
-        out_specs=VMEM,
+        out_specs=(VMEM,) * 3,
         scratch_shapes=[
-            pltpu.VMEM((DEPTH, skeleton + half), BF16),
+            pltpu.VMEM((box_count, DEPTH, skeleton + half), BF16),
             pltpu.VMEM((4, skeleton + half, skeleton), F32),
             pltpu.VMEM((2, 2, 2 * skeleton, 2 * skeleton), BF16),
             pltpu.VMEM((2, 2 * half, 2 * skeleton), F32),
@@ -749,19 +771,19 @@
             jax.ShapeDtypeStruct(buffer.shape, F32),
             jax.ShapeDtypeStruct((box_count, 2, width, skeleton), F32),
         ),
-        in_specs=[SMEM] + [VMEM] * 6,
+        in_specs=[SMEM] + [VMEM] * 8,
         out_specs=(VMEM, VMEM),
         scratch_shapes=[
             pltpu.VMEM((4 * half, 2 * skeleton), BF16),
             pltpu.VMEM((listed // 2, 2 * half, 2 * skeleton), F32),
         ],
         compiler_params=params(),
-    )(neighbour_boxes, buffer, right, kept, arrived, solved, pivots)
+    )(neighbour_boxes, buffer, right, kept, right_last, kept_last, arrived, solved, pivots)
     interpolation = jnp.swapaxes(inter, 2, 3)
 
     strip = skeleton // col_count
     block = (box_count, 2, strip, skeleton)
-    jobs = (2 + 3 * PIECES) * 2 * box_count
+    jobs = 5 * PIECES * 2 * box_count + EARLY
     skeleton_update = pl.pallas_call(
         functools.partial(reduce_kernel, box_total),
         out_shape=jax.ShapeDtypeStruct(block, F32),
@@ -769,6 +791,7 @@
         out_specs=VMEM,
         scratch_shapes=[
             pltpu.VMEM((3,) + block, F32),
+            pltpu.VMEM(block, F32),
             pltpu.VMEM(block, F32),
             pltpu.VMEM(block, F32),
             pltpu.VMEM(block, F32),

time: 63.2 us -> 59.6 us (0.943)
  Pallas kernels: 59.4 us -> 56.2 us
    pallas_call x1, Pallas kernels: 8.87 us -> 6.5 us  [on_device(): pl.pallas_call(functools.partial(tile_kernel, box_total, entries, group,...]
    pallas_call x1, Pallas kernels: 4.92 us -> 3.94 us  [on_device(): pl.pallas_call(functools.partial(kernel_kernel, box_total, group), out_sh...]
  transfers between devices with their start and end apart: 2 -> 2, of which waited for: 1 -> 1; matrix products, arithmetic and copies ran while one was open for 0% -> 0% of each run, Pallas kernels for 18% -> 19%
where the time goes in v7:
time: 59.6 us; the launch traced here: 59.4 us
  Pallas kernels  56.2 us (94%)
  starting transfers between devices  1.21 us (2%)
  between operations  0.73 us (1%)
  local copies, waits for them, and re-layouts  0.71 us (1%)
    pallas_call x1, Pallas kernels, on_device(): pl.pallas_call(functools.partial(reduce_kernel, box_total), out_shape=jax...  13.9 us
    pallas_call x1, Pallas kernels, on_device(): pl.pallas_call(functools.partial(solve_kernel, group), out_shape=jax.Shap...  10.3 us
    pallas_call x1, Pallas kernels, on_device(): pl.pallas_call(functools.partial(exchange_kernel, box_total, col_count, g...  9.56 us
    pallas_call x1, Pallas kernels, on_device(): pl.pallas_call(functools.partial(near_kernel, box_total, group), out_shap...  7.07 us
    pallas_call x1, Pallas kernels, on_device(): pl.pallas_call(functools.partial(tile_kernel, box_total, entries, group,...  6.5 us
    pallas_call x1, Pallas kernels, on_device(): pl.pallas_call(functools.partial(far_kernel, box_total, group), out_shape...  4.94 us
    pallas_call x1, Pallas kernels, on_device(): pl.pallas_call(functools.partial(kernel_kernel, box_total, group), out_sh...  3.94 us
  transfers between devices with their start and end apart: 2, of which 1 were waited for; matrix products, arithmetic and copies ran while one was open for 0% of the time, Pallas kernels for 19%

profile of v7, /device:TPU:0, one launch (start us, length us, event | category | flops | bytes accessed | tf_op | source)
XLA Modules:
  0.0 59.4 jit_solution(12401304654508257023)
XLA Ops:
  0.6 0.0 copy-start
  0.6 0.0 copy-start.1
  0.7 9.6 %shard_map.77 = (f32[3,2,8,512]{3,2,1,0:T(8,128)S(1)}, f32[2,3,256]{2,1,0:T(4,128)S(1)}, f32[2,2,2,64]{3,2,1,0:T(2,128)S(1)}) custom-call(f32[3,2,512]{2,1,0:T(2,128)} %bitcast.5, s32[2,512]{1,0:T(2,128)} %order_ref.1, f32[3,256]{1,0:T(4,128)} %proxy_ref.1, f32[2,2,64]{2,1,0:T(2,128)} %pivot_ref.1), custom_call_target="tpu_custom_call" | custom-call | flops 4000000000 | bytes 16000000 | tf_op jit(solution)/shard_map/pallas_call | solution.py:679
  10.2 0.0 copy-done
  10.2 0.0 copy-done.1
  10.2 6.5 %shard_map.78.cross_ref = f32[2,256,512]{2,1,0:T(8,128)S(1)} custom-call(s32[2,8]{1,0:T(2,128)S(1)} %copy-done, s32[2,8]{1,0:T(2,128)S(1)} %copy-done.1, f32[3,2,8,512]{3,2,1,0:T(8,128)S(1)} %get-tuple-element.12.points_ref, f32[2,3,256]{2,1,0:T(4,128)S(1)} %get-tuple-element.13.proxy_ref), custom_call_target="tpu_custom_call" | custom-call | tf_op jit(solution)/shard_map/pallas_call | solution.py:698
  16.7 0.1 collective-permute-start
  16.8 3.9 %shard_map.81 = (bf16[3,2,512,512]{3,2,1,0:T(8,128)(2,1)S(1)}, f32[3,256,512]{2,1,0:T(8,128)S(1)}) custom-call(s32[2,8]{1,0:T(2,128)S(1)} %copy-done, s32[2,8]{1,0:T(2,128)S(1)} %copy-done.1, f32[3,2,8,512]{3,2,1,0:T(8,128)S(1)} %get-tuple-element.12.points_ref), custom_call_target="tpu_custom_call" | custom-call | flops 8000000000 | bytes 16000000 | tf_op jit(solution)/shard_map/pallas_call | solution.py:716
  20.8 0.0 collective-permute-done.cross_in
  20.8 10.3 %shard_map.79.x_ref.mine_ref = f32[2,256,128]{2,1,0:T(8,128)S(1)} custom-call(f32[2,256,512]{2,1,0:T(8,128)S(1)} %shard_map.78.cross_ref, f32[2,256,512]{2,1,0:T(8,128)S(1)} %collective-permute-done.cross_in), custom_call_target="tpu_custom_call" | custom-call | tf_op jit(solution)/shard_map/pallas_call | solution.py:732
  31.1 1.1 %collective-permute-start.1 = (f32[2,256,128]{2,1,0:T(8,128)S(1)}, f32[2,256,128]{2,1,0:T(8,128)S(1)}, u32[]{:S(2)}, u32[]{:S(2)}) collective-permute-start(f32[2,256,128]{2,1,0:T(8,128)S(1)} %shard_map.79.x_ref.mine_ref), channel_id=1, source_target_pairs={{0,2},{1,3},{2,0},{3,1},{4,6},{5,7},{6,4},{7,5},{8,10},{9,11},{10,... | collective-permute-start | bytes 786440 | tf_op jit(solution)/shard_map/ppermute | solution.py:744
  32.2 7.1 %shard_map.80 = (f32[6,2,128,256]{3,2,1,0:T(8,128)S(1)}, bf16[2,512,512]{2,1,0:T(8,128)(2,1)S(1)}, f32[256,512]{1,0:T(8,128)S(1)}) custom-call(s32[2,8]{1,0:T(2,128)S(1)} %copy-done, s32[2,8]{1,0:T(2,128)S(1)} %copy-done.1, f32[3,2,8,512]{3,2,1,0:T(8,128)S(1)} %get-tuple-element.12.points_ref, f32[2,256,128]{2,1,0:T(8,128)S(1)} %shard_map.79.x_ref.mine_ref, ...), custom_call_target="tpu_custom_call" | custom-call | flops 8000000000 | bytes 16000000 | tf_op jit(solution)/shard_map/pallas_call | solution.py:747
  39.3 0.6 collective-permute-done.1.x_ref
  39.8 4.9 %shard_map.82 = (f32[6,2,128,256]{3,2,1,0:T(8,128)S(1)}, f32[2,2,64,256]{3,2,1,0:T(8,128)}) custom-call(s32[2,8]{1,0:T(2,128)S(1)} %copy-done, f32[6,2,128,256]{3,2,1,0:T(8,128)S(1)} %get-tuple-element.15.buf_ref, bf16[3,2,512,512]{3,2,1,0:T(8,128)(2,1)S(1)} %get-tuple-element.16.right_ref, f32[3,256,512]{2,1,0:T(8,128)S(1)} %get-tuple-element.17.rest_ref, ...), custom_call_target="tpu_custom_call" | custom-call | tf_op jit(solution)/shard_map/pallas_call | solution.py:768
  44.8 13.9 %shard_map.83 = f32[2,2,64,256]{3,2,1,0:T(8,128)S(1)} custom-call(f32[6,2,2,64,256]{4,3,2,1,0:T(8,128)S(1)} %bitcast.3), custom_call_target="tpu_custom_call" | custom-call | tf_op jit(solution)/shard_map/pallas_call | solution.py:787
  58.7 0.7 %copy.9 = f32[2,2,64,256]{3,2,1,0:T(8,128)} copy(f32[2,2,64,256]{3,2,1,0:T(8,128)S(1)} %shard_map.83) | data formatting | bytes 524288
Async XLA Ops:
  0.6 9.6 %copy-start = (s32[2,8]{1,0:T(2,128)S(1)}, s32[2,8]{1,0:T(2,128)}, u32[]{:S(2)}) copy-start(s32[2,8]{1,0:T(2,128)} %nb_ref.7) | copy-start | bytes 196
  0.6 9.6 %copy-start.1 = (s32[2,8]{1,0:T(2,128)S(1)}, s32[2,8]{1,0:T(2,128)}, u32[]{:S(2)}) copy-start(s32[2,8]{1,0:T(2,128)} %place_ref.5) | copy-start | bytes 196
  16.7 4.0 %collective-permute-start = (f32[2,256,512]{2,1,0:T(8,128)S(1)}, f32[2,256,512]{2,1,0:T(8,128)S(1)}, u32[]{:S(2)}, u32[]{:S(2)}) collective-permute-start(f32[2,256,512]{2,1,0:T(8,128)S(1)} %shard_map.78.cross_ref), channel_id=1, source_target_pairs={{0,1},{1,0},{2,3},{3,2},{4,5},{5,4},{6,7},{7,6},{8,9},{9,8},{10,11... | collective-permute-start | bytes 3145736 | tf_op jit(solution)/shard_map/ppermute | solution.py:713
  31.1 8.8 %collective-permute-start.1 = (f32[2,256,128]{2,1,0:T(8,128)S(1)}, f32[2,256,128]{2,1,0:T(8,128)S(1)}, u32[]{:S(2)}, u32[]{:S(2)}) collective-permute-start(f32[2,256,128]{2,1,0:T(8,128)S(1)} %shard_map.79.x_ref.mine_ref), channel_id=1, source_target_pairs={{0,2},{1,3},{2,0},{3,1},{4,6},{5,7},{6,4},{7,5},{8,10},{9,11},{10,... | collective-permute-start | bytes 786440 | tf_op jit(solution)/shard_map/ppermute | solution.py:744

commit v8 on v7

--- a/solution.py
+++ b/solution.py
@@ -15,8 +15,8 @@
 BLOCK = 256
 ROWS = 16
 DEPTH = 64
-PIECES = 2
-EARLY = 2
+PIECES = 4
+EARLY = 6
 
 SIN = (4.44287959, -7.30781805, 3.59778873, -0.79123822)
 COS = (1.41420408, -6.97764206, 5.7152384, -1.72834866)
@@ -86,6 +86,10 @@
     return stacked([row_three(-2.0 * high, 1.0), row_three(-2.0 * mid, 1.0),
                     row_three(-2.0 * high, 1.0), row_three(-2.0 * low, n_high),
                     row_three(-2.0 * mid, n_mid), row_three(-2.0 * high, n_low)])
+
+
+def padded(points):
+    return jnp.concatenate([points, jnp.zeros_like(points)], axis=0)
 
 
 def three_rows(points):
@@ -166,7 +170,7 @@
                                 + [jnp.zeros((5, count), F32)], axis=0)
         rows = jnp.concatenate(list(three(whole)) + [jnp.zeros_like(whole)], axis=0)
         picked = jnp.dot(rows.astype(BF16), one_hot.astype(BF16), preferred_element_type=F32)
-        points_out[1, box] = (picked[0:8] + picked[8:16]) + picked[16:24]
+        points_out[1, box] = ((picked[0:8] + picked[8:16]) + picked[16:24])[0:4]
     arrived()
     jobs = [
         send(points_out.at[1], points_out.at[0], sends, recvs, 0, after),
@@ -186,13 +190,14 @@
     me = lax.axis_index("col")
     box = me // group
     first = lax.rem(me, group) * entries
-    sources[...] = source_rows(centred(points_ref[1, box]))
+    sources[...] = source_rows(centred(padded(points_ref[1, box])))
     for d in range(box_count):
         directions = jnp.concatenate([proxy_ref[d], jnp.zeros((5, share), F32)], axis=0)
         targets[:, d * share:(d + 1) * share] = target_rows((2.0 * proxy_radius) * directions)
     for k in range(entries):
         slot = slot_of(nb_ref, box, first + k, box_count, box_total)
-        here = shifted(points_ref[slot // box_count, slot % box_count], place_ref[box, first + k])
+        here = shifted(padded(points_ref[slot // box_count, slot % box_count]),
+                       place_ref[box, first + k])
         targets[:, proxies + k * count:proxies + (k + 1) * count] = target_rows(here)
     block = tiles.shape[1] // 2
 
@@ -312,8 +317,7 @@
 
 
 def solve_kernel(group, cross_ref, cross_in, x_ref, mat, head, tail):
-    n = x_ref.shape[1]
-    width = x_ref.shape[2]
+    width, n = x_ref.shape[1:]
     nb = NBLK
     side = lax.rem(lax.axis_index("col"), group)
     diagonal = lax.broadcasted_iota(jnp.int32, (128, 128), 0) == lax.broadcasted_iota(
@@ -408,7 +412,8 @@
             done = upto
         for step in pivots:
             found = step or found
-    x_ref[...] = mat[:, :, n:]
+    for p in range(2):
+        x_ref[p] = jnp.transpose(mat[p, :, n:])
 
 
 def split(x):
@@ -464,7 +469,8 @@
 def entry_squares(box_total, nb_ref, place_ref, points_ref, which, k, n, sources):
     box_count = points_ref.shape[1]
     place = slot_of(nb_ref, which, k, box_count, box_total)
-    here = shifted(points_ref[place // box_count, place % box_count], place_ref[which, k])
+    here = shifted(padded(points_ref[place // box_count, place % box_count]),
+                   place_ref[which, k])
     return dot_tn(sources[...], target_rows(here[:, 0:n]))
 
 
@@ -482,7 +488,7 @@
 
 
 def half_sources(points, side, group, n, width):
-    whole = source_rows(centred(points))
+    whole = source_rows(centred(padded(points)))
     half = whole[:, n:n + width]
     for c in range(1, group):
         half = jnp.where(side == c, whole[:, n + c * width:n + (c + 1) * width], half)
@@ -501,18 +507,15 @@
         squares[slot] = entry_squares(box_total, nb_ref, place_ref, points_ref, fed, k, n, sources)
 
     measure(0, 0)
-
-    @pl.loop(0, pairs)
-    def _(pair):
-        for i in range(2):
-            measure(jnp.minimum(2 * pair + i + 1, 2 * pairs - 1), 1 - i)
-            evaluate(squares.at[i], n, width, right_ref.at[pair], rest_ref.at[pair], i)
+    for k in range(2 * pairs):
+        if k + 1 < 2 * pairs:
+            measure(k + 1, (k + 1) % 2)
+        evaluate(squares.at[k % 2], n, width, right_ref.at[k // 2], rest_ref.at[k // 2], k % 2)
 
 
 def near_kernel(box_total, group, nb_ref, place_ref, points_ref, x_ref, pivot_ref,
                 out_ref, right_ref, rest_ref, sources, squares, right, rest, turned, blocks):
-    n = x_ref.shape[1]
-    width = x_ref.shape[2]
+    width, n = x_ref.shape[1:]
     box_count = points_ref.shape[1]
     entries = nb_ref.shape[1]
     me = lax.axis_index("col")
@@ -536,7 +539,7 @@
         measure(k)
     out_ref[...] = jnp.zeros_like(out_ref)
     values(0, 0, 1)
-    turned[...] = left_side(jnp.transpose(x_ref[0]), jnp.transpose(x_ref[1]))
+    turned[...] = left_side(x_ref[0], x_ref[1])
     pivots = pivot_columns(pivot_ref, box)
     row = first_row(group, out_ref.shape[2])
     values(1, 0, 1)
@@ -565,8 +568,7 @@
     fed = 1 - box
     box_count = pivot_ref.shape[1]
     strip = inter_ref.shape[2]
-    theirs = [jnp.transpose(x_ref[p]) for p in range(2)]
-    turned[...] = left_side(*theirs)
+    turned[...] = left_side(x_ref[0], x_ref[1])
     pivots = pivot_columns(pivot_ref, fed)
     row = first_row(group, out_ref.shape[2])
     for pair in range(pairs + 1):
@@ -581,11 +583,8 @@
                 fold(blocks, pair - 1, i, row, pivots, out_ref,
                      slot_of(nb_ref, fed, 2 * pair - 2 + i, box_count, box_total))
     for p in range(2):
-        for block, where in ((jnp.transpose(mine_ref[p]), box), (theirs[p], fed)):
-            piece = block[0:strip]
-            for c in range(1, block.shape[0] // strip):
-                piece = jnp.where(box == c, block[c * strip:(c + 1) * strip], piece)
-            inter_ref[where, p] = piece
+        for ref, where in ((mine_ref, box), (x_ref, fed)):
+            inter_ref[where, p] = ref[p, pl.ds(pl.multiple_of(box * strip, strip), strip), :]
 
 
 def reduce_kernel(box_total, buf_ref, out_ref, pair_in, line_out, line_in, side_out, side_in,
@@ -640,7 +639,7 @@
         copy.wait()
         side_out[part] = held[part] + line_in[part]
         sides.append(forward(side_out, side_in, part, twin))
-        if i == 1:
+        if i == 3:
             for some, turn in zip(early, turns):
                 turn.wait()
                 onward.append(forward(line_in, last_in, some, source))
@@ -679,7 +678,7 @@
     points, proxies, pivots = pl.pallas_call(
         functools.partial(exchange_kernel, box_total, col_count, group, skeleton),
         out_shape=(
-            jax.ShapeDtypeStruct((3, box_count, 8, point_count), F32),
+            jax.ShapeDtypeStruct((3, box_count, 4, point_count), F32),
             jax.ShapeDtypeStruct((box_count,) + proxy_directions.shape, F32),
             jax.ShapeDtypeStruct((box_count,) + pivot_inverse.shape, F32),
         ),
@@ -731,7 +730,7 @@
 
     solved = pl.pallas_call(
         functools.partial(solve_kernel, group),
-        out_shape=jax.ShapeDtypeStruct((2, skeleton, half), F32),
+        out_shape=jax.ShapeDtypeStruct((2, half, skeleton), F32),
         in_specs=[VMEM] * 2,
         out_specs=VMEM,
         scratch_shapes=[

time: 59.6 us -> 60.4 us (1.013)
  Pallas kernels: 56.2 us -> 56.9 us
    pallas_call x1, Pallas kernels: 13.9 us -> 15.2 us  [on_device(): pl.pallas_call(functools.partial(reduce_kernel, box_total), out_shape=jax...]
    pallas_call x1, Pallas kernels: 3.94 us -> 3.16 us  [on_device(): pl.pallas_call(functools.partial(kernel_kernel, box_total, group), out_sh...]
  transfers between devices with their start and end apart: 2 -> 2, of which waited for: 1 -> 1; matrix products, arithmetic and copies ran while one was open for 0% -> 0% of each run, Pallas kernels for 19% -> 17%
where the time goes in v8:
time: 60.4 us; the launch traced here: 60.2 us
  Pallas kernels  56.9 us (94%)
  starting transfers between devices  1.13 us (2%)
  waiting for transfers between devices  0.78 us (1%)
  between operations  0.72 us (1%)
  local copies, waits for them, and re-layouts  0.71 us (1%)
    pallas_call x1, Pallas kernels, on_device(): pl.pallas_call(functools.partial(reduce_kernel, box_total), out_shape=jax...  15.2 us
    pallas_call x1, Pallas kernels, on_device(): pl.pallas_call(functools.partial(solve_kernel, group), out_shape=jax.Shap...  10.5 us
    pallas_call x1, Pallas kernels, on_device(): pl.pallas_call(functools.partial(exchange_kernel, box_total, col_count, g...  9.47 us
    pallas_call x1, Pallas kernels, on_device(): pl.pallas_call(functools.partial(near_kernel, box_total, group), out_shap...  6.93 us
    pallas_call x1, Pallas kernels, on_device(): pl.pallas_call(functools.partial(tile_kernel, box_total, entries, group,...  6.47 us
    pallas_call x1, Pallas kernels, on_device(): pl.pallas_call(functools.partial(far_kernel, box_total, group), out_shape...  5.1 us
    pallas_call x1, Pallas kernels, on_device(): pl.pallas_call(functools.partial(kernel_kernel, box_total, group), out_sh...  3.16 us
  transfers between devices with their start and end apart: 2, of which 1 were waited for; matrix products, arithmetic and copies ran while one was open for 0% of the time, Pallas kernels for 17%

profile of v8, /device:TPU:0, one launch (start us, length us, event | category | flops | bytes accessed | tf_op | source)
XLA Modules:
  0.0 60.2 jit_solution(10387526563581503097)
XLA Ops:
  0.6 0.0 copy-start
  0.6 0.0 copy-start.1
  0.7 9.5 %shard_map.77 = (f32[3,2,4,512]{3,2,1,0:T(4,128)S(1)}, f32[2,3,256]{2,1,0:T(4,128)S(1)}, f32[2,2,2,64]{3,2,1,0:T(2,128)S(1)}) custom-call(f32[3,2,512]{2,1,0:T(2,128)} %bitcast.5, s32[2,512]{1,0:T(2,128)} %order_ref.1, f32[3,256]{1,0:T(4,128)} %proxy_ref.1, f32[2,2,64]{2,1,0:T(2,128)} %pivot_ref.1), custom_call_target="tpu_custom_call" | custom-call | flops 4000000000 | bytes 16000000 | tf_op jit(solution)/shard_map/pallas_call | solution.py:678
  10.1 0.0 copy-done
  10.1 0.0 copy-done.1
  10.2 6.5 %shard_map.78.cross_ref = f32[2,256,512]{2,1,0:T(8,128)S(1)} custom-call(s32[2,8]{1,0:T(2,128)S(1)} %copy-done, s32[2,8]{1,0:T(2,128)S(1)} %copy-done.1, f32[3,2,4,512]{3,2,1,0:T(4,128)S(1)} %get-tuple-element.12.points_ref, f32[2,3,256]{2,1,0:T(4,128)S(1)} %get-tuple-element.13.proxy_ref), custom_call_target="tpu_custom_call" | custom-call | tf_op jit(solution)/shard_map/pallas_call | solution.py:697
  16.6 0.1 collective-permute-start
  16.7 3.2 %shard_map.81 = (bf16[3,2,512,512]{3,2,1,0:T(8,128)(2,1)S(1)}, f32[3,256,512]{2,1,0:T(8,128)S(1)}) custom-call(s32[2,8]{1,0:T(2,128)S(1)} %copy-done, s32[2,8]{1,0:T(2,128)S(1)} %copy-done.1, f32[3,2,4,512]{3,2,1,0:T(4,128)S(1)} %get-tuple-element.12.points_ref), custom_call_target="tpu_custom_call" | custom-call | flops 8000000000 | bytes 16000000 | tf_op jit(solution)/shard_map/pallas_call | solution.py:715
  19.9 0.0 collective-permute-done.cross_in
  19.9 10.5 %shard_map.79.x_ref.mine_ref = f32[2,128,256]{2,1,0:T(8,128)S(1)} custom-call(f32[2,256,512]{2,1,0:T(8,128)S(1)} %shard_map.78.cross_ref, f32[2,256,512]{2,1,0:T(8,128)S(1)} %collective-permute-done.cross_in), custom_call_target="tpu_custom_call" | custom-call | tf_op jit(solution)/shard_map/pallas_call | solution.py:731
  30.4 1.1 %collective-permute-start.1 = (f32[2,128,256]{2,1,0:T(8,128)S(1)}, f32[2,128,256]{2,1,0:T(8,128)S(1)}, u32[]{:S(2)}, u32[]{:S(2)}) collective-permute-start(f32[2,128,256]{2,1,0:T(8,128)S(1)} %shard_map.79.x_ref.mine_ref), channel_id=1, source_target_pairs={{0,2},{1,3},{2,0},{3,1},{4,6},{5,7},{6,4},{7,5},{8,10},{9,11},{10,... | collective-permute-start | bytes 786440 | tf_op jit(solution)/shard_map/ppermute | solution.py:743
  31.5 6.9 %shard_map.80 = (f32[6,2,128,256]{3,2,1,0:T(8,128)S(1)}, bf16[2,512,512]{2,1,0:T(8,128)(2,1)S(1)}, f32[256,512]{1,0:T(8,128)S(1)}) custom-call(s32[2,8]{1,0:T(2,128)S(1)} %copy-done, s32[2,8]{1,0:T(2,128)S(1)} %copy-done.1, f32[3,2,4,512]{3,2,1,0:T(4,128)S(1)} %get-tuple-element.12.points_ref, f32[2,128,256]{2,1,0:T(8,128)S(1)} %shard_map.79.x_ref.mine_ref, ...), custom_call_target="tpu_custom_call" | custom-call | flops 8000000000 | bytes 16000000 | tf_op jit(solution)/shard_map/pallas_call | solution.py:746
  38.4 0.8 %collective-permute-done.1.x_ref = f32[2,128,256]{2,1,0:T(8,128)S(1)} collective-permute-done((f32[2,128,256]{2,1,0:T(8,128)S(1)}, f32[2,128,256]{2,1,0:T(8,128)S(1)}, u32[]{:S(2)}, u32[]{:S(2)}) %collective-permute-start.1) | collective-permute-done | bytes 262176 | tf_op jit(solution)/shard_map/ppermute | solution.py:743
  39.2 5.1 %shard_map.82 = (f32[6,2,128,256]{3,2,1,0:T(8,128)S(1)}, f32[2,2,64,256]{3,2,1,0:T(8,128)}) custom-call(s32[2,8]{1,0:T(2,128)S(1)} %copy-done, f32[6,2,128,256]{3,2,1,0:T(8,128)S(1)} %get-tuple-element.15.buf_ref, bf16[3,2,512,512]{3,2,1,0:T(8,128)(2,1)S(1)} %get-tuple-element.16.right_ref, f32[3,256,512]{2,1,0:T(8,128)S(1)} %get-tuple-element.17.rest_ref, ...), custom_call_target="tpu_custom_call" | custom-call | tf_op jit(solution)/shard_map/pallas_call | solution.py:767
  44.3 15.2 %shard_map.83 = f32[2,2,64,256]{3,2,1,0:T(8,128)S(1)} custom-call(f32[6,2,2,64,256]{4,3,2,1,0:T(8,128)S(1)} %bitcast.3), custom_call_target="tpu_custom_call" | custom-call | tf_op jit(solution)/shard_map/pallas_call | solution.py:786
  59.5 0.7 %copy.9 = f32[2,2,64,256]{3,2,1,0:T(8,128)} copy(f32[2,2,64,256]{3,2,1,0:T(8,128)S(1)} %shard_map.83) | data formatting | bytes 524288
Async XLA Ops:
  0.6 9.5 %copy-start = (s32[2,8]{1,0:T(2,128)S(1)}, s32[2,8]{1,0:T(2,128)}, u32[]{:S(2)}) copy-start(s32[2,8]{1,0:T(2,128)} %nb_ref.7) | copy-start | bytes 196
  0.6 9.5 %copy-start.1 = (s32[2,8]{1,0:T(2,128)S(1)}, s32[2,8]{1,0:T(2,128)}, u32[]{:S(2)}) copy-start(s32[2,8]{1,0:T(2,128)} %place_ref.5) | copy-start | bytes 196
  16.6 3.2 %collective-permute-start = (f32[2,256,512]{2,1,0:T(8,128)S(1)}, f32[2,256,512]{2,1,0:T(8,128)S(1)}, u32[]{:S(2)}, u32[]{:S(2)}) collective-permute-start(f32[2,256,512]{2,1,0:T(8,128)S(1)} %shard_map.78.cross_ref), channel_id=1, source_target_pairs={{0,1},{1,0},{2,3},{3,2},{4,5},{5,4},{6,7},{7,6},{8,9},{9,8},{10,11... | collective-permute-start | bytes 3145736 | tf_op jit(solution)/shard_map/ppermute | solution.py:712
  30.4 8.8 %collective-permute-start.1 = (f32[2,128,256]{2,1,0:T(8,128)S(1)}, f32[2,128,256]{2,1,0:T(8,128)S(1)}, u32[]{:S(2)}, u32[]{:S(2)}) collective-permute-start(f32[2,128,256]{2,1,0:T(8,128)S(1)} %shard_map.79.x_ref.mine_ref), channel_id=1, source_target_pairs={{0,2},{1,3},{2,0},{3,1},{4,6},{5,7},{6,4},{7,5},{8,10},{9,11},{10,... | collective-permute-start | bytes 786440 | tf_op jit(solution)/shard_map/ppermute | solution.py:743

commit v9 on v7

--- a/solution.py
+++ b/solution.py
@@ -16,7 +16,6 @@
 ROWS = 16
 DEPTH = 64
 PIECES = 2
-EARLY = 2
 
 SIN = (4.44287959, -7.30781805, 3.59778873, -0.79123822)
 COS = (1.41420408, -6.97764206, 5.7152384, -1.72834866)
@@ -86,6 +85,10 @@
     return stacked([row_three(-2.0 * high, 1.0), row_three(-2.0 * mid, 1.0),
                     row_three(-2.0 * high, 1.0), row_three(-2.0 * low, n_high),
                     row_three(-2.0 * mid, n_mid), row_three(-2.0 * high, n_low)])
+
+
+def padded(points):
+    return jnp.concatenate([points, jnp.zeros_like(points)], axis=0)
 
 
 def three_rows(points):
@@ -166,7 +169,7 @@
                                 + [jnp.zeros((5, count), F32)], axis=0)
         rows = jnp.concatenate(list(three(whole)) + [jnp.zeros_like(whole)], axis=0)
         picked = jnp.dot(rows.astype(BF16), one_hot.astype(BF16), preferred_element_type=F32)
-        points_out[1, box] = (picked[0:8] + picked[8:16]) + picked[16:24]
+        points_out[1, box] = ((picked[0:8] + picked[8:16]) + picked[16:24])[0:4]
     arrived()
     jobs = [
         send(points_out.at[1], points_out.at[0], sends, recvs, 0, after),
@@ -186,13 +189,14 @@
     me = lax.axis_index("col")
     box = me // group
     first = lax.rem(me, group) * entries
-    sources[...] = source_rows(centred(points_ref[1, box]))
+    sources[...] = source_rows(centred(padded(points_ref[1, box])))
     for d in range(box_count):
         directions = jnp.concatenate([proxy_ref[d], jnp.zeros((5, share), F32)], axis=0)
         targets[:, d * share:(d + 1) * share] = target_rows((2.0 * proxy_radius) * directions)
     for k in range(entries):
         slot = slot_of(nb_ref, box, first + k, box_count, box_total)
-        here = shifted(points_ref[slot // box_count, slot % box_count], place_ref[box, first + k])
+        here = shifted(padded(points_ref[slot // box_count, slot % box_count]),
+                       place_ref[box, first + k])
         targets[:, proxies + k * count:proxies + (k + 1) * count] = target_rows(here)
     block = tiles.shape[1] // 2
 
@@ -464,7 +468,8 @@
 def entry_squares(box_total, nb_ref, place_ref, points_ref, which, k, n, sources):
     box_count = points_ref.shape[1]
     place = slot_of(nb_ref, which, k, box_count, box_total)
-    here = shifted(points_ref[place // box_count, place % box_count], place_ref[which, k])
+    here = shifted(padded(points_ref[place // box_count, place % box_count]),
+                   place_ref[which, k])
     return dot_tn(sources[...], target_rows(here[:, 0:n]))
 
 
@@ -482,7 +487,7 @@
 
 
 def half_sources(points, side, group, n, width):
-    whole = source_rows(centred(points))
+    whole = source_rows(centred(padded(points)))
     half = whole[:, n:n + width]
     for c in range(1, group):
         half = jnp.where(side == c, whole[:, n + c * width:n + (c + 1) * width], half)
@@ -501,12 +506,10 @@
         squares[slot] = entry_squares(box_total, nb_ref, place_ref, points_ref, fed, k, n, sources)
 
     measure(0, 0)
-
-    @pl.loop(0, pairs)
-    def _(pair):
-        for i in range(2):
-            measure(jnp.minimum(2 * pair + i + 1, 2 * pairs - 1), 1 - i)
-            evaluate(squares.at[i], n, width, right_ref.at[pair], rest_ref.at[pair], i)
+    for k in range(2 * pairs):
+        if k + 1 < 2 * pairs:
+            measure(k + 1, (k + 1) % 2)
+        evaluate(squares.at[k % 2], n, width, right_ref.at[k // 2], rest_ref.at[k // 2], k % 2)
 
 
 def near_kernel(box_total, group, nb_ref, place_ref, points_ref, x_ref, pivot_ref,
@@ -602,14 +605,14 @@
     box_count, _, strip, _ = out_ref.shape
     order = (2 * odd, 2 - 2 * odd, 1)
     piece = strip // PIECES
-    chunks = [(d, p, pl.ds(i * piece, piece)) for d in range(box_count) for p in range(2)
-              for i in range(PIECES)]
-    late, early = chunks[:-EARLY], chunks[-EARLY:]
+    early = (box_count - 1, 1)
+    wholes = [(d, p) for d in range(box_count) for p in range(2) if (d, p) != early]
+    late = [part + (pl.ds(i * piece, piece),) for part in wholes for i in range(PIECES)]
     count = iter(range(sends.shape[0]))
 
-    def pair(g, parts):
-        return [send(buf_ref.at[(order[g] * box_count + part[0], part[1], 1 - side) + part[2:]],
-                     pair_in.at[(g,) + part], sends, recvs, next(count), near) for part in parts]
+    def pair(g, part):
+        return send(buf_ref.at[(order[g] * box_count + part[0], part[1], 1 - side) + part[2:]],
+                    pair_in.at[(g,) + part], sends, recvs, next(count), near)
 
     def both(g, part):
         return (buf_ref[(order[g] * box_count + part[0], part[1], side) + part[2:]]
@@ -618,22 +621,23 @@
     def forward(source_ref, target_ref, part, peer):
         return send(source_ref.at[part], target_ref.at[part], sends, recvs, next(count), peer)
 
-    line_pairs, line_early = pair(0, late), pair(0, early)
-    side_early, side_pairs = pair(1, early), pair(1, late)
-    own_pairs = pair(2, chunks)
-    lines, sides, turns, directs, onward = [], [], [], [], []
+    line_pairs = [pair(0, part) for part in late]
+    line_early, side_early = pair(0, early), pair(1, early)
+    side_pairs = [pair(1, part) for part in wholes]
+    own_pair = send(buf_ref.at[box_count:2 * box_count, :, 1 - side], pair_in.at[2], sends, recvs,
+                    next(count), near)
+    lines, sides = [], []
     for part, copy in zip(late, line_pairs):
         copy.wait()
         line_out[part] = both(0, part)
         lines.append(forward(line_out, line_in, part, relay))
-    for part, copy, other in zip(early, line_early, side_early):
-        copy.wait()
-        line_out[part] = both(0, part)
-        turns.append(forward(line_out, line_in, part, twin))
-        other.wait()
-        side_out[part] = both(1, part)
-        directs.append(forward(side_out, side_in, part, twin))
-    for part, copy in zip(late, side_pairs):
+    line_early.wait()
+    line_out[early] = both(0, early)
+    turn = forward(line_out, line_in, early, twin)
+    side_early.wait()
+    side_out[early] = both(1, early)
+    direct = forward(side_out, side_in, early, twin)
+    for part, copy in zip(wholes, side_pairs):
         copy.wait()
         held[part] = both(1, part)
     for i, (part, copy) in enumerate(zip(late, lines)):
@@ -641,16 +645,15 @@
         side_out[part] = held[part] + line_in[part]
         sides.append(forward(side_out, side_in, part, twin))
         if i == 1:
-            for some, turn in zip(early, turns):
-                turn.wait()
-                onward.append(forward(line_in, last_in, some, source))
-    for part, copy in zip(chunks, own_pairs):
-        copy.wait()
-        held[part] = both(2, part)
-    for part, direct, copy in zip(early, directs, onward):
-        direct.wait()
-        copy.wait()
-        out_ref[part] = (held[part] + side_in[part]) + last_in[part]
+            turn.wait()
+            onward = forward(line_in, last_in, early, source)
+    own_pair.wait()
+    for d in range(box_count):
+        for p in range(2):
+            held[d, p] = both(2, (d, p))
+    direct.wait()
+    onward.wait()
+    out_ref[early] = (held[early] + side_in[early]) + last_in[early]
     for part, copy in zip(late, sides):
         copy.wait()
         out_ref[part] = held[part] + side_in[part]
@@ -679,7 +682,7 @@
     points, proxies, pivots = pl.pallas_call(
         functools.partial(exchange_kernel, box_total, col_count, group, skeleton),
         out_shape=(
-            jax.ShapeDtypeStruct((3, box_count, 8, point_count), F32),
+            jax.ShapeDtypeStruct((3, box_count, 4, point_count), F32),
             jax.ShapeDtypeStruct((box_count,) + proxy_directions.shape, F32),
             jax.ShapeDtypeStruct((box_count,) + pivot_inverse.shape, F32),
         ),
@@ -783,7 +786,7 @@
 
     strip = skeleton // col_count
     block = (box_count, 2, strip, skeleton)
-    jobs = 5 * PIECES * 2 * box_count + EARLY
+    jobs = (3 * PIECES + 1) * (2 * box_count - 1) + 6
     skeleton_update = pl.pallas_call(
         functools.partial(reduce_kernel, box_total),
         out_shape=jax.ShapeDtypeStruct(block, F32),

time: 59.6 us -> 58.5 us (0.982)
  Pallas kernels: 56.2 us -> 54.9 us
    pallas_call x1, Pallas kernels: 3.94 us -> 3.16 us  [on_device(): pl.pallas_call(functools.partial(kernel_kernel, box_total, group), out_sh...]
  transfers between devices with their start and end apart: 2 -> 2, of which waited for: 1 -> 1; matrix products, arithmetic and copies ran while one was open for 0% -> 0% of each run, Pallas kernels for 19% -> 17%
where the time goes in v9:
time: 58.5 us; the launch traced here: 58.3 us
  Pallas kernels  54.9 us (94%)
  starting transfers between devices  1.11 us (2%)
  waiting for transfers between devices  0.9 us (2%)
  between operations  0.72 us (1%)
  local copies, waits for them, and re-layouts  0.71 us (1%)
    pallas_call x1, Pallas kernels, on_device(): pl.pallas_call(functools.partial(reduce_kernel, box_total), out_shape=jax...  13.6 us
    pallas_call x1, Pallas kernels, on_device(): pl.pallas_call(functools.partial(solve_kernel, group), out_shape=jax.Shap...  10.4 us
    pallas_call x1, Pallas kernels, on_device(): pl.pallas_call(functools.partial(exchange_kernel, box_total, col_count, g...  9.47 us
    pallas_call x1, Pallas kernels, on_device(): pl.pallas_call(functools.partial(near_kernel, box_total, group), out_shap...  6.84 us
    pallas_call x1, Pallas kernels, on_device(): pl.pallas_call(functools.partial(tile_kernel, box_total, entries, group,...  6.47 us
    pallas_call x1, Pallas kernels, on_device(): pl.pallas_call(functools.partial(far_kernel, box_total, group), out_shape...  4.93 us
    pallas_call x1, Pallas kernels, on_device(): pl.pallas_call(functools.partial(kernel_kernel, box_total, group), out_sh...  3.16 us
  transfers between devices with their start and end apart: 2, of which 1 were waited for; matrix products, arithmetic and copies ran while one was open for 0% of the time, Pallas kernels for 17%

profile of v9, /device:TPU:0, one launch (start us, length us, event | category | flops | bytes accessed | tf_op | source)
XLA Modules:
  0.0 58.3 jit_solution(7058261934256421211)
XLA Ops:
  0.6 0.0 copy-start
  0.6 0.0 copy-start.1
  0.7 9.5 %shard_map.77 = (f32[3,2,4,512]{3,2,1,0:T(4,128)S(1)}, f32[2,3,256]{2,1,0:T(4,128)S(1)}, f32[2,2,2,64]{3,2,1,0:T(2,128)S(1)}) custom-call(f32[3,2,512]{2,1,0:T(2,128)} %bitcast.5, s32[2,512]{1,0:T(2,128)} %order_ref.1, f32[3,256]{1,0:T(4,128)} %proxy_ref.1, f32[2,2,64]{2,1,0:T(2,128)} %pivot_ref.1), custom_call_target="tpu_custom_call" | custom-call | flops 4000000000 | bytes 16000000 | tf_op jit(solution)/shard_map/pallas_call | solution.py:682
  10.1 0.0 copy-done
  10.1 0.0 copy-done.1
  10.2 6.5 %shard_map.78.cross_ref = f32[2,256,512]{2,1,0:T(8,128)S(1)} custom-call(s32[2,8]{1,0:T(2,128)S(1)} %copy-done, s32[2,8]{1,0:T(2,128)S(1)} %copy-done.1, f32[3,2,4,512]{3,2,1,0:T(4,128)S(1)} %get-tuple-element.12.points_ref, f32[2,3,256]{2,1,0:T(4,128)S(1)} %get-tuple-element.13.proxy_ref), custom_call_target="tpu_custom_call" | custom-call | tf_op jit(solution)/shard_map/pallas_call | solution.py:701
  16.6 0.1 collective-permute-start
  16.7 3.2 %shard_map.81 = (bf16[3,2,512,512]{3,2,1,0:T(8,128)(2,1)S(1)}, f32[3,256,512]{2,1,0:T(8,128)S(1)}) custom-call(s32[2,8]{1,0:T(2,128)S(1)} %copy-done, s32[2,8]{1,0:T(2,128)S(1)} %copy-done.1, f32[3,2,4,512]{3,2,1,0:T(4,128)S(1)} %get-tuple-element.12.points_ref), custom_call_target="tpu_custom_call" | custom-call | flops 8000000000 | bytes 16000000 | tf_op jit(solution)/shard_map/pallas_call | solution.py:719
  19.9 0.0 collective-permute-done.cross_in
  19.9 10.4 %shard_map.79.x_ref.mine_ref = f32[2,256,128]{2,1,0:T(8,128)S(1)} custom-call(f32[2,256,512]{2,1,0:T(8,128)S(1)} %shard_map.78.cross_ref, f32[2,256,512]{2,1,0:T(8,128)S(1)} %collective-permute-done.cross_in), custom_call_target="tpu_custom_call" | custom-call | tf_op jit(solution)/shard_map/pallas_call | solution.py:735
  30.3 1.0 %collective-permute-start.1 = (f32[2,256,128]{2,1,0:T(8,128)S(1)}, f32[2,256,128]{2,1,0:T(8,128)S(1)}, u32[]{:S(2)}, u32[]{:S(2)}) collective-permute-start(f32[2,256,128]{2,1,0:T(8,128)S(1)} %shard_map.79.x_ref.mine_ref), channel_id=1, source_target_pairs={{0,2},{1,3},{2,0},{3,1},{4,6},{5,7},{6,4},{7,5},{8,10},{9,11},{10,... | collective-permute-start | bytes 786440 | tf_op jit(solution)/shard_map/ppermute | solution.py:747
  31.3 6.8 %shard_map.80 = (f32[6,2,128,256]{3,2,1,0:T(8,128)S(1)}, bf16[2,512,512]{2,1,0:T(8,128)(2,1)S(1)}, f32[256,512]{1,0:T(8,128)S(1)}) custom-call(s32[2,8]{1,0:T(2,128)S(1)} %copy-done, s32[2,8]{1,0:T(2,128)S(1)} %copy-done.1, f32[3,2,4,512]{3,2,1,0:T(4,128)S(1)} %get-tuple-element.12.points_ref, f32[2,256,128]{2,1,0:T(8,128)S(1)} %shard_map.79.x_ref.mine_ref, ...), custom_call_target="tpu_custom_call" | custom-call | flops 8000000000 | bytes 16000000 | tf_op jit(solution)/shard_map/pallas_call | solution.py:750
  38.2 0.9 %collective-permute-done.1.x_ref = f32[2,256,128]{2,1,0:T(8,128)S(1)} collective-permute-done((f32[2,256,128]{2,1,0:T(8,128)S(1)}, f32[2,256,128]{2,1,0:T(8,128)S(1)}, u32[]{:S(2)}, u32[]{:S(2)}) %collective-permute-start.1) | collective-permute-done | bytes 262176 | tf_op jit(solution)/shard_map/ppermute | solution.py:747
  39.1 4.9 %shard_map.82 = (f32[6,2,128,256]{3,2,1,0:T(8,128)S(1)}, f32[2,2,64,256]{3,2,1,0:T(8,128)}) custom-call(s32[2,8]{1,0:T(2,128)S(1)} %copy-done, f32[6,2,128,256]{3,2,1,0:T(8,128)S(1)} %get-tuple-element.15.buf_ref, bf16[3,2,512,512]{3,2,1,0:T(8,128)(2,1)S(1)} %get-tuple-element.16.right_ref, f32[3,256,512]{2,1,0:T(8,128)S(1)} %get-tuple-element.17.rest_ref, ...), custom_call_target="tpu_custom_call" | custom-call | tf_op jit(solution)/shard_map/pallas_call | solution.py:771
  44.0 13.6 %shard_map.83 = f32[2,2,64,256]{3,2,1,0:T(8,128)S(1)} custom-call(f32[6,2,2,64,256]{4,3,2,1,0:T(8,128)S(1)} %bitcast.3), custom_call_target="tpu_custom_call" | custom-call | tf_op jit(solution)/shard_map/pallas_call | solution.py:790
  57.6 0.7 %copy.9 = f32[2,2,64,256]{3,2,1,0:T(8,128)} copy(f32[2,2,64,256]{3,2,1,0:T(8,128)S(1)} %shard_map.83) | data formatting | bytes 524288
Async XLA Ops:
  0.6 9.5 %copy-start = (s32[2,8]{1,0:T(2,128)S(1)}, s32[2,8]{1,0:T(2,128)}, u32[]{:S(2)}) copy-start(s32[2,8]{1,0:T(2,128)} %nb_ref.7) | copy-start | bytes 196
  0.6 9.5 %copy-start.1 = (s32[2,8]{1,0:T(2,128)S(1)}, s32[2,8]{1,0:T(2,128)}, u32[]{:S(2)}) copy-start(s32[2,8]{1,0:T(2,128)} %place_ref.5) | copy-start | bytes 196
  16.6 3.2 %collective-permute-start = (f32[2,256,512]{2,1,0:T(8,128)S(1)}, f32[2,256,512]{2,1,0:T(8,128)S(1)}, u32[]{:S(2)}, u32[]{:S(2)}) collective-permute-start(f32[2,256,512]{2,1,0:T(8,128)S(1)} %shard_map.78.cross_ref), channel_id=1, source_target_pairs={{0,1},{1,0},{2,3},{3,2},{4,5},{5,4},{6,7},{7,6},{8,9},{9,8},{10,11... | collective-permute-start | bytes 3145736 | tf_op jit(solution)/shard_map/ppermute | solution.py:716
  30.3 8.8 %collective-permute-start.1 = (f32[2,256,128]{2,1,0:T(8,128)S(1)}, f32[2,256,128]{2,1,0:T(8,128)S(1)}, u32[]{:S(2)}, u32[]{:S(2)}) collective-permute-start(f32[2,256,128]{2,1,0:T(8,128)S(1)} %shard_map.79.x_ref.mine_ref), channel_id=1, source_target_pairs={{0,2},{1,3},{2,0},{3,1},{4,6},{5,7},{6,4},{7,5},{8,10},{9,11},{10,... | collective-permute-start | bytes 786440 | tf_op jit(solution)/shard_map/ppermute | solution.py:747

commit v10 on v9

--- a/solution.py
+++ b/solution.py
@@ -42,7 +42,7 @@
 def kernel_values(square):
     inverse = lax.rsqrt(square)
     turns = square * inverse
-    part = turns - jnp.floor(turns + 0.5)
+    part = turns - lax.round(turns, lax.RoundingMethod.TO_NEAREST_EVEN)
     z = part * part
     amplitude = inverse * (1.0 / (2.0 * math.pi))
     sine = part * horner(SIN, z)
@@ -561,7 +561,7 @@
 
 
 def far_kernel(box_total, group, nb_ref, buf_ref, right_ref, rest_ref, right_last, rest_last,
-               x_ref, mine_ref, pivot_ref, out_ref, inter_ref, turned, blocks):
+               x_ref, mine_ref, pivot_ref, out_ref, inter_hbm, turned, blocks, inter_ref, done):
     pairs = rest_ref.shape[0] + 1
     me = lax.axis_index("col")
     box = me // group
@@ -570,6 +570,14 @@
     strip = inter_ref.shape[2]
     theirs = [jnp.transpose(x_ref[p]) for p in range(2)]
     turned[...] = left_side(*theirs)
+    for p in range(2):
+        for block, where in ((jnp.transpose(mine_ref[p]), box), (theirs[p], fed)):
+            piece = block[0:strip]
+            for c in range(1, block.shape[0] // strip):
+                piece = jnp.where(box == c, block[c * strip:(c + 1) * strip], piece)
+            inter_ref[where, p] = piece
+    copy = pltpu.make_async_copy(inter_ref, inter_hbm, done.at[0])
+    copy.start()
     pivots = pivot_columns(pivot_ref, fed)
     row = first_row(group, out_ref.shape[2])
     for pair in range(pairs + 1):
@@ -583,12 +591,7 @@
             if pair:
                 fold(blocks, pair - 1, i, row, pivots, out_ref,
                      slot_of(nb_ref, fed, 2 * pair - 2 + i, box_count, box_total))
-    for p in range(2):
-        for block, where in ((jnp.transpose(mine_ref[p]), box), (theirs[p], fed)):
-            piece = block[0:strip]
-            for c in range(1, block.shape[0] // strip):
-                piece = jnp.where(box == c, block[c * strip:(c + 1) * strip], piece)
-            inter_ref[where, p] = piece
+    copy.wait()
 
 
 def reduce_kernel(box_total, buf_ref, out_ref, pair_in, line_out, line_in, side_out, side_in,
@@ -775,10 +778,12 @@
             jax.ShapeDtypeStruct((box_count, 2, width, skeleton), F32),
         ),
         in_specs=[SMEM] + [VMEM] * 8,
-        out_specs=(VMEM, VMEM),
+        out_specs=(VMEM, HBM),
         scratch_shapes=[
             pltpu.VMEM((4 * half, 2 * skeleton), BF16),
             pltpu.VMEM((listed // 2, 2 * half, 2 * skeleton), F32),
+            pltpu.VMEM((box_count, 2, width, skeleton), F32),
+            dma((1,)),
         ],
         compiler_params=params(),
     )(neighbour_boxes, buffer, right, kept, right_last, kept_last, arrived, solved, pivots)

time: 58.5 us -> 58.1 us (level)
  Pallas kernels: 54.9 us -> 54.3 us
where the time goes in v10:
time: 58.1 us; the launch traced here: 57.9 us
  Pallas kernels  54.3 us (93%)
  starting transfers between devices  1.11 us (2%)
  waiting for transfers between devices  1.02 us (2%)
  between operations  0.73 us (1%)
  local copies, waits for them, and re-layouts  0.71 us (1%)
    pallas_call x1, Pallas kernels, on_device(): pl.pallas_call(functools.partial(reduce_kernel, box_total), out_shape=jax...  13.6 us
    pallas_call x1, Pallas kernels, on_device(): pl.pallas_call(functools.partial(solve_kernel, group), out_shape=jax.Shap...  10.4 us
    pallas_call x1, Pallas kernels, on_device(): pl.pallas_call(functools.partial(exchange_kernel, box_total, col_count, g...  9.47 us
    pallas_call x1, Pallas kernels, on_device(): pl.pallas_call(functools.partial(near_kernel, box_total, group), out_shap...  6.71 us
    pallas_call x1, Pallas kernels, on_device(): pl.pallas_call(functools.partial(tile_kernel, box_total, entries, group,...  6.29 us
    pallas_call x1, Pallas kernels, on_device(): pl.pallas_call(functools.partial(far_kernel, box_total, group), out_shape...  4.73 us
    pallas_call x1, Pallas kernels, on_device(): pl.pallas_call(functools.partial(kernel_kernel, box_total, group), out_sh...  3.07 us
  transfers between devices with their start and end apart: 2, of which 1 were waited for; matrix products, arithmetic and copies ran while one was open for 0% of the time, Pallas kernels for 17%

profile of v10, /device:TPU:0, one launch (start us, length us, event | category | flops | bytes accessed | tf_op | source)
XLA Modules:
  0.0 57.9 jit_solution(2195665918401827322)
XLA Ops:
  0.6 0.0 copy-start
  0.6 0.0 copy-start.1
  0.7 9.5 %shard_map.77 = (f32[3,2,4,512]{3,2,1,0:T(4,128)S(1)}, f32[2,3,256]{2,1,0:T(4,128)S(1)}, f32[2,2,2,64]{3,2,1,0:T(2,128)S(1)}) custom-call(f32[3,2,512]{2,1,0:T(2,128)} %bitcast.5, s32[2,512]{1,0:T(2,128)} %order_ref.1, f32[3,256]{1,0:T(4,128)} %proxy_ref.1, f32[2,2,64]{2,1,0:T(2,128)} %pivot_ref.1), custom_call_target="tpu_custom_call" | custom-call | flops 4000000000 | bytes 16000000 | tf_op jit(solution)/shard_map/pallas_call | solution.py:685
  10.1 0.0 copy-done
  10.1 0.0 copy-done.1
  10.2 6.3 %shard_map.78.cross_ref = f32[2,256,512]{2,1,0:T(8,128)S(1)} custom-call(s32[2,8]{1,0:T(2,128)S(1)} %copy-done, s32[2,8]{1,0:T(2,128)S(1)} %copy-done.1, f32[3,2,4,512]{3,2,1,0:T(4,128)S(1)} %get-tuple-element.12.points_ref, f32[2,3,256]{2,1,0:T(4,128)S(1)} %get-tuple-element.13.proxy_ref), custom_call_target="tpu_custom_call" | custom-call | tf_op jit(solution)/shard_map/pallas_call | solution.py:704
  16.5 0.1 collective-permute-start
  16.5 3.1 %shard_map.81 = (bf16[3,2,512,512]{3,2,1,0:T(8,128)(2,1)S(1)}, f32[3,256,512]{2,1,0:T(8,128)S(1)}) custom-call(s32[2,8]{1,0:T(2,128)S(1)} %copy-done, s32[2,8]{1,0:T(2,128)S(1)} %copy-done.1, f32[3,2,4,512]{3,2,1,0:T(4,128)S(1)} %get-tuple-element.12.points_ref), custom_call_target="tpu_custom_call" | custom-call | flops 8000000000 | bytes 16000000 | tf_op jit(solution)/shard_map/pallas_call | solution.py:722
  19.6 0.0 collective-permute-done.cross_in
  19.6 10.4 %shard_map.79.x_ref.mine_ref = f32[2,256,128]{2,1,0:T(8,128)S(1)} custom-call(f32[2,256,512]{2,1,0:T(8,128)S(1)} %shard_map.78.cross_ref, f32[2,256,512]{2,1,0:T(8,128)S(1)} %collective-permute-done.cross_in), custom_call_target="tpu_custom_call" | custom-call | tf_op jit(solution)/shard_map/pallas_call | solution.py:738
  30.1 1.0 %collective-permute-start.1 = (f32[2,256,128]{2,1,0:T(8,128)S(1)}, f32[2,256,128]{2,1,0:T(8,128)S(1)}, u32[]{:S(2)}, u32[]{:S(2)}) collective-permute-start(f32[2,256,128]{2,1,0:T(8,128)S(1)} %shard_map.79.x_ref.mine_ref), channel_id=1, source_target_pairs={{0,2},{1,3},{2,0},{3,1},{4,6},{5,7},{6,4},{7,5},{8,10},{9,11},{10,... | collective-permute-start | bytes 786440 | tf_op jit(solution)/shard_map/ppermute | solution.py:750
  31.1 6.7 %shard_map.80 = (f32[6,2,128,256]{3,2,1,0:T(8,128)S(1)}, bf16[2,512,512]{2,1,0:T(8,128)(2,1)S(1)}, f32[256,512]{1,0:T(8,128)S(1)}) custom-call(s32[2,8]{1,0:T(2,128)S(1)} %copy-done, s32[2,8]{1,0:T(2,128)S(1)} %copy-done.1, f32[3,2,4,512]{3,2,1,0:T(4,128)S(1)} %get-tuple-element.12.points_ref, f32[2,256,128]{2,1,0:T(8,128)S(1)} %shard_map.79.x_ref.mine_ref, ...), custom_call_target="tpu_custom_call" | custom-call | flops 8000000000 | bytes 16000000 | tf_op jit(solution)/shard_map/pallas_call | solution.py:753
  37.8 1.0 %collective-permute-done.1.x_ref = f32[2,256,128]{2,1,0:T(8,128)S(1)} collective-permute-done((f32[2,256,128]{2,1,0:T(8,128)S(1)}, f32[2,256,128]{2,1,0:T(8,128)S(1)}, u32[]{:S(2)}, u32[]{:S(2)}) %collective-permute-start.1) | collective-permute-done | bytes 262176 | tf_op jit(solution)/shard_map/ppermute | solution.py:750
  38.8 4.7 %shard_map.82 = (f32[6,2,128,256]{3,2,1,0:T(8,128)S(1)}, f32[2,2,64,256]{3,2,1,0:T(8,128)}) custom-call(s32[2,8]{1,0:T(2,128)S(1)} %copy-done, f32[6,2,128,256]{3,2,1,0:T(8,128)S(1)} %get-tuple-element.15.buf_ref, bf16[3,2,512,512]{3,2,1,0:T(8,128)(2,1)S(1)} %get-tuple-element.16.right_ref, f32[3,256,512]{2,1,0:T(8,128)S(1)} %get-tuple-element.17.rest_ref, ...), custom_call_target="tpu_custom_call" | custom-call | tf_op jit(solution)/shard_map/pallas_call | solution.py:774
  43.6 13.6 %shard_map.83 = f32[2,2,64,256]{3,2,1,0:T(8,128)S(1)} custom-call(f32[6,2,2,64,256]{4,3,2,1,0:T(8,128)S(1)} %bitcast.3), custom_call_target="tpu_custom_call" | custom-call | tf_op jit(solution)/shard_map/pallas_call | solution.py:795
  57.2 0.7 %copy.9 = f32[2,2,64,256]{3,2,1,0:T(8,128)} copy(f32[2,2,64,256]{3,2,1,0:T(8,128)S(1)} %shard_map.83) | data formatting | bytes 524288
Async XLA Ops:
  0.6 9.5 %copy-start = (s32[2,8]{1,0:T(2,128)S(1)}, s32[2,8]{1,0:T(2,128)}, u32[]{:S(2)}) copy-start(s32[2,8]{1,0:T(2,128)} %nb_ref.7) | copy-start | bytes 196
  0.6 9.5 %copy-start.1 = (s32[2,8]{1,0:T(2,128)S(1)}, s32[2,8]{1,0:T(2,128)}, u32[]{:S(2)}) copy-start(s32[2,8]{1,0:T(2,128)} %place_ref.5) | copy-start | bytes 196
  16.5 3.2 %collective-permute-start = (f32[2,256,512]{2,1,0:T(8,128)S(1)}, f32[2,256,512]{2,1,0:T(8,128)S(1)}, u32[]{:S(2)}, u32[]{:S(2)}) collective-permute-start(f32[2,256,512]{2,1,0:T(8,128)S(1)} %shard_map.78.cross_ref), channel_id=1, source_target_pairs={{0,1},{1,0},{2,3},{3,2},{4,5},{5,4},{6,7},{7,6},{8,9},{9,8},{10,11... | collective-permute-start | bytes 3145736 | tf_op jit(solution)/shard_map/ppermute | solution.py:719
  30.1 8.8 %collective-permute-start.1 = (f32[2,256,128]{2,1,0:T(8,128)S(1)}, f32[2,256,128]{2,1,0:T(8,128)S(1)}, u32[]{:S(2)}, u32[]{:S(2)}) collective-permute-start(f32[2,256,128]{2,1,0:T(8,128)S(1)} %shard_map.79.x_ref.mine_ref), channel_id=1, source_target_pairs={{0,2},{1,3},{2,0},{3,1},{4,6},{5,7},{6,4},{7,5},{8,10},{9,11},{10,... | collective-permute-start | bytes 786440 | tf_op jit(solution)/shard_map/ppermute | solution.py:750
